TPU v7x, 32 devices: a whole 2x2x4 slice. The times are simulated.
32 devices in a mesh: dp: 2 (over core), seq: 16 (over z, y, x).
Axes of the slice: x: 2, y: 2, z: 4, core: 2. Of those that a mesh axis runs over, the one named last changes fastest.
Arguments:
- tokens: bfloat16 [32768, 768], P(('dp', 'seq')), may hold values from -6 to 6
- doc_start: int32 [32768], P(('dp', 'seq')), may hold values from 0 to 32767, as said below
- real: int32 [32768], P(('dp', 'seq')), may hold values from 0 to 1, as said below
- w_qkv: bfloat16 [768, 2304], P('dp', 'seq'), may hold values from -0.3125 to 0.3125
- w_out: bfloat16 [768, 768], P('dp', 'seq'), may hold values from -1 to 1
- w_in: bfloat16 [768, 2304], P('dp', 'seq'), may hold values from -0.21875 to 0.21875
- w_down: bfloat16 [1152, 768], P('dp', 'seq'), may hold values from -0.375 to 0.375
- gain_attn: bfloat16 [768], P('seq'), may hold values from 0.5 to 1.5
- gain_mlp: bfloat16 [768], P('seq'), may hold values from 0.5 to 1.5
- cotangent: bfloat16 [32768, 768], P(('dp', 'seq')), may hold values from -6 to 6
Outputs:
- output: bfloat16 [32768, 768], P(('dp', 'seq'))
- grad_tokens: float32 [32768, 768], P(('dp', 'seq'))
- grad_w_qkv: float32 [768, 2304], P('dp', 'seq')
- grad_w_out: float32 [768, 768], P('dp', 'seq')
- grad_w_in: float32 [768, 2304], P('dp', 'seq')
- grad_w_down: float32 [1152, 768], P('dp', 'seq')
- grad_gain_attn: float32 [768], P('seq')
- grad_gain_mlp: float32 [768], P('seq')
Inputs may be any that keep to these rules, and one draw needn't show every extreme that they name: `doc_start`: for each slot, the index in the whole stream of 32768 slots of the first slot of its document; packed rows begin at slots 8192 / 2 + k * 8192, so the first and the last row hold 4096 slots and the others 8192; documents never cross a row, and a row's padding forms a document of its own. `real`: each packed row ends in one or more padding slots and has no others.
All inputs are finite; a program needn't handle non-finite values.
Results may differ from a plain program's by a relative error of at most 0.014.
The roundings to bfloat16 on the way count: a program that leaves them out, or rounds other values in their place, can miss the bound.
Values may be sent and summed in bfloat16 or wider, within the bound.
A program may use at most 192 MiB of HBM per device.

v0:
```python
import math

import jax
import jax.numpy as jnp
from jax import lax
from jax.sharding import PartitionSpec as P

D = 768
HEADS = 12
HEAD = 64
FF = 1152
HALF = 64


def padded(value, sides, width):
    for axis, dim in sides:
        size, length = (lax.axis_size(axis), value.shape[dim])
        up = [(i, (i + 1) % size) for i in range(size - 1)]
        down = [(j, i) for i, j in up]
        last = lax.slice_in_dim(value, length - width, length, axis=dim)
        initial = lax.slice_in_dim(value, 0, width, axis=dim)
        before = lax.ppermute(last, axis, up)
        after = lax.ppermute(initial, axis, down)
        value = jnp.concatenate([before, value, after], axis=dim)
    return value


def shifted(value, axis, by):
    length = lax.axis_size(axis)
    pairs = [(i, i + by) for i in range(length) if 0 <= i + by < length]
    return lax.ppermute(value, axis, pairs)


def layer_norm(value):
    centre = value - jnp.mean(value, axis=-1, keepdims=True)
    factor = lax.rsqrt(jnp.mean(centre * centre, axis=-1, keepdims=True) + 1e-05)
    return (centre * factor, factor)


def norm_back(grad, normed, factor):
    return factor * (
        grad
        - jnp.mean(grad, axis=-1, keepdims=True)
        - normed * jnp.mean(grad * normed, axis=-1, keepdims=True)
    )


def rotary_tables(place):
    freq = jnp.exp(jnp.arange(HEAD // 2, dtype=jnp.float32) * (-2.0 * math.log(10000.0) / HEAD))
    angle = place[:, None] * freq[None, :]
    cosine = jnp.tile(jnp.concatenate([jnp.cos(angle), jnp.cos(angle)], 1), (1, HEADS))
    sine = jnp.tile(jnp.concatenate([jnp.sin(angle), jnp.sin(angle)], 1), (1, HEADS))
    return (cosine, sine)


def rotate(value):
    count = value.shape[0]
    shaped = value.reshape(count, HEADS, HEAD)
    first = shaped[..., : HEAD // 2]
    second = shaped[..., HEAD // 2 :]
    return jnp.concatenate([-second, first], -1).reshape(count, HEADS * HEAD)


def window_mask(own, other, count, width):
    offset = (
        jnp.arange(width, dtype=jnp.int32)[None, :]
        - jnp.arange(count, dtype=jnp.int32)[:, None]
        - HALF
    )
    near = jnp.abs(offset) <= HALF
    return near & ((other[None, :] == own[:, None]) | (offset == 0))


def left_dot(left, right):
    return lax.dot_general(
        left, right, (((0,), (0,)), ((), ())), preferred_element_type=jnp.float32
    )


def right_dot(left, right):
    return lax.dot_general(
        left, right, (((1,), (1,)), ((), ())), preferred_element_type=jnp.float32
    )


def glu_piece(gate_up):
    return jax.nn.gelu(gate_up[:, :FF], approximate=False) * gate_up[:, FF:]


def tiled(value, copies):
    return jnp.broadcast_to(value[None, :], (copies, value.shape[0]))


def on_device(tokens, doc_start, real, w_qkv, w_out, w_in, w_down, gain_attn, gain_mlp, cotangent):
    count = tokens.shape[0]
    col_parts = (
        lax.all_gather(w_qkv, "seq", axis=1, tiled=True),
        lax.all_gather(w_out, "seq", axis=1, tiled=True),
        lax.all_gather(w_in, "seq", axis=1, tiled=True),
        lax.all_gather(w_down, "seq", axis=1, tiled=True),
        lax.all_gather(gain_attn, "seq", axis=0, tiled=True),
        lax.all_gather(gain_mlp, "seq", axis=0, tiled=True),
    )
    full_qkv, full_out, full_in, full_down = (
        lax.all_gather(col_parts[0], "dp", axis=0, tiled=True),
        lax.all_gather(col_parts[1], "dp", axis=0, tiled=True),
        lax.all_gather(col_parts[2], "dp", axis=0, tiled=True),
        lax.all_gather(col_parts[3], "dp", axis=0, tiled=True),
    )
    gain_one, gain_two = (col_parts[4], col_parts[5])
    gain_one = gain_one.astype(jnp.float32)
    gain_two = gain_two.astype(jnp.float32)
    stream = tokens.astype(jnp.float32)
    normed_a, factor_a = layer_norm(stream)
    h_attn = (normed_a * gain_one).astype(jnp.bfloat16)
    qkv = jnp.dot(h_attn, full_qkv, preferred_element_type=jnp.float32)
    offset_base = lax.axis_index(("dp", "seq")) * count
    place = (offset_base + jnp.arange(count, dtype=jnp.int32) - doc_start).astype(jnp.float32)
    cosine, sine = rotary_tables(place)
    query = (qkv[:, :D] * cosine + rotate(qkv[:, :D]) * sine).astype(jnp.bfloat16)
    key_rows = (qkv[:, D : 2 * D] * cosine + rotate(qkv[:, D : 2 * D]) * sine).astype(jnp.bfloat16)
    value_rows = qkv[:, 2 * D :].astype(jnp.bfloat16)
    tag_query = doc_start + 1
    tag_key = jnp.where(real == 1, tag_query, 0)
    key_value = jnp.concatenate([key_rows, value_rows], 1)
    wide_kv, wide_tag = (
        padded(key_value, ((("dp", "seq"), 0),), HALF),
        padded(tag_key, ((("dp", "seq"), 0),), HALF),
    )
    block_rows = 512
    width = block_rows + 2 * HALF
    blocks = count // block_rows

    def block_scores(start):
        q_blk = query[start : start + block_rows].reshape(block_rows, HEADS, HEAD)
        k_blk = wide_kv[start : start + width, :D].reshape(width, HEADS, HEAD)
        v_blk = wide_kv[start : start + width, D:].reshape(width, HEADS, HEAD)
        scores = (
            jnp.einsum("qhd,khd->hqk", q_blk, k_blk, preferred_element_type=jnp.float32) * 0.125
        )
        mask = window_mask(
            tag_query[start : start + block_rows],
            wide_tag[start : start + width],
            block_rows,
            width,
        )
        return (jnp.where(mask[None], scores, -1e30), q_blk, k_blk, v_blk)

    attended = []
    log_totals = []
    for number in range(blocks):
        scores, q_blk, k_blk, v_blk = block_scores(number * block_rows)
        largest = jnp.max(scores, axis=-1, keepdims=True)
        raised = jnp.exp(scores - largest)
        total = jnp.sum(raised, axis=-1, keepdims=True)
        probs = raised / total
        log_totals.append(largest + jnp.log(total))
        mixed = jnp.einsum(
            "hqk,khd->qhd", probs.astype(jnp.bfloat16), v_blk, preferred_element_type=jnp.float32
        )
        attended.append(mixed.reshape(block_rows, D))
    attn_out = jnp.concatenate(attended, 0).astype(jnp.bfloat16)
    mid = stream + jnp.dot(attn_out, full_out, preferred_element_type=jnp.float32)
    normed_m, factor_m = layer_norm(mid)
    h_mlp = (normed_m * gain_two).astype(jnp.bfloat16)
    gate_up = jnp.dot(h_mlp, full_in, preferred_element_type=jnp.float32)
    hidden_out, glu_pull = jax.vjp(glu_piece, gate_up)
    hidden = hidden_out.astype(jnp.bfloat16)
    result = mid + jnp.dot(hidden, full_down, preferred_element_type=jnp.float32)
    output = result.astype(jnp.bfloat16)
    grad_down = left_dot(hidden, cotangent)
    grad_hidden = right_dot(cotangent, full_down)
    grad_gate_up = glu_pull(grad_hidden)[0].astype(jnp.bfloat16)
    grad_inw = left_dot(h_mlp, grad_gate_up)
    grad_hmlp = right_dot(grad_gate_up, full_in)
    grad_gain_two = jnp.sum(grad_hmlp * normed_m, axis=0)
    grad_mid = cotangent.astype(jnp.float32) + norm_back(grad_hmlp * gain_two, normed_m, factor_m)
    grad_branch = grad_mid.astype(jnp.bfloat16)
    grad_outw = left_dot(attn_out, grad_branch)
    grad_attn = right_dot(grad_branch, full_out).astype(jnp.bfloat16)
    grad_wide = jnp.zeros((count + 2 * HALF, 2 * D), jnp.float32)
    grad_queries = []
    for number in range(blocks):
        start = number * block_rows
        scores, q_blk, k_blk, v_blk = block_scores(start)
        probs = jnp.exp(scores - log_totals[number])
        probs_low = probs.astype(jnp.bfloat16)
        grad_blk = grad_attn[start : start + block_rows].reshape(block_rows, HEADS, HEAD)
        grad_probs = jnp.einsum("qhd,khd->hqk", grad_blk, v_blk, preferred_element_type=jnp.float32)
        inner = jnp.sum(probs * grad_probs, axis=-1, keepdims=True)
        grad_scores = (probs * (grad_probs - inner)).astype(jnp.bfloat16)
        grad_qblk = (
            jnp.einsum("hqk,khd->qhd", grad_scores, k_blk, preferred_element_type=jnp.float32)
            * 0.125
        )
        grad_kblk = (
            jnp.einsum("hqk,qhd->khd", grad_scores, q_blk, preferred_element_type=jnp.float32)
            * 0.125
        )
        grad_vblk = jnp.einsum(
            "hqk,qhd->khd", probs_low, grad_blk, preferred_element_type=jnp.float32
        )
        grad_queries.append(grad_qblk.reshape(block_rows, D))
        grad_wide = grad_wide.at[start : start + width].add(
            jnp.concatenate([grad_kblk.reshape(width, D), grad_vblk.reshape(width, D)], 1)
        )
    from_above = shifted(grad_wide[:HALF].astype(jnp.bfloat16), ("dp", "seq"), -1).astype(
        jnp.float32
    )
    from_below = shifted(grad_wide[count + HALF :].astype(jnp.bfloat16), ("dp", "seq"), 1).astype(
        jnp.float32
    )
    grad_kv = grad_wide[HALF : HALF + count]
    grad_kv = grad_kv.at[:HALF].add(from_below)
    grad_kv = grad_kv.at[count - HALF :].add(from_above)
    grad_query = jnp.concatenate(grad_queries, 0)
    grad_keys = grad_kv[:, :D]
    grad_qkv = jnp.concatenate(
        [
            grad_query * cosine - rotate(grad_query) * sine,
            grad_keys * cosine - rotate(grad_keys) * sine,
            grad_kv[:, D:],
        ],
        1,
    ).astype(jnp.bfloat16)
    grad_qkvw = left_dot(h_attn, grad_qkv)
    grad_hattn = right_dot(grad_qkv, full_qkv)
    grad_gain_one = jnp.sum(grad_hattn * normed_a, axis=0)
    grad_tokens = grad_mid + norm_back(grad_hattn * gain_one, normed_a, factor_a)
    copies = lax.axis_size("dp")
    row_sums = (
        lax.psum_scatter(grad_qkvw, "dp", scatter_dimension=0, tiled=True),
        lax.psum_scatter(grad_outw, "dp", scatter_dimension=0, tiled=True),
        lax.psum_scatter(grad_inw, "dp", scatter_dimension=0, tiled=True),
        lax.psum_scatter(grad_down, "dp", scatter_dimension=0, tiled=True),
        lax.psum_scatter(tiled(grad_gain_one, copies), "dp", scatter_dimension=0, tiled=True),
        lax.psum_scatter(tiled(grad_gain_two, copies), "dp", scatter_dimension=0, tiled=True),
    )
    final = (
        lax.psum_scatter(row_sums[0], "seq", scatter_dimension=1, tiled=True),
        lax.psum_scatter(row_sums[1], "seq", scatter_dimension=1, tiled=True),
        lax.psum_scatter(row_sums[2], "seq", scatter_dimension=1, tiled=True),
        lax.psum_scatter(row_sums[3], "seq", scatter_dimension=1, tiled=True),
        lax.psum_scatter(row_sums[4][0], "seq", scatter_dimension=0, tiled=True),
        lax.psum_scatter(row_sums[5][0], "seq", scatter_dimension=0, tiled=True),
    )
    gain_grad_one = final[4]
    gain_grad_two = final[5]
    return (
        output,
        grad_tokens,
        final[0],
        final[1],
        final[2],
        final[3],
        gain_grad_one,
        gain_grad_two,
    )


def solution(mesh):
    placed = (
        P(("dp", "seq"), None),
        P(("dp", "seq")),
        P(("dp", "seq")),
        P("dp", "seq"),
        P("dp", "seq"),
        P("dp", "seq"),
        P("dp", "seq"),
        P("seq"),
        P("seq"),
        P(("dp", "seq"), None),
    )
    return jax.shard_map(
        on_device,
        mesh=mesh,
        in_specs=placed,
        out_specs=(
            P(("dp", "seq"), None),
            P(("dp", "seq"), None),
            P("dp", "seq"),
            P("dp", "seq"),
            P("dp", "seq"),
            P("dp", "seq"),
            P("seq"),
            P("seq"),
        ),
        check_vma=False,
    )
```

profile of v0, /device:TPU:0, one launch (start us, length us, event | category | flops | bytes accessed | tf_op | source)
XLA Modules:
  0.0 1097.3 jit_solution(3463880330074620418)
XLA Ops:
  8.7 63.8 %all-gather.7.cloned.1.call-done = bf16[384,2304]{0,1:T(8,128)(2,1)} async-done(((bf16[384,144]{0,1:T(8,128)(2,1)}), bf16[384,2304]{0,1:T(8,128)(2,1)}) %all-gather.7.cloned.1.call-update) | async-done | bytes 1769488 | tf_op jit(solution)/shard_map/all_gather | solution.py:97
  72.6 45.2 %all_gather.33 = bf16[384,768]{0,1:T(8,128)(2,1)} all-gather(bf16[384,48]{0,1:T(8,128)(2,1)} %param.22), channel_id=1, replica_groups=mesh['dp'=2,'seq'=16] {'seq'}, dimensions={1}, use_global_device_ids=true | all-gather | bytes 626688 | tf_op jit(solution)/shard_map/all_gather | solution.py:98
  117.8 16.7 %all-gather.13.cloned.1.call-done = bf16[384,2304]{0,1:T(8,128)(2,1)} async-done(((bf16[384,144]{0,1:T(8,128)(2,1)}), bf16[384,2304]{0,1:T(8,128)(2,1)}) %all-gather.13.cloned.1.call-update) | async-done | bytes 1769488 | tf_op jit(solution)/shard_map/all_gather | solution.py:99
  134.7 3.3 collective-permute-start.1
  139.3 45.0 %all_gather.38 = bf16[576,768]{0,1:T(8,128)(2,1)S(1)} all-gather(bf16[576,48]{0,1:T(8,128)(2,1)S(1)} %copy-done.35), channel_id=1, replica_groups=mesh['dp'=2,'seq'=16] {'seq'}, dimensions={1}, use_global_device_ids=true | all-gather | bytes 940032 | tf_op jit(solution)/shard_map/all_gather | solution.py:100
  187.5 37.5 %all-reduce.11 = (bf16[768]{0:T(1024)(128)(2,1)S(1)}, bf16[768]{0:T(1024)(128)(2,1)S(1)}) all-reduce(bf16[768]{0:T(1024)(128)(2,1)S(1)} %dynamic-update-slice.12, bf16[768]{0:T(1024)(128)(2,1)S(1)} %dynamic-update-slice.13), channel_id=1, replica_groups=mesh['dp'=2,'seq'=16] {'seq'}, use_global_device_ids=true, to_apply=%add.3 | all-reduce | flops 1536 | bytes 6144
  227.2 2.8 copy.114
  232.0 3.5 copy.100
  237.1 6.2 fusion.51
  244.7 3.6 fusion.61
  249.2 3.5 copy.105
  252.7 3.5 copy.101
  256.3 3.7 slice_negate_fusion.1
  260.0 3.5 maximum_multiply_fusion.1
  263.5 3.6 copy.106
  267.1 3.9 copy.102
  271.0 6.7 add_convert_fusion.2
  277.7 3.7 collective-permute-start
  289.1 3.8 pad_maximum_fusion.10
  301.6 4.5 fusion.67
  306.1 3.4 fusion.1
  311.7 5.8 fusion.42
  317.5 3.3 fusion.68
  320.7 3.4 fusion
  326.3 5.3 fusion.43
  331.6 2.9 fusion.69
  336.6 10.7 fusion.59
  347.3 14.9 %fusion.41 = (f32[1024,1152]{1,0:T(8,128)}, f32[1024,1152]{1,0:T(8,128)S(1)}, f32[1024,1152]{1,0:T(8,128)S(1)}) fusion(f32[1024,2304]{1,0:T(8,128)} %fusion.59, bf16[1024,768]{1,0:T(8,128)(2,1)S(1)} %copy-done.32, bf16[1152,768]{1,0:T(8,128)(2,1)} %all-gather.17.cloned.1.call-done), kind=kOutput, calls=%fused_computation.100 | convolution fusion | flops 1888616448 | bytes 22216704 | tf_op jit(solution)/shard_map/dot_general | solution.py:81
  362.2 3.6 multiply_add_fusion
  365.9 10.0 multiply_reduce_fusion.2
  378.6 2.8 fusion.45
  381.5 5.9 fusion.70
  387.5 4.0 convolution_convert_fusion
  392.8 10.6 fusion.48
  405.0 17.0 %multiply_reduce_fusion = (f32[12,512]{1,0:T(8,128)S(1)}, f32[12,512,640]{2,1,0:T(8,128)}) fusion(f32[12,512,640]{2,1,0:T(8,128)} %copy-done, f32[12,512]{1,0:T(8,128)S(1)} %log_add_fusion, bf16[512,12,64]{0,2,1:T(8,128)(2,1)S(1)} %bitcast.126, bf16[640,12,64]{0,2,1:T(8,128)(2,1)S(1)} %bitcast.134), kind=kOutput, calls=%fused_computation.1 | convolution fusion | flops 515106816 | bytes 33275904 | tf_op jit(solution)/shard_map/qhd,khd->hqk/dot_general | solution.py:189
  422.0 7.8 multiply_convert_fusion
  433.0 11.5 %multiply_reduce_fusion.1 = (f32[12,512]{1,0:T(8,128)S(1)}, f32[12,512,640]{2,1,0:T(8,128)}) fusion(f32[12,512,640]{2,1,0:T(8,128)} %copy-done.1, f32[12,512]{1,0:T(8,128)S(1)} %log_add_fusion.1, bf16[512,12,64]{0,2,1:T(8,128)(2,1)} %bitcast.128, bf16[640,12,64]{0,2,1:T(8,128)(2,1)} %bitcast.131), kind=kOutput, calls=%fused_computation.4 | convolution fusion | flops 515106816 | bytes 33275904 | tf_op jit(solution)/shard_map/qhd,khd->hqk/dot_general | solution.py:189
  444.5 11.2 %multiply_convert_fusion.1 = bf16[12,512,640]{2,1,0:T(8,128)(2,1)S(1)} fusion(f32[12,512,640]{2,1,0:T(8,128)} %get-tuple-element.156, f32[12,512,640]{2,1,0:T(8,128)} %copy-done.1, f32[12,512]{1,0:T(8,128)S(1)} %get-tuple-element.155, f32[12,512]{1,0:T(8,128)S(1)} %log_add_fusion.1), kind=kLoop, calls=%fused_computation.3 | loop fusion | flops 15728640 | bytes 39370752 | tf_op jit(solution)/shard_map/convert_element_type | solution.py:191
  455.7 3.1 copy-done.3
  460.2 8.3 fusion.6
  468.5 4.1 fusion.4
  474.8 5.2 constant_dynamic-update-slice_fusion
  481.2 4.4 collective-permute-start.4
  485.6 3.7 convolution_multiply_fusion.2
  492.0 4.3 slice.252
  499.3 4.8 scatter-add.16
  508.2 4.6 scatter-add.19
  512.8 3.3 slice.298
  521.9 4.3 fusion.35
  526.2 9.1 fusion.37
  538.4 2.9 copy.128
  541.4 5.5 copy.126
  546.9 4.9 reduce-scatter.17.cloned.1.call-done
  551.8 5.2 copy.122
  558.9 6.7 add_convert_fusion.1
  568.1 9.2 fusion.30
  577.3 3.3 all-reduce.10
  581.9 42.5 %all-reduce.9 = (f32[768]{0:T(1024)S(1)}, f32[768]{0:T(1024)S(1)}) all-reduce(f32[768]{0:T(1024)S(1)} %dynamic-slice_reduce_fusion.1, f32[768]{0:T(1024)S(1)} %dynamic-slice_reduce_fusion), channel_id=11, replica_groups=mesh['dp'=2,'seq'=16] {'seq'}, use_global_device_ids=true, to_apply=%region_24.25.clone | all-reduce | flops 1536 | bytes 12288
  625.7 5.5 fusion.29
  631.2 3.5 copy.116
  634.7 47.1 %reduce-scatter.27.cloned.1.call-done = f32[48,384]{1,0:T(8,128)} async-done(((f32[768,384]{1,0:T(8,128)}), f32[48,384]{1,0:T(8,128)}) %reduce-scatter.27.cloned.1.call-update) | async-done | bytes 73744
  681.8 130.3 %reduce-scatter.31.cloned.1.call-done = f32[48,576]{1,0:T(8,128)} async-done(((f32[768,576]{1,0:T(8,128)}), f32[48,576]{1,0:T(8,128)}) %reduce-scatter.31.cloned.1.call-update) | async-done | bytes 110608
  812.2 139.1 %reduce-scatter.29.cloned.1.call-done = f32[144,384]{1,0:T(8,128)} async-done(((f32[2304,384]{1,0:T(8,128)}), f32[144,384]{1,0:T(8,128)}) %reduce-scatter.29.cloned.1.call-update) | async-done | bytes 221200
  951.3 139.2 %reduce-scatter.25.cloned.1.call-done = f32[144,384]{1,0:T(8,128)} async-done(((f32[2304,384]{1,0:T(8,128)}), f32[144,384]{1,0:T(8,128)}) %reduce-scatter.25.cloned.1.call-update) | async-done | bytes 221200
  (236 shorter events, 74.6 us)
Async XLA Ops:
  7.2 127.4 %copy-start.44 = (s32[1024]{0:T(1024)S(1)}, s32[1024]{0:T(1024)}, u32[]{:S(2)}) copy-start(s32[1024]{0:T(1024)} %param.20) | copy-start | bytes 12292
  7.2 127.4 %copy-start.43 = (s32[1024]{0:T(1024)S(1)}, s32[1024]{0:T(1024)}, u32[]{:S(2)}) copy-start(s32[1024]{0:T(1024)} %param.19) | copy-start | bytes 12292
  7.2 132.1 %copy-start.35 = (bf16[576,48]{0,1:T(8,128)(2,1)S(1)}, bf16[576,48]{0,1:T(8,128)(2,1)}, u32[]{:S(2)}) copy-start(bf16[576,48]{0,1:T(8,128)(2,1)} %param.24) | copy-start | bytes 165892
  7.2 65.3 %all-gather.7.cloned.1.call-start = ((), (), s32[]{:S(2)}) async-start(), calls=%async_computation.8 | async-start | bytes 1880064 | tf_op jit(solution)/shard_map/all_gather | solution.py:97
  7.9 126.6 %all-gather.13.cloned.1.call-start = ((), (), s32[]{:S(2)}) async-start(), calls=%async_computation.11 | async-start | bytes 1880064 | tf_op jit(solution)/shard_map/all_gather | solution.py:99
  8.7 228.4 %all-gather.9.cloned.1.call-start = ((), (), s32[]{:S(2)}) async-start(), calls=%async_computation.9 | async-start | bytes 5308416 | tf_op jit(solution)/shard_map/all_gather | solution.py:105
  72.5 259.1 %all-gather.11.cloned.1.call-start = ((), (), s32[]{:S(2)}) async-start(), calls=%async_computation.10 | async-start | bytes 1769472 | tf_op jit(solution)/shard_map/all_gather | solution.py:106
  117.7 68.0 %copy-start.45 = (u32[32]{0:T(128)S(1)}, u32[32]{0:T(128)}, u32[]{:S(2)}) copy-start(u32[32]{0:T(128)} %constant.221) | copy-start | bytes 388
  117.7 69.3 %copy-start.46 = (bf16[48]{0:T(256)(128)(2,1)S(1)}, bf16[48]{0:T(256)(128)(2,1)}, u32[]{:S(2)}) copy-start(bf16[48]{0:T(256)(128)(2,1)} %param.25) | copy-start | bytes 292
  117.7 69.6 %copy-start.47 = (bf16[48]{0:T(256)(128)(2,1)S(1)}, bf16[48]{0:T(256)(128)(2,1)}, u32[]{:S(2)}) copy-start(bf16[48]{0:T(256)(128)(2,1)} %param.26) | copy-start | bytes 292
  117.7 107.3 %copy-start.31 = (bf16[1024,768]{1,0:T(8,128)(2,1)S(1)}, bf16[1024,768]{1,0:T(8,128)(2,1)}, u32[]{:S(2)}) copy-start(bf16[1024,768]{1,0:T(8,128)(2,1)} %param.18) | copy-start | bytes 4718596
  117.8 218.9 %all-gather.15.cloned.1.call-start = ((), (), s32[]{:S(2)}) async-start(), calls=%async_computation.12 | async-start | bytes 5308416 | tf_op jit(solution)/shard_map/all_gather | solution.py:107
  134.5 212.8 %all-gather.17.cloned.1.call-start = ((), (), s32[]{:S(2)}) async-start(), calls=%async_computation.13 | async-start | bytes 2654208 | tf_op jit(solution)/shard_map/all_gather | solution.py:108
  134.7 100.8 %collective-permute-start.1 = (s32[64]{0:T(128)S(1)}, s32[64]{0:T(128)S(1)}, u32[]{:S(2)}, u32[]{:S(2)}) collective-permute-start(s32[64]{0:T(128)S(1)} %get-tuple-element.140), channel_id=1, source_target_pairs={{0,1},{1,2},{2,3},{3,4},{4,5},{5,6},{6,7},{7,8},{8,9},{9,10},{10,1... | collective-permute-start | bytes 776 | tf_op jit(solution)/shard_map/ppermute | solution.py:22
  138.0 97.5 %collective-permute-start.3 = (s32[64]{0:T(128)S(1)}, s32[64]{0:T(128)S(1)}, u32[]{:S(2)}, u32[]{:S(2)}) collective-permute-start(s32[64]{0:T(128)S(1)} %get-tuple-element.141), channel_id=1, source_target_pairs={{1,0},{2,1},{3,2},{4,3},{5,4},{6,5},{7,6},{8,7},{9,8},{10,9},{11,1... | collective-permute-start | bytes 776 | tf_op jit(solution)/shard_map/ppermute | solution.py:23
  185.7 349.7 %reduce-scatter.19.cloned.1.call-start = ((), (), s32[]{:S(2)}) async-start(), calls=%async_computation.15 | async-start | bytes 3538944 | tf_op jit(solution)/shard_map/reduce_scatter | solution.py:233
  225.0 12.1 %copy-start.38 = (f32[768]{0:T(1024)}, f32[768]{0:T(1024)S(1)}, u32[]{:S(2)}) copy-start(f32[768]{0:T(1024)S(1)} %convert_element_type.72) | copy-start | bytes 9220
  225.8 105.8 %copy-start.4 = (bf16[1024,768]{0,1:T(8,128)(2,1)}, bf16[1024,768]{0,1:T(8,128)(2,1)S(1)}, u32[]{:S(2)}) copy-start(bf16[1024,768]{0,1:T(8,128)(2,1)S(1)} %copy.99) | copy-start | bytes 4718596
  226.1 11.0 %copy-start.36 = (f32[1024]{0:T(1024)}, f32[1024]{0:T(1024)S(1)}, u32[]{:S(2)}) copy-start(f32[1024]{0:T(1024)S(1)} %broadcast_multiply_fusion.5) | copy-start | bytes 12292
  226.5 10.5 copy-start.40
  227.1 4.9 copy-start.30
  227.2 32.8 %copy-start.28 = (f32[1024,64]{0,1:T(8,128)}, f32[1024,64]{0,1:T(8,128)S(1)}, u32[]{:S(2)}) copy-start(f32[1024,64]{0,1:T(8,128)S(1)} %get-tuple-element.161) | copy-start | bytes 786436
  243.3 5.9 copy-start.8
  271.0 6.7 copy-start.9
  277.7 10.9 collective-permute-start
  281.4 7.7 collective-permute-start.2
  294.4 23.0 %copy-start.18 = (bf16[640,768]{0,1:T(8,128)(2,1)}, bf16[640,768]{0,1:T(8,128)(2,1)S(1)}, u32[]{:S(2)}) copy-start(bf16[640,768]{0,1:T(8,128)(2,1)S(1)} %copy.108) | copy-start | bytes 2949124
  294.5 7.1 copy-start.15
  306.1 5.5 copy-start
  306.1 5.5 copy-start.26
  311.7 5.8 copy-start.13
  311.7 5.8 copy-start.34
  320.7 5.5 copy-start.1
  320.7 5.5 copy-start.25
  326.3 5.3 copy-start.48
  336.6 10.7 copy-start.32
  347.3 14.9 %copy-start.17 = (f32[1024,2304]{1,0:T(8,128)S(1)}, f32[1024,2304]{1,0:T(8,128)}, u32[]{:S(2)}) copy-start(f32[1024,2304]{1,0:T(8,128)} %fusion.59) | copy-start | bytes 28311556
  365.9 10.1 copy-start.24
  365.9 10.1 copy-start.22
  381.5 156.9 %reduce-scatter.23.cloned.1.call-start = ((), (), s32[]{:S(2)}) async-start(), calls=%async_computation.17 | async-start | bytes 5308416 | tf_op jit(solution)/shard_map/reduce_scatter | solution.py:235
  387.5 153.9 %reduce-scatter.21.cloned.1.call-start = ((), (), s32[]{:S(2)}) async-start(), calls=%async_computation.16 | async-start | bytes 10616832 | tf_op jit(solution)/shard_map/reduce_scatter | solution.py:234
  403.4 148.4 %reduce-scatter.17.cloned.1.call-start = ((), (), s32[]{:S(2)}) async-start(), calls=%async_computation.14 | async-start | bytes 10616832 | tf_op jit(solution)/shard_map/reduce_scatter | solution.py:232
  403.5 18.5 %slice-start = ((s8[15728640]{0:T(1024)(128)(4,1)}), s8[4194304]{0:T(1024)(128)(4,1)S(1)}, s32[]{:S(2)}) async-start(s8[15728640]{0:T(1024)(128)(4,1)} %bitcast.91), calls=%async_computation.22 | async-start | bytes 8388608
  405.0 17.0 %slice-start.1 = ((s8[15728640]{0:T(1024)(128)(4,1)}), s8[4194304]{0:T(1024)(128)(4,1)S(1)}, s32[]{:S(2)}) async-start(s8[15728640]{0:T(1024)(128)(4,1)} %bitcast.91), calls=%async_computation.23 | async-start | bytes 8388608
  405.0 17.0 %slice-start.2 = ((s8[15728640]{0:T(1024)(128)(4,1)}), s8[4194304]{0:T(1024)(128)(4,1)S(1)}, s32[]{:S(2)}) async-start(s8[15728640]{0:T(1024)(128)(4,1)} %bitcast.91), calls=%async_computation.24 | async-start | bytes 8388608
  405.0 17.0 %slice-start.3 = ((s8[15728640]{0:T(1024)(128)(4,1)}), s8[3145728]{0:T(1024)(128)(4,1)S(1)}, s32[]{:S(2)}) async-start(s8[15728640]{0:T(1024)(128)(4,1)} %bitcast.91), calls=%async_computation.25 | async-start | bytes 6291456
  422.0 7.9 copy-start.16
  444.5 14.3 %copy-start.14 = (bf16[512,768]{0,1:T(8,128)(2,1)S(1)}, bf16[512,768]{0,1:T(8,128)(2,1)}, u32[]{:S(2)}) copy-start(bf16[512,768]{0,1:T(8,128)(2,1)} %copy.107) | copy-start | bytes 2359300
  472.6 13.0 %slice-start.4 = ((s8[7864320]{0:T(1024)(128)(4,1)}), s8[4194304]{0:T(1024)(128)(4,1)S(1)}, s32[]{:S(2)}) async-start(s8[7864320]{0:T(1024)(128)(4,1)} %bitcast.93), calls=%async_computation.26 | async-start | bytes 8388608
  472.6 16.7 %slice-start.6 = ((s8[7864320]{0:T(1024)(128)(4,1)}), s8[4194304]{0:T(1024)(128)(4,1)S(1)}, s32[]{:S(2)}) async-start(s8[7864320]{0:T(1024)(128)(4,1)} %bitcast.95), calls=%async_computation.28 | async-start | bytes 8388608
  474.8 10.8 slice-start.5
  474.8 14.6 %slice-start.7 = ((s8[7864320]{0:T(1024)(128)(4,1)}), s8[3670016]{0:T(1024)(128)(4,1)S(1)}, s32[]{:S(2)}) async-start(s8[7864320]{0:T(1024)(128)(4,1)} %bitcast.95), calls=%async_computation.29 | async-start | bytes 7340032
  481.2 8.2 copy-start.19
  481.2 17.8 %collective-permute-start.4 = (bf16[64,1536]{0,1:T(8,128)(2,1)S(1)}, bf16[64,1536]{0,1:T(8,128)(2,1)S(1)}, u32[]{:S(2)}, u32[]{:S(2)}) collective-permute-start(bf16[64,1536]{0,1:T(8,128)(2,1)S(1)} %slice.301), channel_id=1, source_target_pairs={{0,1},{1,2},{2,3},{3,4},{4,5},{5,6},{6,7},{7,8},{8,9},{9,10},{10,1... | collective-permute-start | bytes 589832 | tf_op jit(solution)/shard_map/ppermute | solution.py:31
  491.9 5.7 copy-start.6
  496.3 10.3 collective-permute-start.5
  521.9 4.3 copy-start.39
  521.9 4.3 copy-start.41
  535.3 146.5 %reduce-scatter.27.cloned.1.call-start = ((), (), s32[]{:S(2)}) async-start(), calls=%async_computation.19 | async-start | bytes 1253376
  538.1 274.1 %reduce-scatter.31.cloned.1.call-start = ((), (), s32[]{:S(2)}) async-start(), calls=%async_computation.21 | async-start | bytes 2088960
  541.3 410.0 %reduce-scatter.29.cloned.1.call-start = ((), (), s32[]{:S(2)}) async-start(), calls=%async_computation.20 | async-start | bytes 3760128
  546.9 543.7 %reduce-scatter.25.cloned.1.call-start = ((), (), s32[]{:S(2)}) async-start(), calls=%async_computation.18 | async-start | bytes 3760128
  558.8 9.3 copy-start.33
  568.1 9.2 copy-start.42
  (19 other events, 45.4 us)
Sparse Core Ops, SparseCore 0:
  10.8 61.6 all-gather.6
  75.3 59.1 all-gather.12
  136.1 11.3 all-gather.8
  148.9 10.3 all-gather.10
  160.7 13.7 all-gather.14
  185.8 6.7 all-gather.16
  381.6 8.0 reduce-scatter.18
  392.0 12.5 reduce-scatter.22
  406.9 16.6 reduce-scatter.20
  535.5 16.2 reduce-scatter.16
  557.1 124.6 reduce-scatter.26
  687.1 125.0 reduce-scatter.30
  818.7 132.6 reduce-scatter.28
  957.7 132.8 reduce-scatter.24
where the time goes:
time: 1110 us; the launch traced here: 1100 us
  waiting for transfers between devices  546 us (49%)
  blocking collectives  174 us (16%)
  matrix products  162 us (15%)
  local copies, waits for them, and re-layouts  110 us (10%)
  other arithmetic  73.2 us (7%)
  between operations  16.4 us (1%)
  starting transfers between devices  16.1 us (1%)
    unnamed x18, waiting for transfers between devices  457 us
    unnamed x3, blocking collectives  83.3 us
    all_gather x1, waiting for transfers between devices, on_device(): lax.all_gather(w_qkv, 'seq', axis=1, tiled=True)  63.8 us
    unnamed x142, local copies, waits for them, and re-layouts  46.3 us
    all_gather x1, blocking collectives, on_device(): lax.all_gather(w_out, 'seq', axis=1, tiled=True)  45.2 us
    all_gather x1, blocking collectives, on_device(): lax.all_gather(w_down, 'seq', axis=1, tiled=True)  45 us
    dot_general x4, matrix products, right_dot(): lax.dot_general(left, right, (((1,), (1,)), ((), ())), preferred_element_...  38 us
    dot_general x2, matrix products, on_device(): jnp.einsum('qhd,khd->hqk', grad_blk, v_blk, preferred_element_type=jnp.fl...  28.5 us
  transfers between devices with their start and end apart: 20, of which 9 were waited for; matrix products, arithmetic and copies ran while one was open for 27% of the time, Pallas kernels for 0%

commit v1 on v0

--- a/solution.py
+++ b/solution.py
@@ -87,27 +87,61 @@
     return jax.nn.gelu(gate_up[:, :FF], approximate=False) * gate_up[:, FF:]
 
 
-def tiled(value, copies):
-    return jnp.broadcast_to(value[None, :], (copies, value.shape[0]))
+def gather_blocks(parts, n_dp, n_seq):
+    flat = jnp.concatenate([p.reshape(-1) for p in parts])
+    every = lax.all_gather(flat, ("dp", "seq"), axis=0, tiled=False)
+    out = []
+    offset = 0
+    for p in parts:
+        size = p.size
+        piece = every[:, offset : offset + size]
+        offset += size
+        if p.ndim == 2:
+            rows, cols = p.shape
+            out.append(
+                piece.reshape(n_dp, n_seq, rows, cols)
+                .transpose(0, 2, 1, 3)
+                .reshape(n_dp * rows, n_seq * cols)
+            )
+        else:
+            out.append(piece[:n_seq].reshape(-1))
+    return out
+
+
+def scatter_blocks(parts, n_dp, n_seq):
+    pieces = []
+    for p in parts:
+        if p.ndim == 2:
+            rows, cols = p.shape
+            pieces.append(
+                p.reshape(n_dp, rows // n_dp, n_seq, cols // n_seq)
+                .transpose(0, 2, 1, 3)
+                .reshape(n_dp * n_seq, -1)
+            )
+        else:
+            block = p.reshape(1, n_seq, -1)
+            pieces.append(jnp.broadcast_to(block, (n_dp, n_seq, block.shape[-1])).reshape(n_dp * n_seq, -1))
+    flat = jnp.concatenate(pieces, 1)
+    mine = lax.psum_scatter(flat, ("dp", "seq"), scatter_dimension=0, tiled=False)
+    out = []
+    offset = 0
+    for p in parts:
+        if p.ndim == 2:
+            rows, cols = p.shape
+            shape = (rows // n_dp, cols // n_seq)
+        else:
+            shape = (p.shape[0] // n_seq,)
+        size = math.prod(shape)
+        out.append(mine[offset : offset + size].reshape(shape))
+        offset += size
+    return out
 
 
 def on_device(tokens, doc_start, real, w_qkv, w_out, w_in, w_down, gain_attn, gain_mlp, cotangent):
     count = tokens.shape[0]
-    col_parts = (
-        lax.all_gather(w_qkv, "seq", axis=1, tiled=True),
-        lax.all_gather(w_out, "seq", axis=1, tiled=True),
-        lax.all_gather(w_in, "seq", axis=1, tiled=True),
-        lax.all_gather(w_down, "seq", axis=1, tiled=True),
-        lax.all_gather(gain_attn, "seq", axis=0, tiled=True),
-        lax.all_gather(gain_mlp, "seq", axis=0, tiled=True),
-    )
-    full_qkv, full_out, full_in, full_down = (
-        lax.all_gather(col_parts[0], "dp", axis=0, tiled=True),
-        lax.all_gather(col_parts[1], "dp", axis=0, tiled=True),
-        lax.all_gather(col_parts[2], "dp", axis=0, tiled=True),
-        lax.all_gather(col_parts[3], "dp", axis=0, tiled=True),
-    )
-    gain_one, gain_two = (col_parts[4], col_parts[5])
+    n_dp, n_seq = lax.axis_size("dp"), lax.axis_size("seq")
+    full_qkv, gain_one = gather_blocks((w_qkv, gain_attn), n_dp, n_seq)
+    full_out, full_in, full_down, gain_two = gather_blocks((w_out, w_in, w_down, gain_mlp), n_dp, n_seq)
     gain_one = gain_one.astype(jnp.float32)
     gain_two = gain_two.astype(jnp.float32)
     stream = tokens.astype(jnp.float32)
@@ -227,35 +261,10 @@
     grad_hattn = right_dot(grad_qkv, full_qkv)
     grad_gain_one = jnp.sum(grad_hattn * normed_a, axis=0)
     grad_tokens = grad_mid + norm_back(grad_hattn * gain_one, normed_a, factor_a)
-    copies = lax.axis_size("dp")
-    row_sums = (
-        lax.psum_scatter(grad_qkvw, "dp", scatter_dimension=0, tiled=True),
-        lax.psum_scatter(grad_outw, "dp", scatter_dimension=0, tiled=True),
-        lax.psum_scatter(grad_inw, "dp", scatter_dimension=0, tiled=True),
-        lax.psum_scatter(grad_down, "dp", scatter_dimension=0, tiled=True),
-        lax.psum_scatter(tiled(grad_gain_one, copies), "dp", scatter_dimension=0, tiled=True),
-        lax.psum_scatter(tiled(grad_gain_two, copies), "dp", scatter_dimension=0, tiled=True),
-    )
-    final = (
-        lax.psum_scatter(row_sums[0], "seq", scatter_dimension=1, tiled=True),
-        lax.psum_scatter(row_sums[1], "seq", scatter_dimension=1, tiled=True),
-        lax.psum_scatter(row_sums[2], "seq", scatter_dimension=1, tiled=True),
-        lax.psum_scatter(row_sums[3], "seq", scatter_dimension=1, tiled=True),
-        lax.psum_scatter(row_sums[4][0], "seq", scatter_dimension=0, tiled=True),
-        lax.psum_scatter(row_sums[5][0], "seq", scatter_dimension=0, tiled=True),
-    )
-    gain_grad_one = final[4]
-    gain_grad_two = final[5]
-    return (
-        output,
-        grad_tokens,
-        final[0],
-        final[1],
-        final[2],
-        final[3],
-        gain_grad_one,
-        gain_grad_two,
-    )
+    final = scatter_blocks(
+        (grad_qkvw, grad_outw, grad_inw, grad_down, grad_gain_one, grad_gain_two), n_dp, n_seq
+    )
+    return (output, grad_tokens) + tuple(final)
 
 
 def solution(mesh):

time: 1110 us -> 1100 us (level)
  local copies, waits for them, and re-layouts: 110 us -> 365 us
  blocking collectives: 174 us -> 0 us
  waiting for transfers between devices: 546 us -> 485 us
  matrix products: 162 us -> 133 us
    reshape x0 -> x21, local copies, waits for them, and re-layouts: none -> 119 us  [the longest x4 46.6 us: scatter_blocks(): pieces.append(p.reshape(n_dp, rows // n_dp, n_seq, cols // n_seq).transpo...]
    all_gather x2 -> x0, blocking collectives: 90.2 us -> none  [the longest x1 45.2 us: on_device(): lax.all_gather(w_out, 'seq', axis=1, tiled=True)]
    unnamed x3 -> x0, blocking collectives: 83.3 us -> none
    all_gather x6 -> x0, waiting for transfers between devices: 80.5 us -> none  [the longest x1 63.8 us: on_device(): lax.all_gather(w_qkv, 'seq', axis=1, tiled=True)]
    transpose x0 -> x8, local copies, waits for them, and re-layouts: none -> 79.4 us  [the longest x4 43.1 us: scatter_blocks(): pieces.append(p.reshape(n_dp, rows // n_dp, n_seq, cols // n_seq).transpo...]
    unnamed x142 -> x170, local copies, waits for them, and re-layouts: 46.3 us -> 76.1 us
    unnamed x18 -> x4, waiting for transfers between devices: 457 us -> 485 us
    all_gather x1 -> x2, local copies, waits for them, and re-layouts: 1.28 us -> 22.9 us  [gather_blocks(): every = lax.all_gather(flat, ('dp', 'seq'), axis=0, tiled=False)]
  transfers between devices with their start and end apart: 20 -> 8, of which waited for: 9 -> 2; matrix products, arithmetic and copies ran while one was open for 27% -> 12% of each run, Pallas kernels for 0% -> 0%
where the time goes in v1:
time: 1100 us
  waiting for transfers between devices  485 us (44%)
  local copies, waits for them, and re-layouts  365 us (33%)
  matrix products  133 us (12%)
  other arithmetic  78.5 us (7%)
  starting transfers between devices  18.3 us (2%)
  between operations  15.5 us (1%)
    unnamed x4, waiting for transfers between devices  485 us
    unnamed x170, local copies, waits for them, and re-layouts  76.1 us
    reshape x4, local copies, waits for them, and re-layouts, scatter_blocks(): pieces.append(p.reshape(n_dp, rows // n_dp, n_seq, cols // n_seq).transpo...  46.6 us
    transpose x4, local copies, waits for them, and re-layouts, scatter_blocks(): pieces.append(p.reshape(n_dp, rows // n_dp, n_seq, cols // n_seq).transpo...  43.1 us
    transpose x4, local copies, waits for them, and re-layouts, gather_blocks(): out.append(piece.reshape(n_dp, n_seq, rows, cols).transpose(0, 2, 1, 3).r...  36.3 us
    reshape x4, local copies, waits for them, and re-layouts, gather_blocks(): piece.reshape(n_dp, n_seq, rows, cols).transpose(0, 2, 1, 3)  36.2 us
    dot_general x4, matrix products, right_dot(): lax.dot_general(left, right, (((1,), (1,)), ((), ())), preferred_element_...  29.6 us
    reshape x4, local copies, waits for them, and re-layouts, scatter_blocks(): p.reshape(n_dp, rows // n_dp, n_seq, cols // n_seq).transpose(0, 2, 1, 3)  29.4 us
  transfers between devices with their start and end apart: 8, of which 2 were waited for; matrix products, arithmetic and copies ran while one was open for 12% of the time, Pallas kernels for 0%

profile of v1, /device:TPU:0, one launch (start us, length us, event | category | flops | bytes accessed | tf_op | source)
XLA Modules:
  0.0 1095.7 jit_solution(15093451907326433929)
XLA Ops:
  17.3 4.4 dynamic-update-slice.13
  26.1 4.8 collective-permute-start.1
  37.7 3.8 copy.98
  44.6 183.0 %all-reduce.12.cloned.1.call-done = (bf16[3245568]{0:T(1024)(128)(2,1)}, bf16[1771008]{0:T(1024)(128)(2,1)}) async-done(((bf16[3245568]{0:T(1024)(128)(2,1)}, bf16[1771008]{0:T(1024)(128)(2,1)}), (bf16[3245568]{0:T(1024)(128)(2,1)}, bf16[1771008]{0:T(1024)(128)(2,1)})) %all-reduce.12.cloned.1.call-update) | async-done | bytes 10033168
  227.7 8.3 reshape.503
  236.6 4.1 slice.302
  240.8 13.3 %reshape.457 = bf16[2,16,384,144]{3,2,1,0:T(8,128)(2,1)} reshape(bf16[32,55296]{1,0:T(8,128)(2,1)} %slice.302) | data formatting | bytes 7077888 | tf_op jit(solution)/shard_map/reshape | solution.py:102
  254.1 12.1 %copy.97 = bf16[2,384,16,144]{1,0,3,2:T(2,128)(2,1)} copy(bf16[2,384,16,144]{3,1,2,0:T(8,128)(2,1)} %bitcast.140) | data formatting | bytes 7077888 | tf_op jit(solution)/shard_map/transpose | solution.py:103
  268.9 4.2 fusion.50
  278.8 14.6 %reshape.504 = bf16[32,101424]{1,0:T(8,128)(2,1)} reshape(bf16[3245568]{0:T(1024)(128)(2,1)} %get-tuple-element.88) | data formatting | bytes 12982272 | tf_op jit(solution)/shard_map/all_gather | solution.py:92
  296.9 3.6 copy.103
  300.5 3.7 slice_negate_fusion.1
  304.2 3.6 maximum_multiply_fusion.1
  311.3 3.6 copy.104
  314.8 6.6 add_convert_fusion.2
  322.3 4.0 collective-permute-start
  330.1 4.2 reshape.472
  334.3 5.5 copy.113
  343.1 12.8 %reshape.474 = bf16[2,16,384,144]{3,2,1,0:T(8,128)(2,1)} reshape(bf16[32,55296]{1,0:T(8,128)(2,1)S(1)} %slice-done.9) | data formatting | bytes 7077888 | tf_op jit(solution)/shard_map/reshape | solution.py:102
  355.9 11.7 %copy.114 = bf16[2,384,16,144]{1,0,3,2:T(2,128)(2,1)} copy(bf16[2,384,16,144]{3,1,2,0:T(8,128)(2,1)} %bitcast.141) | data formatting | bytes 7077888 | tf_op jit(solution)/shard_map/transpose | solution.py:103
  367.6 4.5 copy.141
  372.1 5.9 reshape.476
  378.0 6.9 copy.115
  385.0 5.1 reshape.477
  405.3 3.8 fusion
  410.8 5.1 fusion.42
  424.7 5.1 fusion.41
  432.2 4.2 fusion.58
  436.3 13.2 %bitcast_multiply_fusion.1 = (f32[1024,1152]{1,0:T(8,128)}, f32[1024,1152]{1,0:T(8,128)S(1)}, f32[1152,1024]{0,1:T(8,128)S(1)}) fusion(f32[1024,2304]{1,0:T(8,128)S(1)} %fusion.58, bf16[1024,768]{1,0:T(8,128)(2,1)S(1)} %copy-done.45, bf16[1152,768]{0,1:T(8,128)(2,1)S(1)} %copy-done.42), kind=kOutput, calls=%fused_computation.32 | convolution fusion | flops 1888616448 | bytes 22216704 | tf_op jit(solution)/shard_map/dot_general | solution.py:81
  449.5 3.8 multiply_add_fusion
  453.3 9.5 fusion.47
  462.8 8.6 multiply_reduce_fusion.2
  480.2 15.1 %multiply_reduce_fusion = (f32[12,512]{1,0:T(8,128)S(1)}, f32[12,512,640]{2,1,0:T(8,128)}) fusion(f32[12,512,640]{2,1,0:T(8,128)} %copy-done.1, f32[12,512]{1,0:T(8,128)S(1)} %log_add_fusion, bf16[512,12,64]{0,2,1:T(8,128)(2,1)S(1)} %bitcast.174, bf16[640,12,64]{0,2,1:T(8,128)(2,1)S(1)} %bitcast.180), kind=kOutput, calls=%fused_computation.1 | convolution fusion | flops 515106816 | bytes 33275904 | tf_op jit(solution)/shard_map/qhd,khd->hqk/dot_general | solution.py:223
  495.2 8.4 fusion.4
  503.7 8.1 multiply_reduce_fusion.1
  511.7 4.1 fusion.6
  515.9 11.2 %multiply_convert_fusion = bf16[12,512,640]{2,1,0:T(8,128)(2,1)S(1)} fusion(f32[12,512,640]{2,1,0:T(8,128)} %get-tuple-element.148, f32[12,512,640]{2,1,0:T(8,128)} %copy-done.1, f32[12,512]{1,0:T(8,128)S(1)} %get-tuple-element.147, f32[12,512]{1,0:T(8,128)S(1)} %log_add_fusion), kind=kLoop, calls=%fused_computation | loop fusion | flops 15728640 | bytes 39370752 | tf_op jit(solution)/shard_map/convert_element_type | solution.py:225
  530.2 8.0 multiply_convert_fusion.1
  545.9 4.7 slice.322
  557.5 10.1 reshape.491
  567.6 14.0 %copy.124 = f32[2,16,384,144]{3,2,1,0:T(8,128)} copy(f32[2,16,384,144]{2,0,3,1:T(2,128)} %bitcast.138) | data formatting | bytes 14155776 | tf_op jit(solution)/shard_map/transpose | solution.py:118
  581.6 14.2 %reshape.492 = f32[32,55296]{1,0:T(8,128)} reshape(f32[2,16,384,144]{3,2,1,0:T(8,128)} %copy.124) | data formatting | bytes 14155776 | tf_op jit(solution)/shard_map/reshape | solution.py:119
  595.8 3.9 reshape.489
  599.6 6.5 copy.122
  606.1 7.5 reshape.490
  615.6 5.3 collective-permute-start.4
  622.1 6.1 fusion.68
  628.3 5.9 reshape.493
  634.2 8.6 copy.126
  642.8 10.7 reshape.494
  657.3 5.0 scatter-add.16
  664.8 4.9 scatter-add.19
  677.2 4.5 fusion.35
  681.7 8.9 fusion.37
  690.6 6.2 fusion.30
  696.8 9.6 reshape.487
  706.3 14.0 %copy.120 = f32[2,16,384,144]{3,2,1,0:T(8,128)} copy(f32[2,16,384,144]{2,0,3,1:T(2,128)} %bitcast.139) | data formatting | bytes 14155776 | tf_op jit(solution)/shard_map/transpose | solution.py:118
  720.4 14.2 %reshape.488 = f32[32,55296]{1,0:T(8,128)} reshape(f32[2,16,384,144]{3,2,1,0:T(8,128)} %copy.120) | data formatting | bytes 14155776 | tf_op jit(solution)/shard_map/reshape | solution.py:119
  734.5 6.4 constant_dynamic-update-slice_fusion.3
  744.3 6.5 constant_dynamic-update-slice_fusion.1
  757.0 6.0 add_convert_fusion.1
  766.0 5.4 fusion.29
  771.4 3.8 copy.128
  775.2 301.9 %all-reduce.10.cloned.1.call-done = f32[32,156768]{1,0:T(8,128)} async-done(((f32[32,156768]{1,0:T(8,128)}), f32[32,156768]{1,0:T(8,128)}) %all-reduce.10.cloned.1.call-update) | async-done | bytes 20066320
  (268 shorter events, 143.1 us)
Async XLA Ops:
  7.2 220.5 %all-reduce.12.cloned.1.call-start = ((), (), s32[]{:S(2)}) async-start(), calls=%async_computation.1 | async-start | bytes 20070400
  26.0 1051.1 %all-reduce.10.cloned.1.call-start = ((), (), s32[]{:S(2)}) async-start(), calls=%async_computation | async-start | bytes 40140800
  26.1 16.9 %collective-permute-start.1 = (s32[64]{0:T(128)S(1)}, s32[64]{0:T(128)S(1)}, u32[]{:S(2)}, u32[]{:S(2)}) collective-permute-start(s32[64]{0:T(128)S(1)} %get-tuple-element.132), channel_id=1, source_target_pairs={{0,1},{1,2},{2,3},{3,4},{4,5},{5,6},{6,7},{7,8},{8,9},{9,10},{10,1... | collective-permute-start | bytes 776 | tf_op jit(solution)/shard_map/ppermute | solution.py:22
  31.0 12.1 %collective-permute-start.3 = (s32[64]{0:T(128)S(1)}, s32[64]{0:T(128)S(1)}, u32[]{:S(2)}, u32[]{:S(2)}) collective-permute-start(s32[64]{0:T(128)S(1)} %get-tuple-element.133), channel_id=1, source_target_pairs={{1,0},{2,1},{3,2},{4,3},{5,4},{6,5},{7,6},{8,7},{9,8},{10,9},{11,1... | collective-permute-start | bytes 776 | tf_op jit(solution)/shard_map/ppermute | solution.py:23
  34.2 234.7 %copy-start.6 = (bf16[1024,768]{0,1:T(8,128)(2,1)}, bf16[1024,768]{0,1:T(8,128)(2,1)S(1)}, u32[]{:S(2)}) copy-start(bf16[1024,768]{0,1:T(8,128)(2,1)S(1)} %copy.95) | copy-start | bytes 4718596
  34.8 269.4 %copy-start.39 = (f32[1024,64]{0,1:T(8,128)}, f32[1024,64]{0,1:T(8,128)S(1)}, u32[]{:S(2)}) copy-start(f32[1024,64]{0,1:T(8,128)S(1)} %get-tuple-element.151) | copy-start | bytes 786436
  35.1 233.8 %copy-start.53 = (f32[1024]{0:T(1024)}, f32[1024]{0:T(1024)S(1)}, u32[]{:S(2)}) copy-start(f32[1024]{0:T(1024)S(1)} %broadcast_multiply_fusion.5) | copy-start | bytes 12292
  35.6 233.3 %copy-start.57 = (f32[1024]{0:T(1024)}, f32[1024]{0:T(1024)S(1)}, u32[]{:S(2)}) copy-start(f32[1024]{0:T(1024)S(1)} %add_rsqrt_fusion.1) | copy-start | bytes 12292
  37.7 3.8 copy-start.44
  240.8 28.1 %copy-start.55 = (f32[768]{0:T(1024)}, f32[768]{0:T(1024)S(1)}, u32[]{:S(2)}) copy-start(f32[768]{0:T(1024)S(1)} %reshape.501) | copy-start | bytes 9220
  268.9 4.3 copy-start.35
  273.1 5.5 copy-start.10
  278.8 42.6 %copy-start.14 = (bf16[1024,768]{1,0:T(8,128)(2,1)}, bf16[1024,768]{1,0:T(8,128)(2,1)S(1)}, u32[]{:S(2)}) copy-start(bf16[1024,768]{1,0:T(8,128)(2,1)S(1)} %slice.371) | copy-start | bytes 4718596
  321.4 6.3 copy-start.12
  322.3 67.8 %collective-permute-start = (bf16[64,1536]{1,0:T(8,128)(2,1)}, bf16[64,1536]{1,0:T(8,128)(2,1)}, u32[]{:S(2)}, u32[]{:S(2)}) collective-permute-start(bf16[64,1536]{1,0:T(8,128)(2,1)} %get-tuple-element.110), channel_id=1, source_target_pairs={{0,1},{1,2},{2,3},{3,4},{4,5},{5,6},{6,7},{7,8},{8,9},{9,10},{10,1... | collective-permute-start | bytes 589832 | tf_op jit(solution)/shard_map/ppermute | solution.py:22
  326.3 63.8 %collective-permute-start.2 = (bf16[64,1536]{1,0:T(8,128)(2,1)}, bf16[64,1536]{1,0:T(8,128)(2,1)}, u32[]{:S(2)}, u32[]{:S(2)}) collective-permute-start(bf16[64,1536]{1,0:T(8,128)(2,1)} %get-tuple-element.111), channel_id=1, source_target_pairs={{1,0},{2,1},{3,2},{4,3},{5,4},{6,5},{7,6},{8,7},{9,8},{10,9},{11,1... | collective-permute-start | bytes 589832 | tf_op jit(solution)/shard_map/ppermute | solution.py:23
  334.3 8.8 slice-start.9
  367.6 4.5 slice-start.10
  385.0 5.1 copy-start.13
  385.0 5.1 copy-start.15
  395.2 10.1 copy-start.23
  395.2 6.8 copy-start.19
  395.2 6.8 copy-start.50
  399.4 16.5 %copy-start.25 = (bf16[640,768]{0,1:T(8,128)(2,1)}, bf16[640,768]{0,1:T(8,128)(2,1)S(1)}, u32[]{:S(2)}) copy-start(bf16[640,768]{0,1:T(8,128)(2,1)S(1)} %copy.109) | copy-start | bytes 2949124
  405.2 5.5 copy-start
  405.2 5.5 copy-start.31
  410.8 5.1 copy-start.21
  410.8 5.1 copy-start.49
  415.9 14.0 %copy-start.61 = (bf16[12,64,512]{2,1,0:T(8,128)(2,1)}, bf16[12,64,512]{2,1,0:T(8,128)(2,1)S(1)}, u32[]{:S(2)}) copy-start(bf16[12,64,512]{2,1,0:T(8,128)(2,1)S(1)} %fusion.42) | copy-start | bytes 2359300
  419.2 5.5 copy-start.1
  419.2 5.5 copy-start.33
  424.7 5.1 copy-start.7
  424.7 5.1 copy-start.51
  431.3 40.1 %copy-start.17 = (f32[1024,768]{0,1:T(8,128)}, f32[1024,768]{0,1:T(8,128)S(1)}, u32[]{:S(2)}) copy-start(f32[1024,768]{0,1:T(8,128)S(1)} %get-tuple-element.142) | copy-start | bytes 9437188
  432.2 4.2 copy-start.42
  432.2 4.2 copy-start.45
  453.3 9.5 copy-start.38
  462.8 8.6 copy-start.29
  480.2 23.5 %slice-start = ((s8[15728640]{0:T(1024)(128)(4,1)}), s8[4194304]{0:T(1024)(128)(4,1)S(1)}, s32[]{:S(2)}) async-start(s8[15728640]{0:T(1024)(128)(4,1)} %bitcast.132), calls=%async_computation.2 | async-start | bytes 8388608
  480.2 23.5 %slice-start.1 = ((s8[15728640]{0:T(1024)(128)(4,1)}), s8[4194304]{0:T(1024)(128)(4,1)S(1)}, s32[]{:S(2)}) async-start(s8[15728640]{0:T(1024)(128)(4,1)} %bitcast.132), calls=%async_computation.3 | async-start | bytes 8388608
  480.2 23.5 %slice-start.2 = ((s8[15728640]{0:T(1024)(128)(4,1)}), s8[4194304]{0:T(1024)(128)(4,1)S(1)}, s32[]{:S(2)}) async-start(s8[15728640]{0:T(1024)(128)(4,1)} %bitcast.132), calls=%async_computation.4 | async-start | bytes 8388608
  495.2 8.4 slice-start.3
  495.2 8.4 copy-start.32
  515.9 11.2 %copy-start.22 = (bf16[512,768]{0,1:T(8,128)(2,1)S(1)}, bf16[512,768]{0,1:T(8,128)(2,1)}, u32[]{:S(2)}) copy-start(bf16[512,768]{0,1:T(8,128)(2,1)} %copy.108) | copy-start | bytes 2359300
  530.2 8.0 copy-start.20
  541.6 10.7 slice-start.6
  543.1 9.2 slice-start.7
  543.1 11.8 %slice-start.4 = ((s8[7864320]{0:T(1024)(128)(4,1)}), s8[3670016]{0:T(1024)(128)(4,1)S(1)}, s32[]{:S(2)}) async-start(s8[7864320]{0:T(1024)(128)(4,1)} %bitcast.134), calls=%async_computation.6 | async-start | bytes 7340032
  545.9 6.3 copy-start.4
  545.9 6.4 copy-start.24
  545.9 9.0 slice-start.5
  557.5 117.7 %copy-start.9 = (f32[12,64,512]{2,1,0:T(8,128)}, f32[12,64,512]{2,1,0:T(8,128)S(1)}, u32[]{:S(2)}) copy-start(f32[12,64,512]{2,1,0:T(8,128)S(1)} %convolution_multiply_fusion.2) | copy-start | bytes 4718596
  615.6 39.4 %collective-permute-start.4 = (bf16[64,1536]{0,1:T(8,128)(2,1)}, bf16[64,1536]{0,1:T(8,128)(2,1)}, u32[]{:S(2)}, u32[]{:S(2)}) collective-permute-start(bf16[64,1536]{0,1:T(8,128)(2,1)} %slice.373), channel_id=1, source_target_pairs={{0,1},{1,2},{2,3},{3,4},{4,5},{5,6},{6,7},{7,8},{8,9},{9,10},{10,1... | collective-permute-start | bytes 589832 | tf_op jit(solution)/shard_map/ppermute | solution.py:31
  620.9 41.5 %collective-permute-start.5 = (bf16[64,1536]{0,1:T(8,128)(2,1)S(1)}, bf16[64,1536]{0,1:T(8,128)(2,1)}, u32[]{:S(2)}, u32[]{:S(2)}) collective-permute-start(bf16[64,1536]{0,1:T(8,128)(2,1)S(1)} %slice.372), channel_id=1, source_target_pairs={{1,0},{2,1},{3,2},{4,3},{5,4},{6,5},{7,6},{8,7},{9,8},{10,9},{11,1... | collective-permute-start | bytes 589832 | tf_op jit(solution)/shard_map/ppermute | solution.py:31
  669.7 3.7 copy-start.5
  677.1 4.5 copy-start.8
  677.2 4.5 copy-start.46
  677.2 4.5 copy-start.54
  677.2 4.5 copy-start.56
  677.2 4.5 copy-start.58
  681.7 8.9 copy-start.36
  681.7 8.9 copy-start.47
  681.7 8.9 copy-start.48
  744.3 6.5 copy-start.16
  (20 other events, 45.9 us)
Sparse Core Ops, SparseCore 0:
  26.1 201.5 all-reduce.11
  755.7 321.4 all-reduce.9

commit v2 on v1

--- a/solution.py
+++ b/solution.py
@@ -87,9 +87,17 @@
     return jax.nn.gelu(gate_up[:, :FF], approximate=False) * gate_up[:, FF:]
 
 
+def padded_to(flat, unit):
+    extra = (-flat.shape[0]) % unit
+    return jnp.pad(flat, (0, extra)) if extra else flat
+
+
 def gather_blocks(parts, n_dp, n_seq):
     flat = jnp.concatenate([p.reshape(-1) for p in parts])
-    every = lax.all_gather(flat, ("dp", "seq"), axis=0, tiled=False)
+    size = flat.shape[0]
+    flat = padded_to(flat, 8 * 128)
+    every = lax.all_gather(flat.reshape(8, -1), ("dp", "seq"), axis=0, tiled=True)
+    every = every.reshape(n_dp * n_seq, -1)[:, :size]
     out = []
     offset = 0
     for p in parts:
@@ -122,7 +130,13 @@
             block = p.reshape(1, n_seq, -1)
             pieces.append(jnp.broadcast_to(block, (n_dp, n_seq, block.shape[-1])).reshape(n_dp * n_seq, -1))
     flat = jnp.concatenate(pieces, 1)
-    mine = lax.psum_scatter(flat, ("dp", "seq"), scatter_dimension=0, tiled=False)
+    size = flat.shape[1]
+    extra = (-size) % (8 * 128)
+    if extra:
+        flat = jnp.pad(flat, ((0, 0), (0, extra)))
+    flat = flat.reshape(n_dp * n_seq * 8, -1)
+    half = lax.psum_scatter(flat, "dp", scatter_dimension=0, tiled=True)
+    mine = lax.psum_scatter(half, "seq", scatter_dimension=0, tiled=True).reshape(-1)
     out = []
     offset = 0
     for p in parts:
@@ -261,10 +275,20 @@
     grad_hattn = right_dot(grad_qkv, full_qkv)
     grad_gain_one = jnp.sum(grad_hattn * normed_a, axis=0)
     grad_tokens = grad_mid + norm_back(grad_hattn * gain_one, normed_a, factor_a)
-    final = scatter_blocks(
-        (grad_qkvw, grad_outw, grad_inw, grad_down, grad_gain_one, grad_gain_two), n_dp, n_seq
-    )
-    return (output, grad_tokens) + tuple(final)
+    late_out, late_in, late_down, late_gain_two = scatter_blocks(
+        (grad_outw, grad_inw, grad_down, grad_gain_two), n_dp, n_seq
+    )
+    late_qkv, late_gain_one = scatter_blocks((grad_qkvw, grad_gain_one), n_dp, n_seq)
+    return (
+        output,
+        grad_tokens,
+        late_qkv,
+        late_out,
+        late_in,
+        late_down,
+        late_gain_one,
+        late_gain_two,
+    )
 
 
 def solution(mesh):

time: 1100 us -> 993 us (0.903)
  waiting for transfers between devices: 485 us -> 354 us
  local copies, waits for them, and re-layouts: 365 us -> 343 us
  other arithmetic: 78.5 us -> 99 us
  matrix products: 133 us -> 151 us
    unnamed x4 -> x7, waiting for transfers between devices: 485 us -> 145 us
    reduce_scatter x0 -> x3, waiting for transfers between devices: none -> 162 us  [the longest x1 140 us: scatter_blocks(): lax.psum_scatter(half, 'seq', scatter_dimension=0, tiled=True).reshape(-1)]
    all_gather x0 -> x2, waiting for transfers between devices: none -> 40 us  [gather_blocks(): lax.all_gather(flat.reshape(8, -1), ('dp', 'seq'), axis=0, tiled=True)]
    unnamed x170 -> x151, local copies, waits for them, and re-layouts: 76.1 us -> 38.9 us
    reshape x0 -> x8, local copies, waits for them, and re-layouts: none -> 32.2 us  [the longest x2 16.8 us: scatter_blocks(): flat = flat.reshape(n_dp * n_seq * 8, -1)]
    all_gather x2 -> x0, local copies, waits for them, and re-layouts: 22.9 us -> none  [gather_blocks(): every = lax.all_gather(flat, ('dp', 'seq'), axis=0, tiled=False)]
    concatenate x0 -> x2, other arithmetic: none -> 15.7 us  [scatter_blocks(): flat = jnp.concatenate(pieces, 1)]
  transfers between devices with their start and end apart: 8 -> 12, of which waited for: 2 -> 6; matrix products, arithmetic and copies ran while one was open for 12% -> 31% of each run, Pallas kernels for 0% -> 0%
where the time goes in v2:
time: 993 us; the launch traced here: 979 us
  waiting for transfers between devices  354 us (36%)
  local copies, waits for them, and re-layouts  343 us (35%)
  matrix products  151 us (15%)
  other arithmetic  99 us (10%)
  between operations  16.2 us (2%)
  starting transfers between devices  15.6 us (2%)
    unnamed x7, waiting for transfers between devices  145 us
    reduce_scatter x1, waiting for transfers between devices, scatter_blocks(): lax.psum_scatter(half, 'seq', scatter_dimension=0, tiled=True).reshape(-1)  140 us
    reshape x4, local copies, waits for them, and re-layouts, gather_blocks(): piece.reshape(n_dp, n_seq, rows, cols).transpose(0, 2, 1, 3)  47 us
    reshape x4, local copies, waits for them, and re-layouts, scatter_blocks(): pieces.append(p.reshape(n_dp, rows // n_dp, n_seq, cols // n_seq).transpo...  47 us
    transpose x4, local copies, waits for them, and re-layouts, scatter_blocks(): pieces.append(p.reshape(n_dp, rows // n_dp, n_seq, cols // n_seq).transpo...  43.6 us
    all_gather x2, waiting for transfers between devices, gather_blocks(): lax.all_gather(flat.reshape(8, -1), ('dp', 'seq'), axis=0, tiled=True)  40 us
    unnamed x151, local copies, waits for them, and re-layouts  38.9 us
    transpose x4, local copies, waits for them, and re-layouts, gather_blocks(): out.append(piece.reshape(n_dp, n_seq, rows, cols).transpose(0, 2, 1, 3).r...  34.8 us
  transfers between devices with their start and end apart: 12, of which 6 were waited for; matrix products, arithmetic and copies ran while one was open for 31% of the time, Pallas kernels for 0%

profile of v2, /device:TPU:0, one launch (start us, length us, event | category | flops | bytes accessed | tf_op | source)
XLA Modules:
  0.0 978.9 jit_solution(16408850958304640506)
XLA Ops:
  11.0 4.8 collective-permute-start.1
  34.4 40.0 %all-gather.3.cloned.1.call-done = bf16[256,7040]{1,0:T(8,128)(2,1)} async-done(((bf16[8,7040]{1,0:T(8,128)(2,1)}), bf16[256,7040]{1,0:T(8,128)(2,1)}) %all-gather.3.cloned.1.call-update) | async-done | bytes 3604496 | tf_op jit(solution)/shard_map/all_gather | solution.py:99
  74.5 5.2 reshape.472
  79.6 4.0 slice.298
  84.4 13.4 %reshape.473 = bf16[2,16,384,144]{3,2,1,0:T(8,128)(2,1)} reshape(bf16[32,55296]{1,0:T(8,128)(2,1)} %slice.298) | data formatting | bytes 7077888 | tf_op jit(solution)/shard_map/reshape | solution.py:110
  97.8 11.7 %copy.93 = bf16[2,384,16,144]{1,0,3,2:T(2,128)(2,1)} copy(bf16[2,384,16,144]{3,1,2,0:T(8,128)(2,1)} %bitcast.135) | data formatting | bytes 7077888 | tf_op jit(solution)/shard_map/transpose | solution.py:111
  112.2 4.2 fusion.54
  121.9 4.0 copy.95
  144.0 6.9 add_convert_fusion.2
  150.9 4.2 collective-permute-start
  185.0 7.2 fusion.76
  192.2 7.4 fusion
  200.2 8.2 fusion.42
  208.5 5.8 fusion.41
  214.3 7.5 reshape.489
  223.7 14.9 %reshape.490 = bf16[2,16,384,48]{3,2,1,0:T(8,128)(2,1)} reshape(bf16[32,18432]{1,0:T(8,128)(2,1)S(1)} %slice-done.6) | data formatting | bytes 2359296 | tf_op jit(solution)/shard_map/reshape | solution.py:110
  238.6 4.4 copy.109
  249.7 12.9 %reshape.492 = bf16[2,16,384,144]{3,2,1,0:T(8,128)(2,1)} reshape(bf16[32,55296]{1,0:T(8,128)(2,1)S(1)} %slice-done.7) | data formatting | bytes 7077888 | tf_op jit(solution)/shard_map/reshape | solution.py:110
  262.6 11.7 %copy.110 = bf16[2,384,16,144]{1,0,3,2:T(2,128)(2,1)} copy(bf16[2,384,16,144]{3,1,2,0:T(8,128)(2,1)} %bitcast.136) | data formatting | bytes 7077888 | tf_op jit(solution)/shard_map/transpose | solution.py:111
  274.3 4.6 copy.137
  278.9 5.9 reshape.494
  284.8 7.0 copy.111
  291.8 5.1 reshape.495
  296.9 6.3 fusion.68
  303.3 13.2 %bitcast_multiply_fusion.1 = (f32[1024,1152]{1,0:T(8,128)}, f32[1024,1152]{1,0:T(8,128)S(1)}, f32[1152,1024]{0,1:T(8,128)S(1)}) fusion(f32[1024,2304]{1,0:T(8,128)S(1)} %fusion.68, bf16[1024,768]{1,0:T(8,128)(2,1)S(1)} %copy-done.34, bf16[1152,768]{0,1:T(8,128)(2,1)S(1)} %copy-done.31), kind=kOutput, calls=%fused_computation.38 | convolution fusion | flops 1888616448 | bytes 22216704 | tf_op jit(solution)/shard_map/dot_general | solution.py:81
  316.5 4.7 multiply_add_fusion
  321.2 12.5 %multiply_reduce_fusion.2 = (f32[768]{0:T(1024)}, f32[1024]{0:T(1024)S(1)}, f32[1024]{0:T(1024)S(1)}, f32[1024,768]{0,1:T(8,128)}) fusion(f32[1024,768]{0,1:T(8,128)} %copy-done.7, f32[1024]{0:T(1024)S(1)} %copy-done.55, f32[1024]{0:T(1024)S(1)} %broadcast_multiply_fusion.4, f32[768]{0:T(1024)S(1)} %reshape.524, bf16[768,2304]{0,1:T(8,128)(2,1)} %bitcast.179, ...), kind=kOutput, calls=%fused_computation.86 | convolution fusion | flops 3634885888 | bytes 19290112 | tf_op jit(solution)/shard_map/dot_general | solution.py:81
  341.4 7.7 multiply_reduce_fusion
  349.1 4.1 fusion.4
  353.2 13.9 %multiply_reduce_fusion.1 = (f32[12,512]{1,0:T(8,128)S(1)}, f32[12,512,640]{2,1,0:T(8,128)}) fusion(f32[12,512,640]{2,1,0:T(8,128)} %get-tuple-element.134, f32[12,512]{1,0:T(8,128)S(1)} %copy-done.44, bf16[512,12,64]{0,2,1:T(8,128)(2,1)S(1)} %bitcast.167, bf16[640,12,64]{0,2,1:T(8,128)(2,1)S(1)} %bitcast.173), kind=kOutput, calls=%fused_computation.4 | convolution fusion | flops 515106816 | bytes 33275904 | tf_op jit(solution)/shard_map/qhd,khd->hqk/dot_general | solution.py:237
  367.1 8.3 fusion.6
  375.5 11.2 %multiply_convert_fusion.1 = bf16[12,512,640]{2,1,0:T(8,128)(2,1)S(1)} fusion(f32[12,512,640]{2,1,0:T(8,128)} %get-tuple-element.140, f32[12,512,640]{2,1,0:T(8,128)} %get-tuple-element.134, f32[12,512]{1,0:T(8,128)S(1)} %get-tuple-element.139, f32[12,512]{1,0:T(8,128)S(1)} %copy-done.44), kind=kLoop, calls=%fused_computation.3 | loop fusion | flops 15728640 | bytes 39370752 | tf_op jit(solution)/shard_map/convert_element_type | solution.py:239
  390.7 7.4 multiply_convert_fusion
  409.8 4.4 slice.318
  418.0 5.4 scatter-add.16
  423.4 4.4 collective-permute-done.5
  430.2 4.9 scatter-add.19
  442.6 4.6 fusion.35
  447.3 8.9 fusion.37
  456.2 6.0 fusion.30
  462.2 9.5 reshape.505
  471.7 14.0 %copy.116 = f32[2,16,384,144]{3,2,1,0:T(8,128)} copy(f32[2,16,384,144]{2,0,3,1:T(2,128)} %bitcast.133) | data formatting | bytes 14155776 | tf_op jit(solution)/shard_map/transpose | solution.py:126
  485.7 14.3 %reshape.506 = f32[32,55296]{1,0:T(8,128)} reshape(f32[2,16,384,144]{3,2,1,0:T(8,128)} %copy.116) | data formatting | bytes 14155776 | tf_op jit(solution)/shard_map/reshape | solution.py:127
  500.2 6.3 select_maximum_fusion.3
  506.5 6.7 reshape.508
  514.5 4.7 fusion.44
  519.3 4.1 reshape.511
  523.4 6.9 copy.118
  530.3 7.4 reshape.512
  537.7 11.6 %fusion.47 = f32[768,2304]{0,1:T(8,128)} fusion(f32[1024,1152]{1,0:T(8,128)} %get-tuple-element.90, f32[1024,1152]{1,0:T(8,128)} %get-tuple-element.88, f32[1024,768]{0,1:T(8,128)} %copy-done.7, f32[768]{0:T(1024)S(1)} %copy-done.52, f32[1024]{0:T(1024)S(1)} %copy-done.56, f32[1024]{0:T(1024)S(1)} %copy-done.48), kind=kOutput, calls=%fused_computation.130 | convolution fusion | flops 3631742976 | bytes 19672064 | tf_op jit(solution)/shard_map/dot_general | solution.py:75
  549.3 9.5 reshape.513
  558.8 14.0 %copy.120 = f32[2,16,384,144]{3,2,1,0:T(8,128)} copy(f32[2,16,384,144]{2,0,3,1:T(2,128)} %bitcast.134) | data formatting | bytes 14155776 | tf_op jit(solution)/shard_map/transpose | solution.py:126
  572.9 14.5 %reshape.514 = f32[32,55296]{1,0:T(8,128)} reshape(f32[2,16,384,144]{3,2,1,0:T(8,128)} %copy.120) | data formatting | bytes 14155776 | tf_op jit(solution)/shard_map/reshape | solution.py:127
  587.4 5.7 fusion.78
  593.1 5.9 reshape.515
  599.0 8.6 copy.122
  607.6 10.7 %reshape.516 = f32[32,27648]{1,0:T(8,128)} reshape(f32[2,16,576,48]{3,2,1,0:T(8,128)} %copy.122) | data formatting | bytes 7077888 | tf_op jit(solution)/shard_map/reshape | solution.py:127
  618.4 9.4 select_maximum_fusion
  627.8 10.1 %reshape.518 = f32[256,12800]{1,0:T(8,128)} reshape(f32[32,102400]{1,0:T(8,128)} %select_maximum_fusion) | data formatting | bytes 26214400 | tf_op jit(solution)/shard_map/reshape | solution.py:137
  638.6 22.0 %reduce-scatter.6.cloned.1.call-done = f32[128,12800]{1,0:T(8,128)} async-done(((f32[256,12800]{1,0:T(8,128)}), f32[128,12800]{1,0:T(8,128)}) %reduce-scatter.6.cloned.1.call-update) | async-done | bytes 6553616 | tf_op jit(solution)/shard_map/reduce_scatter | solution.py:138
  662.5 6.0 add_convert_fusion.1
  671.1 5.6 fusion.29
  680.3 144.3 %all-reduce.10.cloned.1.call-done = f32[128,7040]{1,0:T(8,128)} async-done(((f32[128,7040]{1,0:T(8,128)}), f32[128,7040]{1,0:T(8,128)}) %all-reduce.10.cloned.1.call-update) | async-done | bytes 3604496
  827.2 140.0 %reduce-scatter.8.cloned.1.call-done = f32[8,12800]{1,0:T(8,128)} async-done(((f32[128,12800]{1,0:T(8,128)}), f32[8,12800]{1,0:T(8,128)}) %reduce-scatter.8.cloned.1.call-update) | async-done | bytes 409616 | tf_op jit(solution)/shard_map/reduce_scatter | solution.py:139
  (269 shorter events, 141.7 us)
Async XLA Ops:
  7.2 15.2 %copy-start.33 = (bf16[1024,768]{1,0:T(8,128)(2,1)S(1)}, bf16[1024,768]{1,0:T(8,128)(2,1)}, u32[]{:S(2)}) copy-start(bf16[1024,768]{1,0:T(8,128)(2,1)} %param.18) | copy-start | bytes 4718596
  7.2 67.3 %all-gather.3.cloned.1.call-start = ((), (), s32[]{:S(2)}) async-start(), calls=%async_computation.3 | async-start | bytes 3717120 | tf_op jit(solution)/shard_map/all_gather | solution.py:99
  10.2 204.1 %all-gather.5.cloned.1.call-start = ((), (), s32[]{:S(2)}) async-start(), calls=%async_computation.4 | async-start | bytes 6758400 | tf_op jit(solution)/shard_map/all_gather | solution.py:99
  11.0 21.9 %collective-permute-start.1 = (s32[64]{0:T(128)S(1)}, s32[64]{0:T(128)S(1)}, u32[]{:S(2)}, u32[]{:S(2)}) collective-permute-start(s32[64]{0:T(128)S(1)} %get-tuple-element.126), channel_id=1, source_target_pairs={{0,1},{1,2},{2,3},{3,4},{4,5},{5,6},{6,7},{7,8},{8,9},{9,10},{10,1... | collective-permute-start | bytes 776 | tf_op jit(solution)/shard_map/ppermute | solution.py:22
  15.8 17.1 %collective-permute-start.3 = (s32[64]{0:T(128)S(1)}, s32[64]{0:T(128)S(1)}, u32[]{:S(2)}, u32[]{:S(2)}) collective-permute-start(s32[64]{0:T(128)S(1)} %get-tuple-element.127), channel_id=1, source_target_pairs={{1,0},{2,1},{3,2},{4,3},{5,4},{6,5},{7,6},{8,7},{9,8},{10,9},{11,1... | collective-permute-start | bytes 776 | tf_op jit(solution)/shard_map/ppermute | solution.py:23
  22.3 615.7 %reduce-scatter.4.cloned.1.call-start = ((), (), s32[]{:S(2)}) async-start(), calls=%async_computation.5 | async-start | bytes 10813440 | tf_op jit(solution)/shard_map/reduce_scatter | solution.py:138
  23.2 89.0 %copy-start.3 = (bf16[1024,768]{0,1:T(8,128)(2,1)}, bf16[1024,768]{0,1:T(8,128)(2,1)S(1)}, u32[]{:S(2)}) copy-start(bf16[1024,768]{0,1:T(8,128)(2,1)S(1)} %copy.91) | copy-start | bytes 4718596
  24.1 6.2 copy-start.30
  24.1 109.2 %copy-start.28 = (f32[1024,64]{0,1:T(8,128)}, f32[1024,64]{0,1:T(8,128)S(1)}, u32[]{:S(2)}) copy-start(f32[1024,64]{0,1:T(8,128)S(1)} %get-tuple-element.145) | copy-start | bytes 786436
  24.1 88.1 %copy-start.45 = (f32[1024]{0:T(1024)}, f32[1024]{0:T(1024)S(1)}, u32[]{:S(2)}) copy-start(f32[1024]{0:T(1024)S(1)} %broadcast_multiply_fusion.5) | copy-start | bytes 12292
  24.6 87.6 %copy-start.53 = (f32[1024]{0:T(1024)}, f32[1024]{0:T(1024)S(1)}, u32[]{:S(2)}) copy-start(f32[1024]{0:T(1024)S(1)} %add_rsqrt_fusion.1) | copy-start | bytes 12292
  84.4 27.8 %copy-start.49 = (f32[768]{0:T(1024)}, f32[768]{0:T(1024)S(1)}, u32[]{:S(2)}) copy-start(f32[768]{0:T(1024)S(1)} %reshape.523) | copy-start | bytes 9220
  112.2 4.3 copy-start.26
  116.4 5.5 copy-start.6
  150.9 11.4 %collective-permute-start = (bf16[64,1536]{1,0:T(8,128)(2,1)S(1)}, bf16[64,1536]{1,0:T(8,128)(2,1)}, u32[]{:S(2)}, u32[]{:S(2)}) collective-permute-start(bf16[64,1536]{1,0:T(8,128)(2,1)S(1)} %get-tuple-element.104), channel_id=1, source_target_pairs={{0,1},{1,2},{2,3},{3,4},{4,5},{5,6},{6,7},{7,8},{8,9},{9,10},{10,1... | collective-permute-start | bytes 589832 | tf_op jit(solution)/shard_map/ppermute | solution.py:22
  155.1 10.0 %collective-permute-start.2 = (bf16[64,1536]{1,0:T(8,128)(2,1)S(1)}, bf16[64,1536]{1,0:T(8,128)(2,1)}, u32[]{:S(2)}, u32[]{:S(2)}) collective-permute-start(bf16[64,1536]{1,0:T(8,128)(2,1)S(1)} %get-tuple-element.105), channel_id=1, source_target_pairs={{1,0},{2,1},{3,2},{4,3},{5,4},{6,5},{7,6},{8,7},{9,8},{10,9},{11,1... | collective-permute-start | bytes 589832 | tf_op jit(solution)/shard_map/ppermute | solution.py:23
  170.1 14.9 %copy-start.16 = (bf16[640,768]{0,1:T(8,128)(2,1)}, bf16[640,768]{0,1:T(8,128)(2,1)S(1)}, u32[]{:S(2)}) copy-start(bf16[640,768]{0,1:T(8,128)(2,1)S(1)} %copy.102) | copy-start | bytes 2949124
  170.1 6.8 copy-start.10
  170.2 6.8 copy-start.40
  174.3 5.9 copy-start.14
  180.2 28.2 %copy-start = (f32[12,512,640]{2,1,0:T(8,128)}, f32[12,512,640]{2,1,0:T(8,128)S(1)}, u32[]{:S(2)}) copy-start(f32[12,512,640]{2,1,0:T(8,128)S(1)} %get-tuple-element.132) | copy-start | bytes 47185924
  180.2 4.7 copy-start.12
  180.3 4.7 copy-start.39
  192.2 8.1 copy-start.22
  200.2 8.2 copy-start.24
  243.2 6.5 slice-start.7
  247.0 86.7 %copy-start.47 = (f32[1024]{0:T(1024)}, f32[1024]{0:T(1024)S(1)}, u32[]{:S(2)}) copy-start(f32[1024]{0:T(1024)S(1)} %broadcast_multiply_fusion.4) | copy-start | bytes 12292
  249.7 84.0 %copy-start.51 = (f32[768]{0:T(1024)}, f32[768]{0:T(1024)S(1)}, u32[]{:S(2)}) copy-start(f32[768]{0:T(1024)S(1)} %reshape.524) | copy-start | bytes 9220
  274.3 4.6 slice-start.8
  291.8 5.1 copy-start.8
  291.8 5.1 copy-start.55
  296.9 6.3 copy-start.31
  296.9 6.3 copy-start.34
  321.2 12.6 %copy-start.20 = (bf16[1024,768]{0,1:T(8,128)(2,1)S(1)}, bf16[1024,768]{0,1:T(8,128)(2,1)}, u32[]{:S(2)}) copy-start(bf16[1024,768]{0,1:T(8,128)(2,1)} %copy.113) | copy-start | bytes 4718596
  321.2 18.3 %slice-start = ((s8[15728640]{0:T(1024)(128)(4,1)}), s8[4194304]{0:T(1024)(128)(4,1)S(1)}, s32[]{:S(2)}) async-start(s8[15728640]{0:T(1024)(128)(4,1)} %bitcast.129), calls=%async_computation.9 | async-start | bytes 8388608
  321.2 18.3 %slice-start.1 = ((s8[15728640]{0:T(1024)(128)(4,1)}), s8[4194304]{0:T(1024)(128)(4,1)S(1)}, s32[]{:S(2)}) async-start(s8[15728640]{0:T(1024)(128)(4,1)} %bitcast.129), calls=%async_computation.10 | async-start | bytes 8388608
  321.2 18.3 %slice-start.2 = ((s8[15728640]{0:T(1024)(128)(4,1)}), s8[3145728]{0:T(1024)(128)(4,1)S(1)}, s32[]{:S(2)}) async-start(s8[15728640]{0:T(1024)(128)(4,1)} %bitcast.129), calls=%async_computation.11 | async-start | bytes 6291456
  333.7 3.9 copy-start.42
  349.1 4.1 copy-start.23
  349.1 4.1 copy-start.44
  375.5 11.2 %copy-start.13 = (bf16[512,768]{0,1:T(8,128)(2,1)S(1)}, bf16[512,768]{0,1:T(8,128)(2,1)}, u32[]{:S(2)}) copy-start(bf16[512,768]{0,1:T(8,128)(2,1)} %copy.101) | copy-start | bytes 2359300
  390.7 7.5 copy-start.11
  401.5 5.7 slice-start.4
  403.1 4.1 slice-start.5
  403.1 4.1 copy-start.15
  404.8 12.0 %collective-permute-start.4 = (bf16[64,1536]{0,1:T(8,128)(2,1)S(1)}, bf16[64,1536]{0,1:T(8,128)(2,1)S(1)}, u32[]{:S(2)}, u32[]{:S(2)}) collective-permute-start(bf16[64,1536]{0,1:T(8,128)(2,1)S(1)} %slice.375), channel_id=1, source_target_pairs={{0,1},{1,2},{2,3},{3,4},{4,5},{5,6},{6,7},{7,8},{8,9},{9,10},{10,1... | collective-permute-start | bytes 589832 | tf_op jit(solution)/shard_map/ppermute | solution.py:31
  409.7 30.9 %copy-start.5 = (f32[12,64,512]{2,1,0:T(8,128)}, f32[12,64,512]{2,1,0:T(8,128)S(1)}, u32[]{:S(2)}) copy-start(f32[12,64,512]{2,1,0:T(8,128)S(1)} %convolution_multiply_fusion.2) | copy-start | bytes 4718596
  414.2 13.6 %collective-permute-start.5 = (bf16[64,1536]{0,1:T(8,128)(2,1)S(1)}, bf16[64,1536]{0,1:T(8,128)(2,1)}, u32[]{:S(2)}, u32[]{:S(2)}) collective-permute-start(bf16[64,1536]{0,1:T(8,128)(2,1)S(1)} %slice.374), channel_id=1, source_target_pairs={{1,0},{2,1},{3,2},{4,3},{5,4},{6,5},{7,6},{8,7},{9,8},{10,9},{11,1... | collective-permute-start | bytes 589832 | tf_op jit(solution)/shard_map/ppermute | solution.py:31
  442.6 4.6 copy-start.4
  442.6 4.6 copy-start.36
  442.6 4.6 copy-start.46
  442.6 4.6 copy-start.50
  442.6 4.6 copy-start.54
  447.2 8.9 copy-start.27
  447.2 8.9 copy-start.37
  447.3 8.9 copy-start.38
  513.2 147.5 %reduce-scatter.6.cloned.1.call-start = ((), (), s32[]{:S(2)}) async-start(), calls=%async_computation.6 | async-start | bytes 19660800 | tf_op jit(solution)/shard_map/reduce_scatter | solution.py:138
  530.3 7.4 copy-start.48
  530.3 7.4 copy-start.52
  530.3 7.4 copy-start.56
  572.9 14.5 %copy-start.35 = (bf16[1024,768]{1,0:T(8,128)(2,1)S(1)}, bf16[1024,768]{1,0:T(8,128)(2,1)}, u32[]{:S(2)}) copy-start(bf16[1024,768]{1,0:T(8,128)(2,1)} %param.27) | copy-start | bytes 4718596
  607.6 10.7 %copy-start.57 = (f32[768]{0:T(1024)S(1)}, f32[768]{0:T(1024)}, u32[]{:S(2)}) copy-start(f32[768]{0:T(1024)} %get-tuple-element.80) | copy-start | bytes 9220
  638.0 186.6 %all-reduce.10.cloned.1.call-start = ((), (), s32[]{:S(2)}) async-start(), calls=%async_computation.8 | async-start | bytes 7208960
  638.6 328.6 %reduce-scatter.8.cloned.1.call-start = ((), (), s32[]{:S(2)}) async-start(), calls=%async_computation.7 | async-start | bytes 6963200 | tf_op jit(solution)/shard_map/reduce_scatter | solution.py:139
  (18 other events, 37.2 us)
Sparse Core Ops, SparseCore 0:
  11.4 62.9 all-gather.2
  77.9 69.4 all-gather.4
  513.3 16.4 reduce-scatter.3
  638.1 22.5 reduce-scatter.5
  667.2 157.3 all-reduce.9
  826.8 140.3 reduce-scatter.7

commit v3 on v0

--- a/solution.py
+++ b/solution.py
@@ -87,33 +87,82 @@
     return jax.nn.gelu(gate_up[:, :FF], approximate=False) * gate_up[:, FF:]
 
 
-def tiled(value, copies):
-    return jnp.broadcast_to(value[None, :], (copies, value.shape[0]))
+def gain_rows(gain, width, rows=8):
+    line = jnp.pad(gain, (0, width - gain.shape[0]))
+    return jnp.concatenate([line[None], jnp.zeros((rows - 1, width), gain.dtype)], 0)
+
+
+def gather_rows(payload, n_dp, n_seq):
+    every = lax.all_gather(payload, ("dp", "seq"), axis=0, tiled=True)
+    return every.reshape(n_dp, n_seq, payload.shape[0], payload.shape[1])
+
+
+def reduce_rows(blocks):
+    n_dp, n_seq, rows, width = blocks.shape
+    half = lax.psum_scatter(
+        blocks.reshape(n_dp, n_seq * rows, width), "dp", scatter_dimension=0, tiled=True
+    )
+    return lax.psum_scatter(
+        half.reshape(n_seq * rows, width), "seq", scatter_dimension=0, tiled=True
+    )
+
+
+def gain_blocks(grad_gain, n_dp, n_seq, width):
+    part = jnp.pad(grad_gain.reshape(n_seq, -1), ((0, 0), (0, width - grad_gain.shape[0] // n_seq)))
+    rows = jnp.concatenate([part[:, None], jnp.zeros((n_seq, 7, width), part.dtype)], 1)
+    return jnp.broadcast_to(rows[None], (n_dp, n_seq, 8, width))
+
+
+def front(value, n_dp):
+    return value.reshape(value.shape[0], n_dp, -1)
+
+
+def apply_t(left, weight_t, n_dp):
+    return jnp.einsum("tdr,dnr->tn", front(left, n_dp), weight_t, preferred_element_type=jnp.float32)
+
+
+def apply_back(grad, weight_t):
+    out = jnp.einsum("tn,dnr->tdr", grad, weight_t, preferred_element_type=jnp.float32)
+    return out.reshape(out.shape[0], -1)
+
+
+def grad_t(grad, left, n_dp):
+    return jnp.einsum("tn,tdr->dnr", grad, front(left, n_dp), preferred_element_type=jnp.float32)
 
 
 def on_device(tokens, doc_start, real, w_qkv, w_out, w_in, w_down, gain_attn, gain_mlp, cotangent):
     count = tokens.shape[0]
-    col_parts = (
-        lax.all_gather(w_qkv, "seq", axis=1, tiled=True),
-        lax.all_gather(w_out, "seq", axis=1, tiled=True),
-        lax.all_gather(w_in, "seq", axis=1, tiled=True),
-        lax.all_gather(w_down, "seq", axis=1, tiled=True),
-        lax.all_gather(gain_attn, "seq", axis=0, tiled=True),
-        lax.all_gather(gain_mlp, "seq", axis=0, tiled=True),
-    )
-    full_qkv, full_out, full_in, full_down = (
-        lax.all_gather(col_parts[0], "dp", axis=0, tiled=True),
-        lax.all_gather(col_parts[1], "dp", axis=0, tiled=True),
-        lax.all_gather(col_parts[2], "dp", axis=0, tiled=True),
-        lax.all_gather(col_parts[3], "dp", axis=0, tiled=True),
-    )
-    gain_one, gain_two = (col_parts[4], col_parts[5])
-    gain_one = gain_one.astype(jnp.float32)
-    gain_two = gain_two.astype(jnp.float32)
+    n_dp, n_seq = lax.axis_size("dp"), lax.axis_size("seq")
+    rows, qkv_cols = w_qkv.shape
+    out_cols, in_cols = w_out.shape[1], w_in.shape[1]
+    down_rows, down_cols = w_down.shape
+    down_lines = down_rows * down_cols // rows
+    first = gather_rows(jnp.concatenate([w_qkv.T, gain_rows(gain_attn, rows)], 0), n_dp, n_seq)
+    second = gather_rows(
+        jnp.concatenate(
+            [w_out.T, w_in.T, w_down.T.reshape(down_lines, rows), gain_rows(gain_mlp, rows)], 0
+        ),
+        n_dp,
+        n_seq,
+    )
+    full_qkv = first[:, :, :qkv_cols].reshape(n_dp, n_seq * qkv_cols, rows)
+    gain_one = first[0, :, qkv_cols, : gain_attn.shape[0]].reshape(-1).astype(jnp.float32)
+    at = 0
+    full_out = second[:, :, at : at + out_cols].reshape(n_dp, n_seq * out_cols, rows)
+    at += out_cols
+    full_in = second[:, :, at : at + in_cols].reshape(n_dp, n_seq * in_cols, rows)
+    at += in_cols
+    full_down = (
+        second[:, :, at : at + down_lines]
+        .reshape(n_dp, n_seq, down_cols, down_rows)
+        .reshape(n_dp, n_seq * down_cols, down_rows)
+    )
+    at += down_lines
+    gain_two = second[0, :, at, : gain_mlp.shape[0]].reshape(-1).astype(jnp.float32)
     stream = tokens.astype(jnp.float32)
     normed_a, factor_a = layer_norm(stream)
     h_attn = (normed_a * gain_one).astype(jnp.bfloat16)
-    qkv = jnp.dot(h_attn, full_qkv, preferred_element_type=jnp.float32)
+    qkv = apply_t(h_attn, full_qkv, n_dp)
     offset_base = lax.axis_index(("dp", "seq")) * count
     place = (offset_base + jnp.arange(count, dtype=jnp.int32) - doc_start).astype(jnp.float32)
     cosine, sine = rotary_tables(place)
@@ -160,24 +209,24 @@
         )
         attended.append(mixed.reshape(block_rows, D))
     attn_out = jnp.concatenate(attended, 0).astype(jnp.bfloat16)
-    mid = stream + jnp.dot(attn_out, full_out, preferred_element_type=jnp.float32)
+    mid = stream + apply_t(attn_out, full_out, n_dp)
     normed_m, factor_m = layer_norm(mid)
     h_mlp = (normed_m * gain_two).astype(jnp.bfloat16)
-    gate_up = jnp.dot(h_mlp, full_in, preferred_element_type=jnp.float32)
+    gate_up = apply_t(h_mlp, full_in, n_dp)
     hidden_out, glu_pull = jax.vjp(glu_piece, gate_up)
     hidden = hidden_out.astype(jnp.bfloat16)
-    result = mid + jnp.dot(hidden, full_down, preferred_element_type=jnp.float32)
+    result = mid + apply_t(hidden, full_down, n_dp)
     output = result.astype(jnp.bfloat16)
-    grad_down = left_dot(hidden, cotangent)
-    grad_hidden = right_dot(cotangent, full_down)
+    grad_down = grad_t(cotangent, hidden, n_dp)
+    grad_hidden = apply_back(cotangent, full_down)
     grad_gate_up = glu_pull(grad_hidden)[0].astype(jnp.bfloat16)
-    grad_inw = left_dot(h_mlp, grad_gate_up)
-    grad_hmlp = right_dot(grad_gate_up, full_in)
+    grad_inw = grad_t(grad_gate_up, h_mlp, n_dp)
+    grad_hmlp = apply_back(grad_gate_up, full_in)
     grad_gain_two = jnp.sum(grad_hmlp * normed_m, axis=0)
     grad_mid = cotangent.astype(jnp.float32) + norm_back(grad_hmlp * gain_two, normed_m, factor_m)
     grad_branch = grad_mid.astype(jnp.bfloat16)
-    grad_outw = left_dot(attn_out, grad_branch)
-    grad_attn = right_dot(grad_branch, full_out).astype(jnp.bfloat16)
+    grad_outw = grad_t(grad_branch, attn_out, n_dp)
+    grad_attn = apply_back(grad_branch, full_out).astype(jnp.bfloat16)
     grad_wide = jnp.zeros((count + 2 * HALF, 2 * D), jnp.float32)
     grad_queries = []
     for number in range(blocks):
@@ -223,38 +272,49 @@
         ],
         1,
     ).astype(jnp.bfloat16)
-    grad_qkvw = left_dot(h_attn, grad_qkv)
-    grad_hattn = right_dot(grad_qkv, full_qkv)
+    grad_qkvw = grad_t(grad_qkv, h_attn, n_dp)
+    grad_hattn = apply_back(grad_qkv, full_qkv)
     grad_gain_one = jnp.sum(grad_hattn * normed_a, axis=0)
     grad_tokens = grad_mid + norm_back(grad_hattn * gain_one, normed_a, factor_a)
-    copies = lax.axis_size("dp")
-    row_sums = (
-        lax.psum_scatter(grad_qkvw, "dp", scatter_dimension=0, tiled=True),
-        lax.psum_scatter(grad_outw, "dp", scatter_dimension=0, tiled=True),
-        lax.psum_scatter(grad_inw, "dp", scatter_dimension=0, tiled=True),
-        lax.psum_scatter(grad_down, "dp", scatter_dimension=0, tiled=True),
-        lax.psum_scatter(tiled(grad_gain_one, copies), "dp", scatter_dimension=0, tiled=True),
-        lax.psum_scatter(tiled(grad_gain_two, copies), "dp", scatter_dimension=0, tiled=True),
-    )
-    final = (
-        lax.psum_scatter(row_sums[0], "seq", scatter_dimension=1, tiled=True),
-        lax.psum_scatter(row_sums[1], "seq", scatter_dimension=1, tiled=True),
-        lax.psum_scatter(row_sums[2], "seq", scatter_dimension=1, tiled=True),
-        lax.psum_scatter(row_sums[3], "seq", scatter_dimension=1, tiled=True),
-        lax.psum_scatter(row_sums[4][0], "seq", scatter_dimension=0, tiled=True),
-        lax.psum_scatter(row_sums[5][0], "seq", scatter_dimension=0, tiled=True),
-    )
-    gain_grad_one = final[4]
-    gain_grad_two = final[5]
+    late = reduce_rows(
+        jnp.concatenate(
+            [
+                grad_outw.reshape(n_dp, n_seq, out_cols, rows),
+                grad_inw.reshape(n_dp, n_seq, in_cols, rows),
+                grad_down.reshape(n_dp, n_seq, down_cols, down_rows).reshape(
+                    n_dp, n_seq, down_lines, rows
+                ),
+                gain_blocks(grad_gain_two, n_dp, n_seq, rows),
+            ],
+            2,
+        )
+    )
+    last = reduce_rows(
+        jnp.concatenate(
+            [
+                grad_qkvw.reshape(n_dp, n_seq, qkv_cols, rows),
+                gain_blocks(grad_gain_one, n_dp, n_seq, rows),
+            ],
+            2,
+        )
+    )
+    at = 0
+    late_out = late[at : at + out_cols].T
+    at += out_cols
+    late_in = late[at : at + in_cols].T
+    at += in_cols
+    late_down = late[at : at + down_lines].reshape(down_cols, down_rows).T
+    at += down_lines
+    late_gain_two = late[at, : gain_mlp.shape[0]]
     return (
         output,
         grad_tokens,
-        final[0],
-        final[1],
-        final[2],
-        final[3],
-        gain_grad_one,
-        gain_grad_two,
+        last[:qkv_cols].T,
+        late_out,
+        late_in,
+        late_down,
+        last[qkv_cols, : gain_attn.shape[0]],
+        late_gain_two,
     )
 
 

time: 1110 us -> 923 us (0.83)
  blocking collectives: 174 us -> 0 us
  waiting for transfers between devices: 546 us -> 430 us
  local copies, waits for them, and re-layouts: 110 us -> 197 us
  other arithmetic: 73.2 us -> 119 us
  matrix products: 162 us -> 137 us
    unnamed x18 -> x7, waiting for transfers between devices: 457 us -> 148 us
    reduce_scatter x4 -> x3, waiting for transfers between devices: 4.94 us -> 176 us  [the longest x1 151 us: reduce_rows(): lax.psum_scatter(half.reshape(n_seq * rows, width), 'seq', scatter_dimens...]
    all_gather x2 -> x0, blocking collectives: 90.2 us -> none  [the longest x1 45.2 us: on_device(): lax.all_gather(w_out, 'seq', axis=1, tiled=True)]
    unnamed x3 -> x0, blocking collectives: 83.3 us -> none
    transpose x0 -> x7, local copies, waits for them, and re-layouts: none -> 29.8 us  [the longest x4 25 us: grad_t(): jnp.einsum('tn,tdr->dnr', grad, front(left, n_dp), preferred_element_type...]
    all_gather x6 -> x2, waiting for transfers between devices: 80.5 us -> 104 us  [gather_rows(): every = lax.all_gather(payload, ('dp', 'seq'), axis=0, tiled=True)]
    reshape x0 -> x11, local copies, waits for them, and re-layouts: none -> 20.8 us  [the longest x1 6.1 us: apply_back(): return out.reshape(out.shape[0], -1)]
    unnamed x142 -> x161, local copies, waits for them, and re-layouts: 46.3 us -> 25.6 us
  transfers between devices with their start and end apart: 20 -> 12, of which waited for: 9 -> 6; matrix products, arithmetic and copies ran while one was open for 27% -> 17% of each run, Pallas kernels for 0% -> 0%
where the time goes in v3:
time: 923 us; the launch traced here: 916 us
  waiting for transfers between devices  430 us (47%)
  local copies, waits for them, and re-layouts  197 us (21%)
  matrix products  137 us (15%)
  other arithmetic  119 us (13%)
  starting transfers between devices  18.2 us (2%)
  between operations  15.9 us (2%)
    reduce_scatter x1, waiting for transfers between devices, reduce_rows(): lax.psum_scatter(half.reshape(n_seq * rows, width), 'seq', scatter_dimens...  151 us
    unnamed x7, waiting for transfers between devices  148 us
    all_gather x2, waiting for transfers between devices, gather_rows(): every = lax.all_gather(payload, ('dp', 'seq'), axis=0, tiled=True)  104 us
    dot_general x4, matrix products, grad_t(): jnp.einsum('tn,tdr->dnr', grad, front(left, n_dp), preferred_element_type...  27.8 us
    dot_general x4, matrix products, apply_back(): jnp.einsum('tn,dnr->tdr', grad, weight_t, preferred_element_type=jnp.floa...  26.1 us
    unnamed x161, local copies, waits for them, and re-layouts  25.6 us
    reduce_scatter x2, waiting for transfers between devices, reduce_rows(): lax.psum_scatter(blocks.reshape(n_dp, n_seq * rows, width), 'dp', scatter...  25.1 us
    transpose x4, local copies, waits for them, and re-layouts, grad_t(): jnp.einsum('tn,tdr->dnr', grad, front(left, n_dp), preferred_element_type...  25 us
  transfers between devices with their start and end apart: 12, of which 6 were waited for; matrix products, arithmetic and copies ran while one was open for 17% of the time, Pallas kernels for 0%

profile of v3, /device:TPU:0, one launch (start us, length us, event | category | flops | bytes accessed | tf_op | source)
XLA Modules:
  0.0 916.5 jit_solution(12975275654983406810)
XLA Ops:
  11.2 4.2 concatenate.101
  16.2 4.8 collective-permute-start.1
  27.5 3.7 copy.113
  34.4 40.5 %all-gather.3.cloned.1.call-done = bf16[4864,384]{1,0:T(8,128)(2,1)} async-done(((bf16[152,384]{1,0:T(8,128)(2,1)}), bf16[4864,384]{1,0:T(8,128)(2,1)}) %all-gather.3.cloned.1.call-update) | async-done | bytes 3735568 | tf_op jit(solution)/shard_map/all_gather | solution.py:96
  74.8 4.1 slice.285
  79.0 5.8 copy.148
  84.8 63.5 %all-gather.5.cloned.1.call-done = bf16[8704,384]{1,0:T(8,128)(2,1)} async-done(((bf16[272,384]{1,0:T(8,128)(2,1)}), bf16[8704,384]{1,0:T(8,128)(2,1)}) %all-gather.5.cloned.1.call-update) | async-done | bytes 6684688 | tf_op jit(solution)/shard_map/all_gather | solution.py:96
  149.8 6.7 convolution_bitcast_fusion.1
  156.5 3.3 fusion.65
  168.1 3.6 copy.118
  171.7 3.4 slice_negate_fusion.1
  175.2 3.5 copy.114
  181.1 3.4 maximum_multiply_fusion.1
  184.5 13.2 %copy.115 = f32[1024,768]{1,0:T(8,128)} copy(f32[1024,768]{0,1:T(8,128)} %bitcast.182) | data formatting | bytes 6291456 | tf_op jit(solution)/shard_map/mul | solution.py:170
  197.7 3.5 copy.119
  201.2 7.8 add_convert_fusion.1
  209.1 4.0 collective-permute-start
  214.4 4.8 reshape_reshape.6
  219.2 6.7 fusion.44
  231.8 6.1 copy.133
  237.9 5.8 copy.135
  246.1 3.8 pad_maximum_fusion.12
  254.2 4.2 fusion.71
  258.4 3.4 fusion
  264.2 5.1 fusion.48
  275.1 4.2 fusion.70
  279.3 3.4 fusion.1
  284.8 5.8 fusion.47
  299.2 3.9 convolution_bitcast_fusion
  303.1 11.3 %fusion.46 = (f32[1024,1152]{1,0:T(8,128)}, f32[1024,1152]{1,0:T(8,128)S(1)}) fusion(f32[1024,1152]{1,0:T(8,128)S(1)} %bitcast.161, f32[1024,2304]{1,0:T(8,128)S(1)} %convolution_bitcast_fusion), kind=kLoop, calls=%fused_computation.112 | loop fusion | flops 76677120 | bytes 18874368 | tf_op jit(solution)/shard_map/transpose(jvp())/mul | solution.py:87
  314.5 3.6 multiply_add_fusion
  318.1 8.6 multiply_reduce_fusion.2
  330.6 15.1 %multiply_reduce_fusion = (f32[12,512]{1,0:T(8,128)S(1)}, f32[12,512,640]{2,1,0:T(8,128)}) fusion(f32[12,512,640]{2,1,0:T(8,128)} %copy-done.1, f32[12,512]{1,0:T(8,128)S(1)} %copy-done.51, bf16[512,12,64]{0,2,1:T(8,128)(2,1)S(1)} %bitcast.198, bf16[640,12,64]{0,2,1:T(8,128)(2,1)S(1)} %bitcast.213), kind=kOutput, calls=%fused_computation.1 | convolution fusion | flops 515106816 | bytes 33275904 | tf_op jit(solution)/shard_map/qhd,khd->hqk/dot_general | solution.py:238
  345.7 8.3 fusion.4
  354.1 8.8 multiply_reduce_fusion.1
  362.9 4.1 fusion.6
  367.0 11.4 %multiply_convert_fusion = bf16[12,512,640]{2,1,0:T(8,128)(2,1)S(1)} fusion(f32[12,512,640]{2,1,0:T(8,128)} %get-tuple-element.141, f32[12,512,640]{2,1,0:T(8,128)} %copy-done.1, f32[12,512]{1,0:T(8,128)S(1)} %get-tuple-element.140, f32[12,512]{1,0:T(8,128)S(1)} %copy-done.51), kind=kLoop, calls=%fused_computation | loop fusion | flops 15728640 | bytes 39370752 | tf_op jit(solution)/shard_map/convert_element_type | solution.py:240
  387.2 11.2 %multiply_convert_fusion.1 = bf16[12,512,640]{2,1,0:T(8,128)(2,1)S(1)} fusion(f32[12,512,640]{2,1,0:T(8,128)} %get-tuple-element.139, f32[12,512,640]{2,1,0:T(8,128)} %copy-done, f32[12,512]{1,0:T(8,128)S(1)} %copy-done.58, f32[12,512]{1,0:T(8,128)S(1)} %copy-done.53), kind=kLoop, calls=%fused_computation.3 | loop fusion | flops 15728640 | bytes 39370752 | tf_op jit(solution)/shard_map/convert_element_type | solution.py:240
  410.9 5.2 collective-permute-start.4
  433.2 3.8 slice.311
  440.2 4.0 copy.146
  446.6 3.4 fusion.35
  450.0 3.6 copy.140
  453.6 3.8 copy.147
  457.4 6.1 fusion.37
  465.3 6.1 convolution_bitcast_fusion.3
  471.4 8.2 copy.149
  479.6 9.4 %fusion.32 = (f32[768]{0:T(1024)S(1)}, f32[1024]{0:T(1024)}, f32[1024]{0:T(1024)S(1)}, f32[1024,768]{0,1:T(8,128)}) fusion(bf16[1024,768]{0,1:T(8,128)(2,1)S(1)} %copy-done.5, f32[1024]{0:T(1024)S(1)} %copy-done.64, f32[1024]{0:T(1024)S(1)} %copy-done.60, f32[768]{0:T(1024)S(1)} %copy-done.62, bf16[768,2304]{1,0:T(8,128)(2,1)} %bitcast.215, ...), kind=kOutput, calls=%fused_computation.68 | convolution fusion | flops 3645109504 | bytes 12998656 | tf_op jit(solution)/shard_map/tn,dnr->tdr/dot_general | solution.py:125
  489.2 6.5 pad_maximum_fusion.1
  497.0 4.8 convolution_bitcast_fusion.5
  501.8 3.4 copy.153
  505.3 11.5 %convolution_bitcast_fusion.2 = f32[2,2304,384]{1,2,0:T(8,128)} fusion(bf16[1024,2,384]{0,2,1:T(8,128)(2,1)S(1)} %bitcast.224, f32[1024,1152]{1,0:T(8,128)} %copy-done.27, f32[1024,1152]{1,0:T(8,128)} %get-tuple-element.88), kind=kOutput, calls=%fused_computation.30 | convolution fusion | flops 3628597248 | bytes 18087936 | tf_op jit(solution)/shard_map/tn,tdr->dnr/dot_general | solution.py:130
  516.7 8.1 copy.154
  525.0 4.4 copy.128
  529.3 5.5 convolution_bitcast_fusion.4
  534.8 5.3 copy.155
  540.1 5.5 reshape_reshape.7
  545.6 10.8 %pad_maximum_fusion = f32[2,16,272,384]{3,2,1,0:T(8,128)} fusion(f32[2,16,8,384]{3,2,1,0:T(8,128)S(1)} %broadcast_in_dim.51, f32[2,16,72,384]{3,2,1,0:T(8,128)} %reshape_reshape.7, f32[2,16,144,384]{3,2,1,0:T(8,128)} %bitcast.164, f32[2,16,48,384]{3,2,1,0:T(8,128)} %bitcast.189), kind=kLoop, calls=%fused_computation.14 | loop fusion | flops 10027008 | bytes 26738688 | tf_op jit(solution)/shard_map/concatenate | solution.py:280
  557.1 25.1 %reduce-scatter.6.cloned.1.call-done = f32[1,4352,384]{2,1,0:T(8,128)} async-done(((f32[2,4352,384]{2,1,0:T(8,128)}), f32[1,4352,384]{2,1,0:T(8,128)}) %reduce-scatter.6.cloned.1.call-update) | async-done | bytes 6684688 | tf_op jit(solution)/shard_map/reduce_scatter | solution.py:102
  584.3 5.9 fusion.38
  592.8 5.6 fusion.31
  598.4 3.5 copy.158
  602.0 147.3 %all-reduce.12.cloned.1.call-done = f32[2432,384]{1,0:T(8,128)} async-done(((f32[2432,384]{1,0:T(8,128)}), f32[2432,384]{1,0:T(8,128)}) %all-reduce.12.cloned.1.call-update) | async-done | bytes 3735568
  752.1 151.4 %reduce-scatter.8.cloned.1.call-done = f32[272,384]{1,0:T(8,128)} async-done(((f32[4352,384]{1,0:T(8,128)}), f32[272,384]{1,0:T(8,128)}) %reduce-scatter.8.cloned.1.call-update) | async-done | bytes 417808 | tf_op jit(solution)/shard_map/reduce_scatter | solution.py:105
  (275 shorter events, 123.5 us)
Async XLA Ops:
  7.2 67.7 %all-gather.3.cloned.1.call-start = ((), (), s32[]{:S(2)}) async-start(), calls=%async_computation.3 | async-start | bytes 3852288 | tf_op jit(solution)/shard_map/all_gather | solution.py:96
  9.5 138.9 %all-gather.5.cloned.1.call-start = ((), (), s32[]{:S(2)}) async-start(), calls=%async_computation.4 | async-start | bytes 6893568 | tf_op jit(solution)/shard_map/all_gather | solution.py:96
  15.4 541.2 %reduce-scatter.4.cloned.1.call-start = ((), (), s32[]{:S(2)}) async-start(), calls=%async_computation.5 | async-start | bytes 11206656 | tf_op jit(solution)/shard_map/reduce_scatter | solution.py:102
  16.2 16.7 %collective-permute-start.1 = (s32[64]{0:T(128)S(1)}, s32[64]{0:T(128)S(1)}, u32[]{:S(2)}, u32[]{:S(2)}) collective-permute-start(s32[64]{0:T(128)S(1)} %get-tuple-element.126), channel_id=1, source_target_pairs={{0,1},{1,2},{2,3},{3,4},{4,5},{5,6},{6,7},{7,8},{8,9},{9,10},{10,1... | collective-permute-start | bytes 776 | tf_op jit(solution)/shard_map/ppermute | solution.py:22
  21.0 11.8 %collective-permute-start.3 = (s32[64]{0:T(128)S(1)}, s32[64]{0:T(128)S(1)}, u32[]{:S(2)}, u32[]{:S(2)}) collective-permute-start(s32[64]{0:T(128)S(1)} %get-tuple-element.127), channel_id=1, source_target_pairs={{1,0},{2,1},{3,2},{4,3},{5,4},{6,5},{7,6},{8,7},{9,8},{10,9},{11,1... | collective-permute-start | bytes 776 | tf_op jit(solution)/shard_map/ppermute | solution.py:23
  24.1 268.8 %copy-start.4 = (bf16[1024,768]{0,1:T(8,128)(2,1)}, bf16[1024,768]{0,1:T(8,128)(2,1)S(1)}, u32[]{:S(2)}) copy-start(bf16[1024,768]{0,1:T(8,128)(2,1)S(1)} %copy.111) | copy-start | bytes 4718596
  24.7 156.4 %copy-start.34 = (f32[1024,64]{0,1:T(8,128)}, f32[1024,64]{0,1:T(8,128)S(1)}, u32[]{:S(2)}) copy-start(f32[1024,64]{0,1:T(8,128)S(1)} %get-tuple-element.146) | copy-start | bytes 786436
  25.0 124.3 %copy-start.59 = (f32[1024]{0:T(1024)}, f32[1024]{0:T(1024)S(1)}, u32[]{:S(2)}) copy-start(f32[1024]{0:T(1024)S(1)} %broadcast_multiply_fusion.5) | copy-start | bytes 12292
  25.4 123.8 %copy-start.63 = (f32[1024]{0:T(1024)}, f32[1024]{0:T(1024)S(1)}, u32[]{:S(2)}) copy-start(f32[1024]{0:T(1024)S(1)} %add_rsqrt_fusion.1) | copy-start | bytes 12292
  27.5 3.7 copy-start.40
  149.2 7.3 copy-start.61
  149.2 14.2 %slice-start.8 = ((s8[6684672]{0:T(1024)(128)(4,1)}), s8[4194304]{0:T(1024)(128)(4,1)S(1)}, s32[]{:S(2)}) async-start(s8[6684672]{0:T(1024)(128)(4,1)} %bitcast.202), calls=%async_computation.17 | async-start | bytes 8388608
  149.8 6.8 copy-start.42
  149.8 13.6 %slice-start.9 = ((s8[6684672]{0:T(1024)(128)(4,1)}), s8[2490368]{0:T(1024)(128)(4,1)S(1)}, s32[]{:S(2)}) async-start(s8[6684672]{0:T(1024)(128)(4,1)} %bitcast.202), calls=%async_computation.18 | async-start | bytes 4980736
  156.5 5.6 copy-start.8
  201.2 7.8 copy-start.9
  209.1 37.0 %collective-permute-start = (bf16[64,1536]{1,0:T(8,128)(2,1)S(1)}, bf16[64,1536]{1,0:T(8,128)(2,1)}, u32[]{:S(2)}, u32[]{:S(2)}) collective-permute-start(bf16[64,1536]{1,0:T(8,128)(2,1)S(1)} %get-tuple-element.106), channel_id=1, source_target_pairs={{0,1},{1,2},{2,3},{3,4},{4,5},{5,6},{6,7},{7,8},{8,9},{9,10},{10,1... | collective-permute-start | bytes 589832 | tf_op jit(solution)/shard_map/ppermute | solution.py:22
  213.1 33.0 %collective-permute-start.2 = (bf16[64,1536]{1,0:T(8,128)(2,1)S(1)}, bf16[64,1536]{1,0:T(8,128)(2,1)}, u32[]{:S(2)}, u32[]{:S(2)}) collective-permute-start(bf16[64,1536]{1,0:T(8,128)(2,1)S(1)} %get-tuple-element.107), channel_id=1, source_target_pairs={{1,0},{2,1},{3,2},{4,3},{5,4},{6,5},{7,6},{8,7},{9,8},{10,9},{11,1... | collective-permute-start | bytes 589832 | tf_op jit(solution)/shard_map/ppermute | solution.py:23
  219.2 6.7 copy-start.25
  249.9 4.3 copy-start.12
  251.6 6.8 copy-start.16
  258.4 5.6 copy-start
  258.4 5.8 copy-start.54
  258.4 5.8 copy-start.29
  269.3 5.7 copy-start.14
  272.0 7.2 copy-start.18
  279.3 5.6 copy-start.1
  279.3 5.6 copy-start.31
  284.8 8.1 copy-start.28
  284.8 8.1 copy-start.48
  295.5 31.2 %copy-start.7 = (f32[1024,768]{0,1:T(8,128)}, f32[1024,768]{0,1:T(8,128)S(1)}, u32[]{:S(2)}) copy-start(f32[1024,768]{0,1:T(8,128)S(1)} %get-tuple-element.136) | copy-start | bytes 9437188
  295.9 7.2 slice-start.6
  299.2 3.9 slice-start.7
  318.0 8.6 copy-start.27
  318.1 8.7 copy-start.23
  330.6 23.4 %slice-start = ((s8[15728640]{0:T(1024)(128)(4,1)}), s8[4194304]{0:T(1024)(128)(4,1)S(1)}, s32[]{:S(2)}) async-start(s8[15728640]{0:T(1024)(128)(4,1)} %bitcast.155), calls=%async_computation.9 | async-start | bytes 8388608
  330.6 23.4 %slice-start.1 = ((s8[15728640]{0:T(1024)(128)(4,1)}), s8[4194304]{0:T(1024)(128)(4,1)S(1)}, s32[]{:S(2)}) async-start(s8[15728640]{0:T(1024)(128)(4,1)} %bitcast.155), calls=%async_computation.10 | async-start | bytes 8388608
  330.6 23.4 %slice-start.2 = ((s8[15728640]{0:T(1024)(128)(4,1)}), s8[4194304]{0:T(1024)(128)(4,1)S(1)}, s32[]{:S(2)}) async-start(s8[15728640]{0:T(1024)(128)(4,1)} %bitcast.155), calls=%async_computation.11 | async-start | bytes 8388608
  345.7 8.3 copy-start.55
  345.7 8.3 copy-start.57
  345.7 8.4 slice-start.3
  345.7 8.4 copy-start.30
  354.0 8.9 copy-start.52
  367.0 11.4 %copy-start.15 = (bf16[512,768]{0,1:T(8,128)(2,1)S(1)}, bf16[512,768]{0,1:T(8,128)(2,1)}, u32[]{:S(2)}) copy-start(bf16[512,768]{0,1:T(8,128)(2,1)} %copy.123) | copy-start | bytes 2359300
  387.2 11.2 %copy-start.13 = (bf16[512,768]{0,1:T(8,128)(2,1)S(1)}, bf16[512,768]{0,1:T(8,128)(2,1)}, u32[]{:S(2)}) copy-start(bf16[512,768]{0,1:T(8,128)(2,1)} %copy.120) | copy-start | bytes 2359300
  406.5 9.6 %slice-start.4 = ((s8[7864320]{0:T(1024)(128)(4,1)}), s8[4194304]{0:T(1024)(128)(4,1)S(1)}, s32[]{:S(2)}) async-start(s8[7864320]{0:T(1024)(128)(4,1)} %bitcast.157), calls=%async_computation.13 | async-start | bytes 8388608
  409.2 6.9 slice-start.5
  409.2 6.9 copy-start.17
  410.8 10.9 %copy-start.3 = (f32[1152,1536]{1,0:T(8,128)}, f32[1152,1536]{1,0:T(8,128)S(1)}, u32[]{:S(2)}) copy-start(f32[1152,1536]{1,0:T(8,128)S(1)} %get-tuple-element.86) | copy-start | bytes 21233668
  410.9 16.8 %collective-permute-start.4 = (bf16[64,1536]{1,0:T(8,128)(2,1)S(1)}, bf16[64,1536]{1,0:T(8,128)(2,1)}, u32[]{:S(2)}, u32[]{:S(2)}) collective-permute-start(bf16[64,1536]{1,0:T(8,128)(2,1)S(1)} %slice.372), channel_id=1, source_target_pairs={{0,1},{1,2},{2,3},{3,4},{4,5},{5,6},{6,7},{7,8},{8,9},{9,10},{10,1... | collective-permute-start | bytes 589832 | tf_op jit(solution)/shard_map/ppermute | solution.py:31
  421.7 9.7 %collective-permute-start.5 = (bf16[64,1536]{1,0:T(8,128)(2,1)S(1)}, bf16[64,1536]{1,0:T(8,128)(2,1)}, u32[]{:S(2)}, u32[]{:S(2)}) collective-permute-start(bf16[64,1536]{1,0:T(8,128)(2,1)S(1)} %slice.371), channel_id=1, source_target_pairs={{1,0},{2,1},{3,2},{4,3},{5,4},{6,5},{7,6},{8,7},{9,8},{10,9},{11,1... | collective-permute-start | bytes 589832 | tf_op jit(solution)/shard_map/ppermute | solution.py:31
  453.6 3.8 copy-start.6
  457.4 7.8 copy-start.43
  457.4 7.8 copy-start.44
  471.4 8.2 copy-start.5
  471.4 8.2 copy-start.38
  471.4 8.2 copy-start.60
  471.4 8.2 copy-start.62
  471.4 8.2 copy-start.64
  495.7 86.5 %reduce-scatter.6.cloned.1.call-start = ((), (), s32[]{:S(2)}) async-start(), calls=%async_computation.6 | async-start | bytes 20054016 | tf_op jit(solution)/shard_map/reduce_scatter | solution.py:102
  516.7 8.1 copy-start.65
  524.8 4.5 copy-start.41
  556.4 192.8 %all-reduce.12.cloned.1.call-start = ((), (), s32[]{:S(2)}) async-start(), calls=%async_computation.8 | async-start | bytes 7471104
  557.0 346.4 %reduce-scatter.8.cloned.1.call-start = ((), (), s32[]{:S(2)}) async-start(), calls=%async_computation.7 | async-start | bytes 7102464 | tf_op jit(solution)/shard_map/reduce_scatter | solution.py:105
  (25 other events, 55.1 us)
Sparse Core Ops, SparseCore 0:
  11.4 63.3 all-gather.2
  78.3 69.9 all-gather.4
  495.8 18.8 reduce-scatter.3
  556.6 25.5 reduce-scatter.5
  588.8 160.3 all-reduce.11
  755.3 148.1 reduce-scatter.7

commit v4 on v3

--- a/solution.py
+++ b/solution.py
@@ -1,8 +1,11 @@
+import functools
 import math
 
 import jax
 import jax.numpy as jnp
 from jax import lax
+from jax.experimental import pallas as pl
+from jax.experimental.pallas import tpu as pltpu
 from jax.sharding import PartitionSpec as P
 
 D = 768
@@ -87,6 +90,134 @@
     return jax.nn.gelu(gate_up[:, :FF], approximate=False) * gate_up[:, FF:]
 
 
+MESH = pl.DeviceIdType.MESH
+
+
+def ring_order(mesh):
+    n = mesh.shape["seq"]
+    try:
+        coords = [tuple(mesh.devices[0, s].coords) for s in range(n)]
+    except Exception:
+        return list(range(n))
+    near = [
+        [t for t in range(n) if sum(abs(a - b) for a, b in zip(coords[s], coords[t])) == 1]
+        for s in range(n)
+    ]
+    path, seen = [0], {0}
+
+    def grow(budget=[200000]):
+        budget[0] -= 1
+        if budget[0] < 0:
+            return False
+        if len(path) == n:
+            return 0 in near[path[-1]]
+        options = sorted(
+            (t for t in near[path[-1]] if t not in seen),
+            key=lambda t: sum(1 for u in near[t] if u not in seen),
+        )
+        for t in options:
+            path.append(t)
+            seen.add(t)
+            if grow():
+                return True
+            path.pop()
+            seen.discard(t)
+        return False
+
+    return list(path) if n > 2 and grow() else list(range(n))
+
+
+def lookup(index, table):
+    n = len(table)
+    square = n * n
+    total = jnp.int32(0)
+    for k, value in enumerate(table):
+        if value:
+            gap = index - k
+            differs = lax.div(gap * gap + (square - 1), jnp.int32(square))
+            total = total + value * (1 - differs)
+    return total
+
+
+def ring_kernel(order, per_way, h_ref, out_ref, recv, send, ssem, rsem, free):
+    n = len(order)
+    where = [0] * n
+    for p, s in enumerate(order):
+        where[s] = p
+    d = lax.axis_index("dp")
+    me = lax.axis_index("seq")
+    pos = lookup(me, where)
+    nxt = lookup(lax.rem(pos + 1, n), order)
+    prv = lookup(lax.rem(pos + n - 1, n), order)
+    piece = out_ref.shape[0] // (2 * per_way)
+
+    barrier = pltpu.get_barrier_semaphore()
+    pl.semaphore_signal(barrier, 1, device_id=(d, nxt), device_id_type=MESH)
+    pl.semaphore_signal(barrier, 1, device_id=(d, prv), device_id_type=MESH)
+    pl.semaphore_wait(barrier, 2)
+
+    lanes = []
+    for li in range(2 * per_way):
+        forward = li % 2 == 0
+        lanes.append((recv.at[li], send.at[li], ssem.at[li], rsem.at[li], free.at[li],
+                      nxt if forward else prv, prv if forward else nxt,
+                      slice(li * piece, (li + 1) * piece), -1 if forward else 1))
+    copies = {}
+    for step in range(n - 1):
+        slot = step % 2
+        for li, (recv, send, ssem, rsem, free, to, frm, rows, sign) in enumerate(lanes):
+            q = lax.rem(pos + sign * (1 + step) + n * (step + 2), n)
+            own = h_ref[q, rows, :]
+            if step == 0:
+                part = own
+            else:
+                copies[(li, step - 1)].wait_recv()
+                part = recv[1 - slot].astype(jnp.float32) + own
+                if step <= n - 3:
+                    pl.semaphore_signal(free, 1, device_id=(d, frm), device_id_type=MESH)
+            if step >= 2:
+                copies[(li, step - 2)].wait_send()
+                pl.semaphore_wait(free, 1)
+            send[slot] = part.astype(send.dtype)
+            c = pltpu.make_async_remote_copy(
+                src_ref=send.at[slot], dst_ref=recv.at[slot],
+                send_sem=ssem.at[slot], recv_sem=rsem.at[slot],
+                device_id=(d, to), device_id_type=MESH)
+            c.start()
+            copies[(li, step)] = c
+    last = n - 2
+    for li, (recv, send, ssem, rsem, free, to, frm, rows, sign) in enumerate(lanes):
+        copies[(li, last)].wait_recv()
+        out_ref[rows, :] = recv[last % 2].astype(jnp.float32) + h_ref[pos, rows, :]
+        if last >= 1:
+            copies[(li, last - 1)].wait_send()
+        copies[(li, last)].wait_send()
+
+
+RING_WAYS = 2
+
+
+def ring_reduce(h, order, per_way, link_dtype=jnp.bfloat16):
+    n, rows, width = h.shape
+    lanes = 2 * per_way
+    piece = rows // lanes
+    return pl.pallas_call(
+        functools.partial(ring_kernel, tuple(order), per_way),
+        out_shape=jax.ShapeDtypeStruct((rows, width), jnp.float32),
+        in_specs=[pl.BlockSpec(memory_space=pltpu.VMEM)],
+        out_specs=pl.BlockSpec(memory_space=pltpu.VMEM),
+        scratch_shapes=[
+            pltpu.VMEM((lanes, 2, piece, width), link_dtype),
+            pltpu.VMEM((lanes, 2, piece, width), link_dtype),
+            pltpu.SemaphoreType.DMA((lanes, 2)),
+            pltpu.SemaphoreType.DMA((lanes, 2)),
+            pltpu.SemaphoreType.REGULAR((lanes,)),
+        ],
+        compiler_params=pltpu.CompilerParams(collective_id=1, has_side_effects=True,
+                                             vmem_limit_bytes=48 * 1024 * 1024),
+    )(h)
+
+
 def gain_rows(gain, width, rows=8):
     line = jnp.pad(gain, (0, width - gain.shape[0]))
     return jnp.concatenate([line[None], jnp.zeros((rows - 1, width), gain.dtype)], 0)
@@ -95,16 +226,6 @@
 def gather_rows(payload, n_dp, n_seq):
     every = lax.all_gather(payload, ("dp", "seq"), axis=0, tiled=True)
     return every.reshape(n_dp, n_seq, payload.shape[0], payload.shape[1])
-
-
-def reduce_rows(blocks):
-    n_dp, n_seq, rows, width = blocks.shape
-    half = lax.psum_scatter(
-        blocks.reshape(n_dp, n_seq * rows, width), "dp", scatter_dimension=0, tiled=True
-    )
-    return lax.psum_scatter(
-        half.reshape(n_seq * rows, width), "seq", scatter_dimension=0, tiled=True
-    )
 
 
 def gain_blocks(grad_gain, n_dp, n_seq, width):
@@ -130,7 +251,7 @@
     return jnp.einsum("tn,tdr->dnr", grad, front(left, n_dp), preferred_element_type=jnp.float32)
 
 
-def on_device(tokens, doc_start, real, w_qkv, w_out, w_in, w_down, gain_attn, gain_mlp, cotangent):
+def on_device(order, tokens, doc_start, real, w_qkv, w_out, w_in, w_down, gain_attn, gain_mlp, cotangent):
     count = tokens.shape[0]
     n_dp, n_seq = lax.axis_size("dp"), lax.axis_size("seq")
     rows, qkv_cols = w_qkv.shape
@@ -276,28 +397,31 @@
     grad_hattn = apply_back(grad_qkv, full_qkv)
     grad_gain_one = jnp.sum(grad_hattn * normed_a, axis=0)
     grad_tokens = grad_mid + norm_back(grad_hattn * gain_one, normed_a, factor_a)
-    late = reduce_rows(
-        jnp.concatenate(
-            [
-                grad_outw.reshape(n_dp, n_seq, out_cols, rows),
-                grad_inw.reshape(n_dp, n_seq, in_cols, rows),
-                grad_down.reshape(n_dp, n_seq, down_cols, down_rows).reshape(
-                    n_dp, n_seq, down_lines, rows
-                ),
-                gain_blocks(grad_gain_two, n_dp, n_seq, rows),
-            ],
-            2,
-        )
-    )
-    last = reduce_rows(
-        jnp.concatenate(
-            [
-                grad_qkvw.reshape(n_dp, n_seq, qkv_cols, rows),
-                gain_blocks(grad_gain_one, n_dp, n_seq, rows),
-            ],
-            2,
-        )
-    )
+    blocks = jnp.concatenate(
+        [
+            grad_outw.reshape(n_dp, n_seq, out_cols, rows),
+            grad_inw.reshape(n_dp, n_seq, in_cols, rows),
+            grad_down.reshape(n_dp, n_seq, down_cols, down_rows).reshape(
+                n_dp, n_seq, down_lines, rows
+            ),
+            gain_blocks(grad_gain_two, n_dp, n_seq, rows),
+            grad_qkvw.reshape(n_dp, n_seq, qkv_cols, rows),
+            gain_blocks(grad_gain_one, n_dp, n_seq, rows),
+        ],
+        2,
+    )
+    height = blocks.shape[2]
+    lanes_rows = 2 * RING_WAYS * 16
+    extra = (-height) % lanes_rows
+    if extra:
+        blocks = jnp.pad(blocks, ((0, 0), (0, 0), (0, extra), (0, 0)))
+    blocks = jnp.stack([blocks[:, s] for s in order], 1)
+    depth = blocks.shape[2]
+    half = lax.psum_scatter(
+        blocks.reshape(n_dp, n_seq * depth, rows), "dp", scatter_dimension=0, tiled=True
+    )
+    late = ring_reduce(half.reshape(n_seq, depth, rows), order, RING_WAYS)
+    last = late[out_cols + in_cols + down_lines + 8 :]
     at = 0
     late_out = late[at : at + out_cols].T
     at += out_cols
@@ -332,7 +456,7 @@
         P(("dp", "seq"), None),
     )
     return jax.shard_map(
-        on_device,
+        functools.partial(on_device, ring_order(mesh)),
         mesh=mesh,
         in_specs=placed,
         out_specs=(

time: 923 us -> 693 us (0.75)
  waiting for transfers between devices: 430 us -> 116 us
  Pallas kernels: 0 us -> 71 us
  local copies, waits for them, and re-layouts: 197 us -> 229 us
  other arithmetic: 119 us -> 104 us
    reduce_scatter x3 -> x1, waiting for transfers between devices: 176 us -> 11.9 us  [on_device(): lax.psum_scatter(blocks.reshape(n_dp, n_seq * depth, rows), 'dp', scatter...]
    unnamed x7 -> x3, waiting for transfers between devices: 148 us -> 0.05 us
    pallas_call x0 -> x1, Pallas kernels: none -> 71 us  [ring_reduce(): pl.pallas_call(functools.partial(ring_kernel, tuple(order), per_way), out...]
    unnamed x161 -> x185, local copies, waits for them, and re-layouts: 25.6 us -> 73.2 us
    concatenate x2 -> x0, other arithmetic: 17.2 us -> none  [the longest x1 10.8 us: on_device(): jnp.concatenate([grad_outw.reshape(n_dp, n_seq, out_cols, rows), grad_inw...]
    mul x1, local copies, waits for them, and re-layouts: 13.2 us -> 3.54 us  [on_device(): rotate(qkv[:, D:2 * D]) * sine]
  transfers between devices with their start and end apart: 12 -> 9, of which waited for: 6 -> 3; matrix products, arithmetic and copies ran while one was open for 17% -> 19% of each run, Pallas kernels for 0% -> 0%
where the time goes in v4:
time: 693 us; the launch traced here: 681 us
  local copies, waits for them, and re-layouts  229 us (33%)
  matrix products  128 us (18%)
  waiting for transfers between devices  116 us (17%)
  other arithmetic  104 us (15%)
  Pallas kernels  71 us (10%)
  starting transfers between devices  18.1 us (3%)
  between operations  15.4 us (2%)
    all_gather x2, waiting for transfers between devices, gather_rows(): every = lax.all_gather(payload, ('dp', 'seq'), axis=0, tiled=True)  104 us
    unnamed x185, local copies, waits for them, and re-layouts  73.2 us
    pallas_call x1, Pallas kernels, ring_reduce(): pl.pallas_call(functools.partial(ring_kernel, tuple(order), per_way), out...  71 us
    transpose x4, local copies, waits for them, and re-layouts, grad_t(): jnp.einsum('tn,tdr->dnr', grad, front(left, n_dp), preferred_element_type...  24.6 us
    dot_general x4, matrix products, apply_back(): jnp.einsum('tn,dnr->tdr', grad, weight_t, preferred_element_type=jnp.floa...  23.8 us
    dot_general x2, matrix products, on_device(): jnp.einsum('qhd,khd->hqk', grad_blk, v_blk, preferred_element_type=jnp.fl...  23.5 us
    convert_element_type x2, other arithmetic, on_device(): grad_scores = (probs * (grad_probs - inner)).astype(jnp.bfloat16)  22.4 us
    dot_general x4, matrix products, grad_t(): jnp.einsum('tn,tdr->dnr', grad, front(left, n_dp), preferred_element_type...  22.1 us
  transfers between devices with their start and end apart: 9, of which 3 were waited for; matrix products, arithmetic and copies ran while one was open for 19% of the time, Pallas kernels for 0%

profile of v4, /device:TPU:0, one launch (start us, length us, event | category | flops | bytes accessed | tf_op | source)
XLA Modules:
  0.0 681.4 jit_solution(11145395742920111489)
XLA Ops:
  11.2 4.2 concatenate.98
  16.2 4.8 collective-permute-start.1
  27.5 3.8 copy.64
  34.5 40.4 %all-gather.3.cloned.1.call-done = bf16[4864,384]{1,0:T(8,128)(2,1)} async-done(((bf16[152,384]{1,0:T(8,128)(2,1)}), bf16[4864,384]{1,0:T(8,128)(2,1)}) %all-gather.3.cloned.1.call-update) | async-done | bytes 3735568 | tf_op jit(solution)/shard_map/all_gather | solution.py:227
  74.8 4.2 slice.346
  79.0 5.8 copy.99
  84.8 63.5 %all-gather.5.cloned.1.call-done = bf16[8704,384]{1,0:T(8,128)(2,1)} async-done(((bf16[272,384]{1,0:T(8,128)(2,1)}), bf16[8704,384]{1,0:T(8,128)(2,1)}) %all-gather.5.cloned.1.call-update) | async-done | bytes 6684688 | tf_op jit(solution)/shard_map/all_gather | solution.py:227
  152.2 6.5 convolution_bitcast_fusion.1
  160.0 3.4 fusion.77
  170.1 3.7 copy.69
  173.7 3.4 slice_negate_fusion.1
  177.1 3.5 copy.65
  183.1 3.4 maximum_multiply_fusion.1
  186.5 4.0 copy.70
  190.5 3.5 copy.66
  194.0 7.8 %add_convert_fusion.1 = (bf16[1024,768]{1,0:T(8,128)(2,1)}, bf16[1024,768]{1,0:T(8,128)(2,1)S(1)}) fusion(f32[1024,768]{1,0:T(8,128)} %copy.70, f32[1024,768]{1,0:T(8,128)} %copy.64, f32[1024,2304]{1,0:T(8,128)} %copy-done.11, f32[1024,768]{1,0:T(8,128)} %copy.66), kind=kLoop, calls=%fused_computation.102 | loop fusion | flops 4718592 | bytes 18874368 | tf_op jit(solution)/shard_map/convert_element_type | solution.py:290
  201.9 4.0 collective-permute-start
  207.2 4.8 reshape_reshape.6
  212.0 6.7 fusion.47
  224.5 6.2 copy.84
  230.7 5.8 copy.86
  238.8 3.8 pad_maximum_fusion.10
  246.6 4.5 fusion.82
  251.1 3.4 fusion.1
  256.9 5.7 fusion.50
  269.2 4.4 fusion.83
  273.7 3.4 fusion
  279.2 5.7 fusion.51
  293.9 3.9 convolution_bitcast_fusion
  297.9 11.4 %fusion.49 = (f32[1024,1152]{1,0:T(8,128)}, f32[1024,1152]{1,0:T(8,128)S(1)}) fusion(f32[1024,1152]{1,0:T(8,128)S(1)} %bitcast.159, f32[1024,2304]{1,0:T(8,128)S(1)} %convolution_bitcast_fusion), kind=kLoop, calls=%fused_computation.126 | loop fusion | flops 76677120 | bytes 18874368 | tf_op jit(solution)/shard_map/transpose(jvp())/mul | solution.py:90
  309.3 3.6 multiply_add_fusion
  312.9 9.1 %multiply_reduce_fusion.2 = (f32[768]{0:T(1024)S(1)}, f32[1024]{0:T(1024)S(1)}, f32[1024]{0:T(1024)S(1)}, f32[1024,768]{0,1:T(8,128)S(1)}) fusion(f32[1024,768]{0,1:T(8,128)S(1)} %get-tuple-element.132, f32[1024]{0:T(1024)S(1)} %add_rsqrt_fusion, f32[1024]{0:T(1024)S(1)} %broadcast_multiply_fusion.4, f32[768]{0:T(1024)S(1)} %reshape.465, ...), kind=kOutput, calls=%fused_computation.96 | convolution fusion | flops 3634885888 | bytes 19290112 | tf_op jit(solution)/shard_map/tn,dnr->tdr/dot_general | solution.py:246
  325.7 7.1 %fusion.6 = f32[12,64,640]{2,1,0:T(8,128)S(1)} fusion(bf16[512,12,64]{0,2,1:T(8,128)(2,1)S(1)} %bitcast.199, f32[12,512,640]{2,1,0:T(8,128)} %copy-done.2, f32[12,512]{1,0:T(8,128)S(1)} %copy-done.47), kind=kOutput, calls=%fused_computation.31 | convolution fusion | flops 511180800 | bytes 18505728 | tf_op jit(solution)/shard_map/hqk,qhd->khd/dot_general | solution.py:370
  332.8 12.8 %multiply_reduce_fusion.1 = (f32[12,512]{1,0:T(8,128)}, f32[12,512,640]{2,1,0:T(8,128)}) fusion(f32[12,512,640]{2,1,0:T(8,128)} %copy-done.2, f32[12,512]{1,0:T(8,128)S(1)} %copy-done.47, bf16[512,12,64]{0,2,1:T(8,128)(2,1)} %bitcast.200, bf16[640,12,64]{0,2,1:T(8,128)(2,1)} %bitcast.216), kind=kOutput, calls=%fused_computation.4 | convolution fusion | flops 515106816 | bytes 33275904 | tf_op jit(solution)/shard_map/qhd,khd->hqk/dot_general | solution.py:359
  345.8 4.2 fusion.4
  349.9 10.6 %multiply_reduce_fusion = (f32[12,512]{1,0:T(8,128)}, f32[12,512,640]{2,1,0:T(8,128)}) fusion(f32[12,512,640]{2,1,0:T(8,128)S(1)} %bitcast.153, f32[12,512]{1,0:T(8,128)S(1)} %log_add_fusion, bf16[512,12,64]{0,2,1:T(8,128)(2,1)S(1)} %bitcast.198, bf16[640,12,64]{0,2,1:T(8,128)(2,1)} %bitcast.214), kind=kOutput, calls=%fused_computation.1 | convolution fusion | flops 515106816 | bytes 33275904 | tf_op jit(solution)/shard_map/qhd,khd->hqk/dot_general | solution.py:359
  362.4 11.2 %multiply_convert_fusion.1 = bf16[12,512,640]{2,1,0:T(8,128)(2,1)S(1)} fusion(f32[12,512,640]{2,1,0:T(8,128)} %get-tuple-element.135, f32[12,512,640]{2,1,0:T(8,128)} %copy-done.2, f32[12,512]{1,0:T(8,128)S(1)} %copy-done.56, f32[12,512]{1,0:T(8,128)S(1)} %copy-done.48), kind=kLoop, calls=%fused_computation.3 | loop fusion | flops 15728640 | bytes 39370752 | tf_op jit(solution)/shard_map/convert_element_type | solution.py:361
  381.4 11.2 %multiply_convert_fusion = bf16[12,512,640]{2,1,0:T(8,128)(2,1)S(1)} fusion(f32[12,512,640]{2,1,0:T(8,128)} %get-tuple-element.137, f32[12,512,640]{2,1,0:T(8,128)} %copy-done.1, f32[12,512]{1,0:T(8,128)S(1)} %copy-done.55, f32[12,512]{1,0:T(8,128)S(1)} %copy-done.50), kind=kLoop, calls=%fused_computation | loop fusion | flops 15728640 | bytes 39370752 | tf_op jit(solution)/shard_map/convert_element_type | solution.py:361
  404.1 3.5 slice.367
  415.5 4.1 convolution_bitcast_fusion.5
  419.7 5.9 convolution_bitcast_fusion.3
  425.6 4.3 copy.79
  430.8 5.3 collective-permute-start.4
  447.2 8.1 %copy.103 = f32[2,2304,384]{2,1,0:T(8,128)} copy(f32[2,2304,384]{1,2,0:T(8,128)} %convolution_bitcast_fusion.3) | data formatting | bytes 14155776 | tf_op jit(solution)/shard_map/tn,tdr->dnr/transpose | solution.py:251
  455.2 5.9 convolution_bitcast_fusion.4
  461.1 5.3 copy.104
  466.4 5.5 reshape_reshape.7
  473.4 7.2 %constant_dynamic-update-slice_fusion.2 = f32[2,16,424,384]{3,2,1,0:T(8,128)} fusion(f32[2,16,424,384]{3,2,1,0:T(8,128)} %constant_dynamic-update-slice_fusion.3, f32[2,16,144,384]{3,2,1,0:T(8,128)} %bitcast.162), kind=kLoop, calls=%fused_computation.175 | loop fusion | bytes 14155776
  490.8 3.7 copy.97
  496.9 3.4 fusion.35
  500.3 3.6 copy.91
  503.9 3.8 copy.98
  507.7 6.1 fusion.37
  513.9 6.2 convolution_bitcast_fusion.2
  520.1 6.7 fusion.32
  526.8 8.0 %copy.106 = f32[2,2304,384]{2,1,0:T(8,128)} copy(f32[2,2304,384]{1,2,0:T(8,128)} %convolution_bitcast_fusion.2) | data formatting | bytes 14155776 | tf_op jit(solution)/shard_map/tn,tdr->dnr/transpose | solution.py:251
  535.0 6.3 constant_dynamic-update-slice_fusion
  542.1 3.7 fusion.39
  545.8 5.0 copy-done
  567.8 6.0 fusion.38
  577.3 7.3 %fusion.31 = f32[1024,768]{0,1:T(8,128)} fusion(f32[1024,768]{0,1:T(8,128)} %copy-done.15, bf16[1024,768]{0,1:T(8,128)(2,1)S(1)} %copy-done.7, f32[1024,768]{0,1:T(8,128)} %get-tuple-element.138, f32[1024]{0:T(1024)S(1)} %broadcast_multiply_fusion, f32[1024]{0:T(1024)S(1)} %broadcast_multiply_fusion.1, f32[768]{0:T(1024)S(1)} %copy-done.60, ...), kind=kLoop, calls=%fused_computation.78 | loop fusion | flops 7077888 | bytes 11029504 | tf_op jit(solution)/shard_map/add | solution.py:399
  584.6 4.3 copy.109
  588.9 11.9 %reduce-scatter.2.cloned.1.call-done = f32[1,7168,384]{2,1,0:T(8,128)} async-done(((f32[2,7168,384]{2,1,0:T(8,128)}), f32[1,7168,384]{2,1,0:T(8,128)}) %reduce-scatter.2.cloned.1.call-update) | async-done | bytes 11010064 | tf_op jit(solution)/shard_map/reduce_scatter | solution.py:420
  600.8 71.0 %shard_map.161 = f32[448,384]{1,0:T(8,128)S(1)} custom-call(f32[16,448,384]{2,1,0:T(8,128)} %bitcast.185), custom_call_target="tpu_custom_call" | custom-call | tf_op jit(solution)/shard_map/pallas_call | solution.py:204
  (291 shorter events, 144.8 us)
Async XLA Ops:
  7.2 67.7 %all-gather.3.cloned.1.call-start = ((), (), s32[]{:S(2)}) async-start(), calls=%async_computation.1 | async-start | bytes 3852288 | tf_op jit(solution)/shard_map/all_gather | solution.py:227
  9.5 138.9 %all-gather.5.cloned.1.call-start = ((), (), s32[]{:S(2)}) async-start(), calls=%async_computation.2 | async-start | bytes 6893568 | tf_op jit(solution)/shard_map/all_gather | solution.py:227
  15.4 585.4 %reduce-scatter.2.cloned.1.call-start = ((), (), s32[]{:S(2)}) async-start(), calls=%async_computation.3 | async-start | bytes 33030144 | tf_op jit(solution)/shard_map/reduce_scatter | solution.py:420
  16.2 16.7 %collective-permute-start.1 = (s32[64]{0:T(128)S(1)}, s32[64]{0:T(128)S(1)}, u32[]{:S(2)}, u32[]{:S(2)}) collective-permute-start(s32[64]{0:T(128)S(1)} %get-tuple-element.122), channel_id=1, source_target_pairs={{0,1},{1,2},{2,3},{3,4},{4,5},{5,6},{6,7},{7,8},{8,9},{9,10},{10,1... | collective-permute-start | bytes 776 | tf_op jit(solution)/shard_map/ppermute | solution.py:25
  21.0 11.9 %collective-permute-start.3 = (s32[64]{0:T(128)S(1)}, s32[64]{0:T(128)S(1)}, u32[]{:S(2)}, u32[]{:S(2)}) collective-permute-start(s32[64]{0:T(128)S(1)} %get-tuple-element.123), channel_id=1, source_target_pairs={{1,0},{2,1},{3,2},{4,3},{5,4},{6,5},{7,6},{8,7},{9,8},{10,9},{11,1... | collective-permute-start | bytes 776 | tf_op jit(solution)/shard_map/ppermute | solution.py:26
  24.1 263.2 %copy-start.6 = (bf16[1024,768]{0,1:T(8,128)(2,1)}, bf16[1024,768]{0,1:T(8,128)(2,1)S(1)}, u32[]{:S(2)}) copy-start(bf16[1024,768]{0,1:T(8,128)(2,1)S(1)} %copy.62) | copy-start | bytes 4718596
  24.7 158.4 %copy-start.34 = (f32[1024,64]{0,1:T(8,128)}, f32[1024,64]{0,1:T(8,128)S(1)}, u32[]{:S(2)}) copy-start(f32[1024,64]{0,1:T(8,128)S(1)} %get-tuple-element.142) | copy-start | bytes 786436
  25.0 126.7 %copy-start.57 = (f32[1024]{0:T(1024)}, f32[1024]{0:T(1024)S(1)}, u32[]{:S(2)}) copy-start(f32[1024]{0:T(1024)S(1)} %broadcast_multiply_fusion.5) | copy-start | bytes 12292
  25.4 126.2 %copy-start.61 = (f32[1024]{0:T(1024)}, f32[1024]{0:T(1024)S(1)}, u32[]{:S(2)}) copy-start(f32[1024]{0:T(1024)S(1)} %add_rsqrt_fusion.1) | copy-start | bytes 12292
  151.7 7.0 %copy-start.59 = (f32[768]{0:T(1024)}, f32[768]{0:T(1024)S(1)}, u32[]{:S(2)}) copy-start(f32[768]{0:T(1024)S(1)} %reshape.464) | copy-start | bytes 9220
  152.2 6.5 copy-start.38
  158.7 7.9 %copy-start.11 = (f32[1024,2304]{1,0:T(8,128)}, f32[1024,2304]{1,0:T(8,128)S(1)}, u32[]{:S(2)}) copy-start(f32[1024,2304]{1,0:T(8,128)S(1)} %convolution_bitcast_fusion.1) | copy-start | bytes 28311556
  158.7 7.9 %slice-start.12 = ((s8[6684672]{0:T(1024)(128)(4,1)}), s8[4194304]{0:T(1024)(128)(4,1)S(1)}, s32[]{:S(2)}) async-start(s8[6684672]{0:T(1024)(128)(4,1)} %bitcast.203), calls=%async_computation.16 | async-start | bytes 8388608
  160.0 6.6 slice-start.13
  194.0 7.8 %copy-start.13 = (bf16[1024,768]{1,0:T(8,128)(2,1)S(1)}, bf16[1024,768]{1,0:T(8,128)(2,1)}, u32[]{:S(2)}) copy-start(bf16[1024,768]{1,0:T(8,128)(2,1)} %slice.468) | copy-start | bytes 4718596
  201.9 37.0 %collective-permute-start = (bf16[64,1536]{1,0:T(8,128)(2,1)S(1)}, bf16[64,1536]{1,0:T(8,128)(2,1)}, u32[]{:S(2)}, u32[]{:S(2)}) collective-permute-start(bf16[64,1536]{1,0:T(8,128)(2,1)S(1)} %get-tuple-element.98), channel_id=1, source_target_pairs={{0,1},{1,2},{2,3},{3,4},{4,5},{5,6},{6,7},{7,8},{8,9},{9,10},{10,1... | collective-permute-start | bytes 589832 | tf_op jit(solution)/shard_map/ppermute | solution.py:25
  205.9 33.0 %collective-permute-start.2 = (bf16[64,1536]{1,0:T(8,128)(2,1)S(1)}, bf16[64,1536]{1,0:T(8,128)(2,1)}, u32[]{:S(2)}, u32[]{:S(2)}) collective-permute-start(bf16[64,1536]{1,0:T(8,128)(2,1)S(1)} %get-tuple-element.99), channel_id=1, source_target_pairs={{1,0},{2,1},{3,2},{4,3},{5,4},{6,5},{7,6},{8,7},{9,8},{10,9},{11,1... | collective-permute-start | bytes 589832 | tf_op jit(solution)/shard_map/ppermute | solution.py:26
  212.0 6.7 copy-start.28
  246.6 4.5 copy-start.20
  251.1 5.6 copy-start.1
  251.1 5.8 copy-start.51
  251.1 5.8 copy-start.31
  254.5 8.1 %copy-start.53 = (f32[12,512]{1,0:T(8,128)}, f32[12,512]{1,0:T(8,128)S(1)}, u32[]{:S(2)}) copy-start(f32[12,512]{1,0:T(8,128)S(1)} %fusion.1) | copy-start | bytes 73732
  262.6 6.6 copy-start.19
  262.6 6.6 copy-start.43
  264.2 23.1 %copy-start.45 = (bf16[512,2,384]{2,0,1:T(8,128)(2,1)}, bf16[512,2,384]{2,0,1:T(8,128)(2,1)S(1)}, u32[]{:S(2)}) copy-start(bf16[512,2,384]{2,0,1:T(8,128)(2,1)S(1)} %copy.77) | copy-start | bytes 2359300
  273.7 5.6 copy-start.2
  273.7 5.5 copy-start.32
  290.2 31.8 %copy-start.10 = (f32[1024,768]{0,1:T(8,128)}, f32[1024,768]{0,1:T(8,128)S(1)}, u32[]{:S(2)}) copy-start(f32[1024,768]{0,1:T(8,128)S(1)} %get-tuple-element.132) | copy-start | bytes 9437188
  290.6 7.2 %slice-start.8 = ((s8[4718592]{0:T(1024)(128)(4,1)}), s8[4194304]{0:T(1024)(128)(4,1)S(1)}, s32[]{:S(2)}) async-start(s8[4718592]{0:T(1024)(128)(4,1)} %bitcast.158), calls=%async_computation.12 | async-start | bytes 8388608
  312.9 9.1 %copy-start.30 = (f32[1024,1152]{1,0:T(8,128)}, f32[1024,1152]{1,0:T(8,128)S(1)}, u32[]{:S(2)}) copy-start(f32[1024,1152]{1,0:T(8,128)S(1)} %get-tuple-element.82) | copy-start | bytes 14155780
  312.9 9.1 %copy-start.26 = (bf16[1024,768]{0,1:T(8,128)(2,1)S(1)}, bf16[1024,768]{0,1:T(8,128)(2,1)}, u32[]{:S(2)}) copy-start(bf16[1024,768]{0,1:T(8,128)(2,1)} %copy.82) | copy-start | bytes 4718596
  325.7 20.0 %slice-start = ((s8[15728640]{0:T(1024)(128)(4,1)}), s8[4194304]{0:T(1024)(128)(4,1)S(1)}, s32[]{:S(2)}) async-start(s8[15728640]{0:T(1024)(128)(4,1)} %bitcast.152), calls=%async_computation.4 | async-start | bytes 8388608
  325.7 20.0 %slice-start.1 = ((s8[15728640]{0:T(1024)(128)(4,1)}), s8[4194304]{0:T(1024)(128)(4,1)S(1)}, s32[]{:S(2)}) async-start(s8[15728640]{0:T(1024)(128)(4,1)} %bitcast.152), calls=%async_computation.5 | async-start | bytes 8388608
  332.8 12.9 %copy-start.52 = (f32[12,512]{1,0:T(8,128)S(1)}, f32[12,512]{1,0:T(8,128)}, u32[]{:S(2)}) copy-start(f32[12,512]{1,0:T(8,128)} %copy-done.51) | copy-start | bytes 73732
  332.8 12.9 %copy-start.54 = (f32[12,512]{1,0:T(8,128)S(1)}, f32[12,512]{1,0:T(8,128)}, u32[]{:S(2)}) copy-start(f32[12,512]{1,0:T(8,128)} %copy-done.53) | copy-start | bytes 73732
  332.8 12.9 %slice-start.2 = ((s8[15728640]{0:T(1024)(128)(4,1)}), s8[4194304]{0:T(1024)(128)(4,1)S(1)}, s32[]{:S(2)}) async-start(s8[15728640]{0:T(1024)(128)(4,1)} %bitcast.152), calls=%async_computation.6 | async-start | bytes 8388608
  332.8 12.9 %slice-start.3 = ((s8[15728640]{0:T(1024)(128)(4,1)}), s8[3145728]{0:T(1024)(128)(4,1)S(1)}, s32[]{:S(2)}) async-start(s8[15728640]{0:T(1024)(128)(4,1)} %bitcast.152), calls=%async_computation.7 | async-start | bytes 6291456
  376.6 4.8 copy-start.50
  376.6 4.8 copy-start.55
  381.4 11.2 %copy-start.18 = (bf16[512,768]{0,1:T(8,128)(2,1)S(1)}, bf16[512,768]{0,1:T(8,128)(2,1)}, u32[]{:S(2)}) copy-start(bf16[512,768]{0,1:T(8,128)(2,1)} %copy.74) | copy-start | bytes 2359300
  397.9 12.4 %slice-start.6 = ((s8[7864320]{0:T(1024)(128)(4,1)}), s8[4194304]{0:T(1024)(128)(4,1)S(1)}, s32[]{:S(2)}) async-start(s8[7864320]{0:T(1024)(128)(4,1)} %bitcast.156), calls=%async_computation.10 | async-start | bytes 8388608
  401.2 9.1 %slice-start.7 = ((s8[7864320]{0:T(1024)(128)(4,1)}), s8[3670016]{0:T(1024)(128)(4,1)S(1)}, s32[]{:S(2)}) async-start(s8[7864320]{0:T(1024)(128)(4,1)} %bitcast.156), calls=%async_computation.11 | async-start | bytes 7340032
  401.2 11.7 %slice-start.4 = ((s8[7864320]{0:T(1024)(128)(4,1)}), s8[3670016]{0:T(1024)(128)(4,1)S(1)}, s32[]{:S(2)}) async-start(s8[7864320]{0:T(1024)(128)(4,1)} %bitcast.154), calls=%async_computation.8 | async-start | bytes 7340032
  404.1 6.2 copy-start.5
  404.1 6.2 copy-start.21
  404.1 8.8 %slice-start.5 = ((s8[7864320]{0:T(1024)(128)(4,1)}), s8[4194304]{0:T(1024)(128)(4,1)S(1)}, s32[]{:S(2)}) async-start(s8[7864320]{0:T(1024)(128)(4,1)} %bitcast.154), calls=%async_computation.9 | async-start | bytes 8388608
  410.3 9.3 %slice-start.14 = ((s8[4718592]{0:T(1024)(128)(4,1)}), s8[524288]{0:T(1024)(128)(4,1)S(1)}, s32[]{:S(2)}) async-start(s8[4718592]{0:T(1024)(128)(4,1)} %bitcast.207), calls=%async_computation.18 | async-start | bytes 1048576
  410.3 9.3 %slice-start.16 = ((s8[4718592]{0:T(1024)(128)(4,1)}), s8[4194304]{0:T(1024)(128)(4,1)S(1)}, s32[]{:S(2)}) async-start(s8[4718592]{0:T(1024)(128)(4,1)} %bitcast.212), calls=%async_computation.20 | async-start | bytes 8388608
  412.9 6.7 slice-start.15
  412.9 6.7 slice-start.17
  430.8 52.7 %collective-permute-start.4 = (bf16[64,1536]{1,0:T(8,128)(2,1)S(1)}, bf16[64,1536]{1,0:T(8,128)(2,1)}, u32[]{:S(2)}, u32[]{:S(2)}) collective-permute-start(bf16[64,1536]{1,0:T(8,128)(2,1)S(1)} %slice.470), channel_id=1, source_target_pairs={{0,1},{1,2},{2,3},{3,4},{4,5},{5,6},{6,7},{7,8},{8,9},{9,10},{10,1... | collective-permute-start | bytes 589832 | tf_op jit(solution)/shard_map/ppermute | solution.py:34
  436.0 48.6 %collective-permute-start.5 = (bf16[64,1536]{1,0:T(8,128)(2,1)S(1)}, bf16[64,1536]{1,0:T(8,128)(2,1)}, u32[]{:S(2)}, u32[]{:S(2)}) collective-permute-start(bf16[64,1536]{1,0:T(8,128)(2,1)S(1)} %slice.469), channel_id=1, source_target_pairs={{1,0},{2,1},{3,2},{4,3},{5,4},{6,5},{7,6},{8,7},{9,8},{10,9},{11,1... | collective-permute-start | bytes 589832 | tf_op jit(solution)/shard_map/ppermute | solution.py:34
  472.0 11.5 %slice-start.10 = ((s8[6291456]{0:T(1024)(128)(4,1)}), s8[4194304]{0:T(1024)(128)(4,1)S(1)}, s32[]{:S(2)}) async-start(s8[6291456]{0:T(1024)(128)(4,1)} %bitcast.160), calls=%async_computation.14 | async-start | bytes 8388608
  473.4 7.3 %copy-start.12 = (f32[2,16,72,384]{3,2,1,0:T(8,128)S(1)}, f32[2,16,72,384]{3,2,1,0:T(8,128)}, u32[]{:S(2)}) copy-start(f32[2,16,72,384]{3,2,1,0:T(8,128)} %reshape_reshape.7) | copy-start | bytes 10616836
  473.4 10.2 %slice-start.11 = ((s8[6291456]{0:T(1024)(128)(4,1)}), s8[2097152]{0:T(1024)(128)(4,1)S(1)}, s32[]{:S(2)}) async-start(s8[6291456]{0:T(1024)(128)(4,1)} %bitcast.160), calls=%async_computation.15 | async-start | bytes 4194304
  507.7 6.1 copy-start.39
  507.7 6.2 copy-start.40
  513.9 6.2 copy-start.7
  513.9 6.2 copy-start.33
  513.9 6.2 copy-start.58
  513.9 6.2 copy-start.60
  513.9 6.2 copy-start.62
  542.1 8.7 %copy-start = (f32[2,16,424,384]{3,2,1,0:T(8,128)S(1)}, f32[2,16,424,384]{3,2,1,0:T(8,128)}, u32[]{:S(2)}) copy-start(f32[2,16,424,384]{3,2,1,0:T(8,128)} %broadcast_dynamic-update-slice_fusion) | copy-start | bytes 62521348
  (26 other events, 70.9 us)
Sparse Core Ops, SparseCore 0:
  11.4 63.3 all-gather.2
  78.3 69.9 all-gather.4
  566.4 34.3 reduce-scatter.1

commit v5 on v4

--- a/solution.py
+++ b/solution.py
@@ -62,16 +62,6 @@
     first = shaped[..., : HEAD // 2]
     second = shaped[..., HEAD // 2 :]
     return jnp.concatenate([-second, first], -1).reshape(count, HEADS * HEAD)
-
-
-def window_mask(own, other, count, width):
-    offset = (
-        jnp.arange(width, dtype=jnp.int32)[None, :]
-        - jnp.arange(count, dtype=jnp.int32)[:, None]
-        - HALF
-    )
-    near = jnp.abs(offset) <= HALF
-    return near & ((other[None, :] == own[:, None]) | (offset == 0))
 
 
 def left_dot(left, right):
@@ -218,6 +208,106 @@
     )(h)
 
 
+QB = 128
+
+
+def window_allow(tq_ref, tk_ref, a0, w0):
+    rows = lax.broadcasted_iota(jnp.int32, (QB, QB + 2 * HALF), 0)
+    cols = lax.broadcasted_iota(jnp.int32, (QB, QB + 2 * HALF), 1)
+    offset = cols - rows - HALF
+    near = jnp.abs(offset) <= HALF
+    same = tk_ref[:, pl.ds(w0, QB + 2 * HALF)] == tq_ref[pl.ds(a0, QB), :]
+    return near & (same | (offset == 0))
+
+
+def nt(a, b):
+    return lax.dot_general(a, b, (((1,), (1,)), ((), ())), preferred_element_type=jnp.float32)
+
+
+def tn(a, b):
+    return lax.dot_general(a, b, (((0,), (0,)), ((), ())), preferred_element_type=jnp.float32)
+
+
+def probs_of(q_ref, kv_ref, allow, a0, w0, h):
+    q_h = q_ref[pl.ds(a0, QB), pl.ds(h * HEAD, HEAD)]
+    k_h = kv_ref[pl.ds(w0, QB + 2 * HALF), pl.ds(h * HEAD, HEAD)]
+    scores = jnp.where(allow, nt(q_h, k_h) * 0.125, -1e30)
+    largest = jnp.max(scores, axis=-1, keepdims=True)
+    raised = jnp.exp(scores - largest)
+    return raised / jnp.sum(raised, axis=-1, keepdims=True), q_h, k_h
+
+
+def attn_fwd_kernel(q_ref, kv_ref, tq_ref, tk_ref, o_ref):
+    width = q_ref.shape[1]
+
+    def block(b, carry):
+        a0 = pl.multiple_of(b * QB, QB)
+        allow = window_allow(tq_ref, tk_ref, a0, a0)
+        for h in range(HEADS):
+            probs, _, _ = probs_of(q_ref, kv_ref, allow, a0, a0, h)
+            v_h = kv_ref[pl.ds(a0, QB + 2 * HALF), pl.ds(width + h * HEAD, HEAD)]
+            mixed = jnp.dot(probs.astype(jnp.bfloat16), v_h, preferred_element_type=jnp.float32)
+            o_ref[pl.ds(a0, QB), pl.ds(h * HEAD, HEAD)] = mixed.astype(o_ref.dtype)
+        return carry
+
+    lax.fori_loop(0, q_ref.shape[0] // QB, block, 0)
+
+
+def attn_bwd_kernel(q_ref, kv_ref, tq_ref, tk_ref, do_ref, dq_ref, dkv_ref):
+    width = q_ref.shape[1]
+    dkv_ref[...] = jnp.zeros(dkv_ref.shape, dkv_ref.dtype)
+
+    def block(b, carry):
+        a0 = pl.multiple_of(b * QB, QB)
+        allow = window_allow(tq_ref, tk_ref, a0, a0)
+        for h in range(HEADS):
+            probs, q_h, k_h = probs_of(q_ref, kv_ref, allow, a0, a0, h)
+            v_h = kv_ref[pl.ds(a0, QB + 2 * HALF), pl.ds(width + h * HEAD, HEAD)]
+            do_h = do_ref[pl.ds(a0, QB), pl.ds(h * HEAD, HEAD)]
+            grad_probs = nt(do_h, v_h)
+            inner = jnp.sum(probs * grad_probs, axis=-1, keepdims=True)
+            grad_scores = (probs * (grad_probs - inner)).astype(jnp.bfloat16)
+            dq_ref[pl.ds(a0, QB), pl.ds(h * HEAD, HEAD)] = (
+                jnp.dot(grad_scores, k_h, preferred_element_type=jnp.float32) * 0.125
+            )
+            rows = pl.ds(a0, QB + 2 * HALF)
+            dkv_ref[rows, pl.ds(h * HEAD, HEAD)] += tn(grad_scores, q_h) * 0.125
+            dkv_ref[rows, pl.ds(width + h * HEAD, HEAD)] += tn(probs.astype(jnp.bfloat16), do_h)
+        return carry
+
+    lax.fori_loop(0, q_ref.shape[0] // QB, block, 0)
+
+
+VMEM_LIMIT = 48 * 1024 * 1024
+
+
+def attn_fwd(query, wide_kv, tag_q, tag_k):
+    count, width = query.shape
+    vm = pl.BlockSpec(memory_space=pltpu.VMEM)
+    return pl.pallas_call(
+        attn_fwd_kernel,
+        out_shape=jax.ShapeDtypeStruct((count, width), jnp.bfloat16),
+        in_specs=[vm] * 4,
+        out_specs=vm,
+        compiler_params=pltpu.CompilerParams(vmem_limit_bytes=VMEM_LIMIT),
+    )(query, wide_kv, tag_q.reshape(count, 1), tag_k.reshape(1, -1))
+
+
+def attn_bwd(query, wide_kv, tag_q, tag_k, grad_out):
+    count, width = query.shape
+    vm = pl.BlockSpec(memory_space=pltpu.VMEM)
+    return pl.pallas_call(
+        attn_bwd_kernel,
+        out_shape=(
+            jax.ShapeDtypeStruct((count, width), jnp.float32),
+            jax.ShapeDtypeStruct(wide_kv.shape, jnp.float32),
+        ),
+        in_specs=[vm] * 5,
+        out_specs=(vm, vm),
+        compiler_params=pltpu.CompilerParams(vmem_limit_bytes=VMEM_LIMIT),
+    )(query, wide_kv, tag_q.reshape(count, 1), tag_k.reshape(1, -1), grad_out)
+
+
 def gain_rows(gain, width, rows=8):
     line = jnp.pad(gain, (0, width - gain.shape[0]))
     return jnp.concatenate([line[None], jnp.zeros((rows - 1, width), gain.dtype)], 0)
@@ -297,39 +387,7 @@
         padded(key_value, ((("dp", "seq"), 0),), HALF),
         padded(tag_key, ((("dp", "seq"), 0),), HALF),
     )
-    block_rows = 512
-    width = block_rows + 2 * HALF
-    blocks = count // block_rows
-
-    def block_scores(start):
-        q_blk = query[start : start + block_rows].reshape(block_rows, HEADS, HEAD)
-        k_blk = wide_kv[start : start + width, :D].reshape(width, HEADS, HEAD)
-        v_blk = wide_kv[start : start + width, D:].reshape(width, HEADS, HEAD)
-        scores = (
-            jnp.einsum("qhd,khd->hqk", q_blk, k_blk, preferred_element_type=jnp.float32) * 0.125
-        )
-        mask = window_mask(
-            tag_query[start : start + block_rows],
-            wide_tag[start : start + width],
-            block_rows,
-            width,
-        )
-        return (jnp.where(mask[None], scores, -1e30), q_blk, k_blk, v_blk)
-
-    attended = []
-    log_totals = []
-    for number in range(blocks):
-        scores, q_blk, k_blk, v_blk = block_scores(number * block_rows)
-        largest = jnp.max(scores, axis=-1, keepdims=True)
-        raised = jnp.exp(scores - largest)
-        total = jnp.sum(raised, axis=-1, keepdims=True)
-        probs = raised / total
-        log_totals.append(largest + jnp.log(total))
-        mixed = jnp.einsum(
-            "hqk,khd->qhd", probs.astype(jnp.bfloat16), v_blk, preferred_element_type=jnp.float32
-        )
-        attended.append(mixed.reshape(block_rows, D))
-    attn_out = jnp.concatenate(attended, 0).astype(jnp.bfloat16)
+    attn_out = attn_fwd(query, wide_kv, tag_query, wide_tag)
     mid = stream + apply_t(attn_out, full_out, n_dp)
     normed_m, factor_m = layer_norm(mid)
     h_mlp = (normed_m * gain_two).astype(jnp.bfloat16)
@@ -348,32 +406,7 @@
     grad_branch = grad_mid.astype(jnp.bfloat16)
     grad_outw = grad_t(grad_branch, attn_out, n_dp)
     grad_attn = apply_back(grad_branch, full_out).astype(jnp.bfloat16)
-    grad_wide = jnp.zeros((count + 2 * HALF, 2 * D), jnp.float32)
-    grad_queries = []
-    for number in range(blocks):
-        start = number * block_rows
-        scores, q_blk, k_blk, v_blk = block_scores(start)
-        probs = jnp.exp(scores - log_totals[number])
-        probs_low = probs.astype(jnp.bfloat16)
-        grad_blk = grad_attn[start : start + block_rows].reshape(block_rows, HEADS, HEAD)
-        grad_probs = jnp.einsum("qhd,khd->hqk", grad_blk, v_blk, preferred_element_type=jnp.float32)
-        inner = jnp.sum(probs * grad_probs, axis=-1, keepdims=True)
-        grad_scores = (probs * (grad_probs - inner)).astype(jnp.bfloat16)
-        grad_qblk = (
-            jnp.einsum("hqk,khd->qhd", grad_scores, k_blk, preferred_element_type=jnp.float32)
-            * 0.125
-        )
-        grad_kblk = (
-            jnp.einsum("hqk,qhd->khd", grad_scores, q_blk, preferred_element_type=jnp.float32)
-            * 0.125
-        )
-        grad_vblk = jnp.einsum(
-            "hqk,qhd->khd", probs_low, grad_blk, preferred_element_type=jnp.float32
-        )
-        grad_queries.append(grad_qblk.reshape(block_rows, D))
-        grad_wide = grad_wide.at[start : start + width].add(
-            jnp.concatenate([grad_kblk.reshape(width, D), grad_vblk.reshape(width, D)], 1)
-        )
+    grad_query, grad_wide = attn_bwd(query, wide_kv, tag_query, wide_tag, grad_attn)
     from_above = shifted(grad_wide[:HALF].astype(jnp.bfloat16), ("dp", "seq"), -1).astype(
         jnp.float32
     )
@@ -383,7 +416,6 @@
     grad_kv = grad_wide[HALF : HALF + count]
     grad_kv = grad_kv.at[:HALF].add(from_below)
     grad_kv = grad_kv.at[count - HALF :].add(from_above)
-    grad_query = jnp.concatenate(grad_queries, 0)
     grad_keys = grad_kv[:, :D]
     grad_qkv = jnp.concatenate(
         [

time: 693 us -> 629 us (0.908)
  Pallas kernels: 71 us -> 147 us
  matrix products: 128 us -> 59.9 us
  local copies, waits for them, and re-layouts: 229 us -> 192 us
  other arithmetic: 104 us -> 69.9 us
    pallas_call x0 -> x2, Pallas kernels: none -> 76.2 us  [the longest x1 55.4 us: attn_bwd(): pl.pallas_call(attn_bwd_kernel, out_shape=(jax.ShapeDtypeStruct((count, w...]
    dot_general x12 -> x0, matrix products: 63 us -> none  [the longest x2 23.5 us: on_device(): jnp.einsum('qhd,khd->hqk', grad_blk, v_blk, preferred_element_type=jnp.fl...]
    convert_element_type x3 -> x1, other arithmetic: 30.2 us -> 6.66 us  [on_device(): (qkv[:, D:2 * D] * cosine + rotate(qkv[:, D:2 * D]) * sine).astype(jnp.bf...]
    slice x11 -> x1, local copies, waits for them, and re-layouts: 15.8 us -> 0.07 us  [padded(): initial = lax.slice_in_dim(value, 0, width, axis=dim)]
    reshape x6 -> x3, local copies, waits for them, and re-layouts: 11.9 us -> 2.65 us  [the longest x1 1.63 us: front(): return value.reshape(value.shape[0], n_dp, -1)]
    unnamed x185 -> x121, local copies, waits for them, and re-layouts: 73.2 us -> 71.5 us
  transfers between devices with their start and end apart: 9 -> 9, of which waited for: 3 -> 3; matrix products, arithmetic and copies ran while one was open for 19% -> 13% of each run, Pallas kernels for 0% -> 0%
where the time goes in v5:
time: 629 us; the launch traced here: 618 us
  local copies, waits for them, and re-layouts  192 us (31%)
  Pallas kernels  147 us (23%)
  waiting for transfers between devices  116 us (18%)
  other arithmetic  69.9 us (11%)
  matrix products  59.9 us (10%)
  starting transfers between devices  18.4 us (3%)
  between operations  14.7 us (2%)
    all_gather x2, waiting for transfers between devices, gather_rows(): every = lax.all_gather(payload, ('dp', 'seq'), axis=0, tiled=True)  103 us
    unnamed x121, local copies, waits for them, and re-layouts  71.5 us
    pallas_call x1, Pallas kernels, ring_reduce(): pl.pallas_call(functools.partial(ring_kernel, tuple(order), per_way), out...  71.1 us
    pallas_call x1, Pallas kernels, attn_bwd(): pl.pallas_call(attn_bwd_kernel, out_shape=(jax.ShapeDtypeStruct((count, w...  55.4 us
    transpose x4, local copies, waits for them, and re-layouts, grad_t(): jnp.einsum('tn,tdr->dnr', grad, front(left, n_dp), preferred_element_type...  22.3 us
    dot_general x4, matrix products, grad_t(): jnp.einsum('tn,tdr->dnr', grad, front(left, n_dp), preferred_element_type...  21.5 us
    pallas_call x1, Pallas kernels, attn_fwd(): pl.pallas_call(attn_fwd_kernel, out_shape=jax.ShapeDtypeStruct((count, wi...  20.9 us
    dot_general x4, matrix products, apply_t(): jnp.einsum('tdr,dnr->tn', front(left, n_dp), weight_t, preferred_element_...  20 us
  transfers between devices with their start and end apart: 9, of which 3 were waited for; matrix products, arithmetic and copies ran while one was open for 13% of the time, Pallas kernels for 0%

profile of v5, /device:TPU:0, one launch (start us, length us, event | category | flops | bytes accessed | tf_op | source)
XLA Modules:
  0.0 617.9 jit_solution(10804468584356825091)
XLA Ops:
  11.2 4.2 concatenate.58
  17.5 5.5 collective-permute-start.2
  31.6 3.5 copy.34
  35.3 39.6 %all-gather.3.cloned.1.call-done = bf16[4864,384]{1,0:T(8,128)(2,1)} async-done(((bf16[152,384]{1,0:T(8,128)(2,1)}), bf16[4864,384]{1,0:T(8,128)(2,1)}) %all-gather.3.cloned.1.call-update) | async-done | bytes 3735568 | tf_op jit(solution)/shard_map/all_gather | solution.py:317
  74.8 4.2 slice.246
  79.0 5.8 copy.59
  84.8 63.5 %all-gather.5.cloned.1.call-done = bf16[8704,384]{1,0:T(8,128)(2,1)} async-done(((bf16[272,384]{1,0:T(8,128)(2,1)}), bf16[8704,384]{1,0:T(8,128)(2,1)}) %all-gather.5.cloned.1.call-update) | async-done | bytes 6684688 | tf_op jit(solution)/shard_map/all_gather | solution.py:317
  152.0 6.5 %convolution_bitcast_fusion.1 = f32[1024,2304]{1,0:T(8,128)S(1)} fusion(bf16[1024,2,384]{0,2,1:T(8,128)(2,1)S(1)} %bitcast.143, bf16[2,2304,384]{2,1,0:T(8,128)(2,1)} %bitcast.116), kind=kOutput, calls=%fused_computation.16 | convolution fusion | flops 3623878656 | bytes 14548992 | tf_op jit(solution)/shard_map/tdr,dnr->tn/dot_general | solution.py:332
  162.6 3.2 fusion.53
  165.7 3.2 reshape_reshape.6
  180.0 3.6 copy.39
  183.6 2.8 copy.36
  186.4 6.7 %add_convert_fusion.1 = (bf16[1024,768]{1,0:T(8,128)(2,1)S(1)}, bf16[1024,768]{1,0:T(8,128)(2,1)S(1)}) fusion(f32[1024,768]{1,0:T(8,128)} %copy.39, f32[1024,768]{1,0:T(8,128)} %copy.34, f32[1024,2304]{1,0:T(8,128)} %copy-done.8, f32[1024,768]{1,0:T(8,128)} %copy.36), kind=kLoop, calls=%fused_computation.72 | loop fusion | flops 4718592 | bytes 18874368 | tf_op jit(solution)/shard_map/convert_element_type | solution.py:381
  193.9 3.6 collective-permute-start
  198.9 4.5 fusion.29
  210.0 5.8 copy.50
  215.7 6.1 copy.48
  221.8 5.3 pad_maximum_fusion.1.kv_ref
  227.1 20.9 %shard_map.161 = bf16[1024,768]{1,0:T(8,128)(2,1)S(1)} custom-call(bf16[1024,768]{1,0:T(8,128)(2,1)S(1)} %get-tuple-element.63.q_ref, bf16[1152,1536]{1,0:T(8,128)(2,1)} %pad_maximum_fusion.1.kv_ref, s32[1024,1]{1,0:T(8,128)S(1)} %copy-done, s32[1,1152]{1,0:T(1,128)S(1)} %reshape.236.tk_ref), custom_call_target="tpu_custom_call" | custom-call | tf_op jit(solution)/shard_map/pallas_call | solution.py:287
  249.7 3.6 fusion.56
  256.5 3.9 convolution_bitcast_fusion
  260.4 11.3 %fusion.31 = (f32[1024,1152]{1,0:T(8,128)}, f32[1024,1152]{1,0:T(8,128)S(1)}) fusion(f32[1024,1152]{1,0:T(8,128)S(1)} %bitcast.106, f32[1024,2304]{1,0:T(8,128)S(1)} %convolution_bitcast_fusion), kind=kLoop, calls=%fused_computation.92 | loop fusion | flops 76677120 | bytes 18874368 | tf_op jit(solution)/shard_map/transpose(jvp())/mul | solution.py:80
  271.7 3.5 multiply_add_fusion
  275.3 8.4 %convolution_bitcast_fusion.3 = f32[2,2304,384]{1,2,0:T(8,128)} fusion(bf16[1024,2,384]{0,2,1:T(8,128)(2,1)S(1)} %bitcast.148, f32[1024,1152]{1,0:T(8,128)S(1)} %get-tuple-element.60, f32[1024,1152]{1,0:T(8,128)} %get-tuple-element.58), kind=kOutput, calls=%fused_computation.18 | convolution fusion | flops 3628597248 | bytes 18087936 | tf_op jit(solution)/shard_map/tn,tdr->dnr/dot_general | solution.py:341
  283.7 5.9 multiply_reduce_fusion
  289.6 3.0 multiply_add_fusion.1
  292.6 2.8 convolution_bitcast_fusion.5
  296.9 55.4 %shard_map.162 = (f32[1024,768]{1,0:T(8,128)}, f32[1152,1536]{1,0:T(8,128)}) custom-call(bf16[1024,768]{1,0:T(8,128)(2,1)S(1)} %get-tuple-element.63.q_ref, bf16[1152,1536]{1,0:T(8,128)(2,1)} %pad_maximum_fusion.1.kv_ref, s32[1024,1]{1,0:T(8,128)S(1)} %copy-done.1, s32[1,1152]{1,0:T(1,128)S(1)} %reshape.236.tk_ref, ...), custom_call_target="tpu_custom_call" | custom-call | tf_op jit(solution)/shard_map/pallas_call | solution.py:299
  352.3 5.4 convert.21
  358.3 3.1 slice.216
  361.5 2.5 copy.43
  364.7 3.1 copy.62
  367.8 8.0 %copy.63 = f32[2,2304,384]{2,1,0:T(8,128)} copy(f32[2,2304,384]{1,2,0:T(8,128)} %convolution_bitcast_fusion.3) | data formatting | bytes 14155776 | tf_op jit(solution)/shard_map/tn,tdr->dnr/transpose | solution.py:341
  375.8 4.1 convolution_bitcast_fusion.4
  379.9 3.1 copy.64
  383.1 5.5 reshape_reshape.7
  388.6 3.7 copy.54
  392.2 4.2 slice_negate_fusion.1
  398.8 5.2 collective-permute-start.4
  405.7 4.1 constant_dynamic-update-slice_fusion.2
  419.6 2.8 copy.57
  429.0 3.7 copy.58
  432.7 6.1 subtract_convert_fusion.1
  438.9 6.2 %convolution_bitcast_fusion.2 = f32[2,2304,384]{1,2,0:T(8,128)} fusion(bf16[1024,2,384]{0,2,1:T(8,128)(2,1)S(1)} %bitcast.144, bf16[1024,768]{1,0:T(8,128)(2,1)S(1)} %copy-done.32, bf16[1024,768]{1,0:T(8,128)(2,1)S(1)} %get-tuple-element.69, bf16[1024,768]{1,0:T(8,128)(2,1)S(1)} %get-tuple-element.68), kind=kOutput, calls=%fused_computation.17 | convolution fusion | flops 3638034432 | bytes 13369344 | tf_op jit(solution)/shard_map/tn,tdr->dnr/dot_general | solution.py:341
  445.2 6.4 %fusion.20 = (f32[768]{0:T(1024)S(1)}, f32[1024]{0:T(1024)}, f32[1024]{0:T(1024)S(1)}, f32[1024,768]{0,1:T(8,128)}) fusion(bf16[1024,768]{0,1:T(8,128)(2,1)S(1)} %copy-done.3, f32[1024]{0:T(1024)S(1)} %copy-done.40, f32[1024]{0:T(1024)S(1)} %copy-done.36, f32[768]{0:T(1024)S(1)} %copy-done.38, bf16[768,2304]{1,0:T(8,128)(2,1)S(1)} %bitcast.137, ...), kind=kOutput, calls=%fused_computation.55 | convolution fusion | flops 3645109504 | bytes 12998656 | tf_op jit(solution)/shard_map/tn,dnr->tdr/dot_general | solution.py:336
  451.7 8.0 %copy.66 = f32[2,2304,384]{2,1,0:T(8,128)} copy(f32[2,2304,384]{1,2,0:T(8,128)} %convolution_bitcast_fusion.2) | data formatting | bytes 14155776 | tf_op jit(solution)/shard_map/tn,tdr->dnr/transpose | solution.py:341
  459.8 6.3 %constant_dynamic-update-slice_fusion = f32[2,16,424,384]{3,2,1,0:T(8,128)} fusion(f32[2,16,424,384]{3,2,1,0:T(8,128)} %broadcast_dynamic-update-slice_fusion.1, f32[2,16,144,384]{3,2,1,0:T(8,128)} %bitcast.112), kind=kLoop, calls=%fused_computation.121 | loop fusion | bytes 14155776
  466.9 3.4 fusion.23
  472.9 2.5 fusion.33
  475.3 3.5 fusion.24
  478.8 2.5 fusion.34
  481.3 2.5 fusion.35
  486.3 2.5 fusion.37
  488.8 3.5 fusion.25
  492.3 2.5 fusion.38
  494.8 2.5 fusion.39
  497.3 2.5 fusion.40
  499.8 2.5 fusion.41
  503.8 6.0 fusion.22
  509.8 2.7 copy.68
  513.2 7.4 %fusion.19 = f32[1024,768]{0,1:T(8,128)} fusion(f32[1024,768]{0,1:T(8,128)} %copy-done.12, bf16[1024,768]{0,1:T(8,128)(2,1)S(1)} %copy-done.3, f32[1024,768]{0,1:T(8,128)} %get-tuple-element.98, f32[1024]{0:T(1024)S(1)} %broadcast_multiply_fusion, f32[1024]{0:T(1024)S(1)} %broadcast_multiply_fusion.1, f32[768]{0:T(1024)S(1)} %copy-done.38, ...), kind=kLoop, calls=%fused_computation.54 | loop fusion | flops 7077888 | bytes 11029504 | tf_op jit(solution)/shard_map/add | solution.py:431
  520.6 4.2 copy.69
  524.9 12.5 %reduce-scatter.2.cloned.1.call-done = f32[1,7168,384]{2,1,0:T(8,128)} async-done(((f32[2,7168,384]{2,1,0:T(8,128)}), f32[1,7168,384]{2,1,0:T(8,128)}) %reduce-scatter.2.cloned.1.call-update) | async-done | bytes 11010064 | tf_op jit(solution)/shard_map/reduce_scatter | solution.py:452
  537.4 71.1 %shard_map.163 = f32[448,384]{1,0:T(8,128)S(1)} custom-call(f32[16,448,384]{2,1,0:T(8,128)} %bitcast.126), custom_call_target="tpu_custom_call" | custom-call | tf_op jit(solution)/shard_map/pallas_call | solution.py:194
  (191 shorter events, 81.0 us)
Async XLA Ops:
  7.2 67.6 %all-gather.3.cloned.1.call-start = ((), (), s32[]{:S(2)}) async-start(), calls=%async_computation.1 | async-start | bytes 3852288 | tf_op jit(solution)/shard_map/all_gather | solution.py:317
  9.5 138.8 %all-gather.5.cloned.1.call-start = ((), (), s32[]{:S(2)}) async-start(), calls=%async_computation.2 | async-start | bytes 6893568 | tf_op jit(solution)/shard_map/all_gather | solution.py:317
  15.4 522.1 %reduce-scatter.2.cloned.1.call-start = ((), (), s32[]{:S(2)}) async-start(), calls=%async_computation.3 | async-start | bytes 33030144 | tf_op jit(solution)/shard_map/reduce_scatter | solution.py:452
  16.2 19.0 %collective-permute-start.3 = (s32[64]{0:T(128)S(1)}, s32[64]{0:T(128)S(1)}, u32[]{:S(2)}, u32[]{:S(2)}) collective-permute-start(s32[64]{0:T(128)S(1)} %get-tuple-element.90), channel_id=1, source_target_pairs={{1,0},{2,1},{3,2},{4,3},{5,4},{6,5},{7,6},{8,7},{9,8},{10,9},{11,1... | collective-permute-start | bytes 776 | tf_op jit(solution)/shard_map/ppermute | solution.py:26
  17.5 17.7 %collective-permute-start.2 = (s32[64]{0:T(128)S(1)}, s32[64]{0:T(128)S(1)}, u32[]{:S(2)}, u32[]{:S(2)}) collective-permute-start(s32[64]{0:T(128)S(1)} %get-tuple-element.91), channel_id=1, source_target_pairs={{0,1},{1,2},{2,3},{3,4},{4,5},{5,6},{6,7},{7,8},{8,9},{9,10},{10,1... | collective-permute-start | bytes 776 | tf_op jit(solution)/shard_map/ppermute | solution.py:25
  24.0 3.9 copy-start.27
  25.8 125.6 %copy-start.2 = (bf16[1024,768]{0,1:T(8,128)(2,1)}, bf16[1024,768]{0,1:T(8,128)(2,1)S(1)}, u32[]{:S(2)}) copy-start(bf16[1024,768]{0,1:T(8,128)(2,1)S(1)} %copy.32) | copy-start | bytes 4718596
  27.4 124.1 %copy-start.35 = (f32[1024]{0:T(1024)}, f32[1024]{0:T(1024)S(1)}, u32[]{:S(2)}) copy-start(f32[1024]{0:T(1024)S(1)} %broadcast_multiply_fusion.5) | copy-start | bytes 12292
  27.9 123.6 %copy-start.39 = (f32[1024]{0:T(1024)}, f32[1024]{0:T(1024)S(1)}, u32[]{:S(2)}) copy-start(f32[1024]{0:T(1024)S(1)} %add_rsqrt_fusion.1) | copy-start | bytes 12292
  151.5 7.0 %copy-start.37 = (f32[768]{0:T(1024)}, f32[768]{0:T(1024)S(1)}, u32[]{:S(2)}) copy-start(f32[768]{0:T(1024)S(1)} %reshape.255) | copy-start | bytes 9220
  152.0 6.5 %copy-start.29 = (bf16[1024,768]{0,1:T(8,128)(2,1)}, bf16[1024,768]{0,1:T(8,128)(2,1)S(1)}, u32[]{:S(2)}) copy-start(bf16[1024,768]{0,1:T(8,128)(2,1)S(1)} %fusion.15) | copy-start | bytes 4718596
  158.5 4.0 copy-start.8
  175.7 1.4 copy-start.18
  175.7 1.9 copy-start.19
  175.7 1.9 copy-start.23
  186.4 6.7 %copy-start.10 = (bf16[1024,768]{1,0:T(8,128)(2,1)S(1)}, bf16[1024,768]{1,0:T(8,128)(2,1)}, u32[]{:S(2)}) copy-start(bf16[1024,768]{1,0:T(8,128)(2,1)} %slice.348) | copy-start | bytes 4718596
  193.1 5.9 copy-start.25
  193.1 5.9 copy-start.28
  193.1 10.4 %slice-start.6 = ((s8[6684672]{0:T(1024)(128)(4,1)}), s8[4194304]{0:T(1024)(128)(4,1)S(1)}, s32[]{:S(2)}) async-start(s8[6684672]{0:T(1024)(128)(4,1)} %bitcast.130), calls=%async_computation.10 | async-start | bytes 8388608
  193.9 27.9 %collective-permute-start = (bf16[64,1536]{1,0:T(8,128)(2,1)}, bf16[64,1536]{1,0:T(8,128)(2,1)S(1)}, u32[]{:S(2)}, u32[]{:S(2)}) collective-permute-start(bf16[64,1536]{1,0:T(8,128)(2,1)} %get-tuple-element.74), channel_id=1, source_target_pairs={{0,1},{1,2},{2,3},{3,4},{4,5},{5,6},{6,7},{7,8},{8,9},{9,10},{10,1... | collective-permute-start | bytes 589832 | tf_op jit(solution)/shard_map/ppermute | solution.py:25
  197.5 6.0 slice-start.7
  197.5 24.3 %collective-permute-start.1 = (bf16[64,1536]{1,0:T(8,128)(2,1)}, bf16[64,1536]{1,0:T(8,128)(2,1)S(1)}, u32[]{:S(2)}, u32[]{:S(2)}) collective-permute-start(bf16[64,1536]{1,0:T(8,128)(2,1)} %get-tuple-element.75), channel_id=1, source_target_pairs={{1,0},{2,1},{3,2},{4,3},{5,4},{6,5},{7,6},{8,7},{9,8},{10,9},{11,1... | collective-permute-start | bytes 589832 | tf_op jit(solution)/shard_map/ppermute | solution.py:26
  221.8 5.3 copy-start
  253.3 36.3 %copy-start.6 = (f32[1024,768]{0,1:T(8,128)}, f32[1024,768]{0,1:T(8,128)S(1)}, u32[]{:S(2)}) copy-start(f32[1024,768]{0,1:T(8,128)S(1)} %get-tuple-element.96) | copy-start | bytes 9437188
  253.3 3.1 copy-start.11
  253.7 6.7 %slice-start = ((s8[4718592]{0:T(1024)(128)(4,1)}), s8[4194304]{0:T(1024)(128)(4,1)S(1)}, s32[]{:S(2)}) async-start(s8[4718592]{0:T(1024)(128)(4,1)} %bitcast.105), calls=%async_computation.4 | async-start | bytes 8388608
  256.5 4.0 slice-start.1
  275.3 8.4 %copy-start.20 = (f32[1024,1152]{1,0:T(8,128)S(1)}, f32[1024,1152]{1,0:T(8,128)}, u32[]{:S(2)}) copy-start(f32[1024,1152]{1,0:T(8,128)} %get-tuple-element.58) | copy-start | bytes 14155780
  275.3 8.4 %copy-start.22 = (bf16[2,384,2304]{2,1,0:T(8,128)(2,1)S(1)}, bf16[2,384,2304]{2,1,0:T(8,128)(2,1)}, u32[]{:S(2)}) copy-start(bf16[2,384,2304]{2,1,0:T(8,128)(2,1)} %copy.50) | copy-start | bytes 10616836
  283.6 5.9 copy-start.15
  289.6 3.0 copy-start.31
  292.6 2.9 copy-start.12
  292.6 2.8 copy-start.33
  295.5 1.5 copy-start.1
  352.3 6.0 copy-start.7
  358.3 3.1 copy-start.13
  388.6 17.1 %slice-start.4 = ((s8[7077888]{0:T(1024)(128)(4,1)}), s8[2883584]{0:T(1024)(128)(4,1)S(1)}, s32[]{:S(2)}) async-start(s8[7077888]{0:T(1024)(128)(4,1)} %bitcast.109), calls=%async_computation.8 | async-start | bytes 5767168
  392.2 11.7 %copy-start.14 = (f32[2,768,384]{2,1,0:T(8,128)S(1)}, f32[2,768,384]{2,1,0:T(8,128)}, u32[]{:S(2)}) copy-start(f32[2,768,384]{2,1,0:T(8,128)} %copy.62) | copy-start | bytes 7077892
  392.2 13.4 %slice-start.5 = ((s8[7077888]{0:T(1024)(128)(4,1)}), s8[4194304]{0:T(1024)(128)(4,1)S(1)}, s32[]{:S(2)}) async-start(s8[7077888]{0:T(1024)(128)(4,1)} %bitcast.109), calls=%async_computation.9 | async-start | bytes 8388608
  396.4 9.2 %copy-start.34 = (f32[16,1,384]{2,1,0:T(1,128)S(1)}, f32[16,1,384]{2,1,0:T(1,128)}, u32[]{:S(2)}) copy-start(f32[16,1,384]{2,1,0:T(1,128)} %copy.78) | copy-start | bytes 73732
  397.5 17.0 %collective-permute-start.5 = (bf16[64,1536]{1,0:T(8,128)(2,1)S(1)}, bf16[64,1536]{1,0:T(8,128)(2,1)S(1)}, u32[]{:S(2)}, u32[]{:S(2)}) collective-permute-start(bf16[64,1536]{1,0:T(8,128)(2,1)S(1)} %get-tuple-element.66), channel_id=1, source_target_pairs={{1,0},{2,1},{3,2},{4,3},{5,4},{6,5},{7,6},{8,7},{9,8},{10,9},{11,1... | collective-permute-start | bytes 589832 | tf_op jit(solution)/shard_map/ppermute | solution.py:34
  398.8 14.6 %collective-permute-start.4 = (bf16[64,1536]{1,0:T(8,128)(2,1)S(1)}, bf16[64,1536]{1,0:T(8,128)(2,1)S(1)}, u32[]{:S(2)}, u32[]{:S(2)}) collective-permute-start(bf16[64,1536]{1,0:T(8,128)(2,1)S(1)} %get-tuple-element.67), channel_id=1, source_target_pairs={{0,1},{1,2},{2,3},{3,4},{4,5},{5,6},{6,7},{7,8},{8,9},{9,10},{10,1... | collective-permute-start | bytes 589832 | tf_op jit(solution)/shard_map/ppermute | solution.py:34
  404.0 9.4 %slice-start.2 = ((s8[6291456]{0:T(1024)(128)(4,1)}), s8[4194304]{0:T(1024)(128)(4,1)S(1)}, s32[]{:S(2)}) async-start(s8[6291456]{0:T(1024)(128)(4,1)} %bitcast.107), calls=%async_computation.6 | async-start | bytes 8388608
  405.7 4.9 copy-start.9
  405.7 7.7 %slice-start.3 = ((s8[6291456]{0:T(1024)(128)(4,1)}), s8[2097152]{0:T(1024)(128)(4,1)S(1)}, s32[]{:S(2)}) async-start(s8[6291456]{0:T(1024)(128)(4,1)} %bitcast.107), calls=%async_computation.7 | async-start | bytes 4194304
  414.6 3.2 copy-start.4
  422.4 1.4 copy-start.16
  422.4 1.9 copy-start.17
  422.4 1.9 copy-start.24
  429.0 3.7 copy-start.5
  432.7 6.1 copy-start.30
  432.7 6.1 copy-start.32
  438.9 6.3 %copy-start.3 = (bf16[1024,768]{0,1:T(8,128)(2,1)S(1)}, bf16[1024,768]{0,1:T(8,128)(2,1)}, u32[]{:S(2)}) copy-start(bf16[1024,768]{0,1:T(8,128)(2,1)} %copy-done.2) | copy-start | bytes 4718596
  438.9 6.3 %copy-start.21 = (bf16[2,384,2304]{2,1,0:T(8,128)(2,1)S(1)}, bf16[2,384,2304]{2,1,0:T(8,128)(2,1)}, u32[]{:S(2)}) copy-start(bf16[2,384,2304]{2,1,0:T(8,128)(2,1)} %copy.59) | copy-start | bytes 10616836
  438.9 6.3 %copy-start.36 = (f32[1024]{0:T(1024)S(1)}, f32[1024]{0:T(1024)}, u32[]{:S(2)}) copy-start(f32[1024]{0:T(1024)} %copy-done.35) | copy-start | bytes 12292
  438.9 6.3 %copy-start.38 = (f32[768]{0:T(1024)S(1)}, f32[768]{0:T(1024)}, u32[]{:S(2)}) copy-start(f32[768]{0:T(1024)} %copy-done.37) | copy-start | bytes 9220
  438.9 6.3 %copy-start.40 = (f32[1024]{0:T(1024)S(1)}, f32[1024]{0:T(1024)}, u32[]{:S(2)}) copy-start(f32[1024]{0:T(1024)} %copy-done.39) | copy-start | bytes 12292
  502.3 1.5 copy-start.26
Sparse Core Ops, SparseCore 0:
  11.4 63.3 all-gather.2
  78.3 69.9 all-gather.4
  502.4 34.9 reduce-scatter.1

commit v6 on v5

--- a/solution.py
+++ b/solution.py
@@ -156,7 +156,7 @@
     for step in range(n - 1):
         slot = step % 2
         for li, (recv, send, ssem, rsem, free, to, frm, rows, sign) in enumerate(lanes):
-            q = lax.rem(pos + sign * (1 + step) + n * (step + 2), n)
+            q = lookup(lax.rem(pos + sign * (1 + step) + n * (step + 2), n), order)
             own = h_ref[q, rows, :]
             if step == 0:
                 part = own
@@ -178,7 +178,7 @@
     last = n - 2
     for li, (recv, send, ssem, rsem, free, to, frm, rows, sign) in enumerate(lanes):
         copies[(li, last)].wait_recv()
-        out_ref[rows, :] = recv[last % 2].astype(jnp.float32) + h_ref[pos, rows, :]
+        out_ref[rows, :] = recv[last % 2].astype(jnp.float32) + h_ref[me, rows, :]
         if last >= 1:
             copies[(li, last - 1)].wait_send()
         copies[(li, last)].wait_send()
@@ -447,7 +447,6 @@
     extra = (-height) % lanes_rows
     if extra:
         blocks = jnp.pad(blocks, ((0, 0), (0, 0), (0, extra), (0, 0)))
-    blocks = jnp.stack([blocks[:, s] for s in order], 1)
     depth = blocks.shape[2]
     half = lax.psum_scatter(
         blocks.reshape(n_dp, n_seq * depth, rows), "dp", scatter_dimension=0, tiled=True

time: 629 us -> 616 us (0.979)
  local copies, waits for them, and re-layouts: 192 us -> 184 us
    unnamed x121 -> x95, local copies, waits for them, and re-layouts: 71.5 us -> 40.3 us
    pad x0 -> x1, local copies, waits for them, and re-layouts: none -> 15.7 us  [on_device(): blocks = jnp.pad(blocks, ((0, 0), (0, 0), (0, extra), (0, 0)))]
  transfers between devices with their start and end apart: 9 -> 9, of which waited for: 3 -> 3; matrix products, arithmetic and copies ran while one was open for 13% -> 20% of each run, Pallas kernels for 0% -> 0%
where the time goes in v6:
time: 616 us; the launch traced here: 606 us
  local copies, waits for them, and re-layouts  184 us (30%)
  Pallas kernels  147 us (24%)
  waiting for transfers between devices  116 us (19%)
  other arithmetic  64 us (10%)
  matrix products  61.4 us (10%)
  starting transfers between devices  18.3 us (3%)
  between operations  14.9 us (2%)
    all_gather x2, waiting for transfers between devices, gather_rows(): every = lax.all_gather(payload, ('dp', 'seq'), axis=0, tiled=True)  105 us
    pallas_call x1, Pallas kernels, ring_reduce(): pl.pallas_call(functools.partial(ring_kernel, tuple(order), per_way), out...  71.1 us
    pallas_call x1, Pallas kernels, attn_bwd(): pl.pallas_call(attn_bwd_kernel, out_shape=(jax.ShapeDtypeStruct((count, w...  55.1 us
    unnamed x95, local copies, waits for them, and re-layouts  40.3 us
    dot_general x4, matrix products, apply_back(): jnp.einsum('tn,dnr->tdr', grad, weight_t, preferred_element_type=jnp.floa...  22.4 us
    transpose x4, local copies, waits for them, and re-layouts, grad_t(): jnp.einsum('tn,tdr->dnr', grad, front(left, n_dp), preferred_element_type...  21.3 us
    pallas_call x1, Pallas kernels, attn_fwd(): pl.pallas_call(attn_fwd_kernel, out_shape=jax.ShapeDtypeStruct((count, wi...  20.9 us
    dot_general x4, matrix products, apply_t(): jnp.einsum('tdr,dnr->tn', front(left, n_dp), weight_t, preferred_element_...  20 us
  transfers between devices with their start and end apart: 9, of which 3 were waited for; matrix products, arithmetic and copies ran while one was open for 20% of the time, Pallas kernels for 0%

profile of v6, /device:TPU:0, one launch (start us, length us, event | category | flops | bytes accessed | tf_op | source)
XLA Modules:
  0.0 605.8 jit_solution(16891439402315239216)
XLA Ops:
  11.2 4.2 concatenate.58
  16.2 4.8 collective-permute-start.2
  24.7 2.1 tile.6
  26.8 3.5 copy.34
  33.8 41.0 %all-gather.3.cloned.1.call-done = bf16[4864,384]{1,0:T(8,128)(2,1)} async-done(((bf16[152,384]{1,0:T(8,128)(2,1)}), bf16[4864,384]{1,0:T(8,128)(2,1)}) %all-gather.3.cloned.1.call-update) | async-done | bytes 3735568 | tf_op jit(solution)/shard_map/all_gather | solution.py:317
  74.8 4.1 slice.188
  79.0 5.8 copy.59
  84.8 63.6 %all-gather.5.cloned.1.call-done = bf16[8704,384]{1,0:T(8,128)(2,1)} async-done(((bf16[272,384]{1,0:T(8,128)(2,1)}), bf16[8704,384]{1,0:T(8,128)(2,1)}) %all-gather.5.cloned.1.call-update) | async-done | bytes 6684688 | tf_op jit(solution)/shard_map/all_gather | solution.py:317
  150.4 6.5 %convolution_bitcast_fusion.1 = f32[1024,2304]{1,0:T(8,128)S(1)} fusion(bf16[1024,2,384]{0,2,1:T(8,128)(2,1)S(1)} %bitcast.142, bf16[2,2304,384]{2,1,0:T(8,128)(2,1)} %bitcast.115), kind=kOutput, calls=%fused_computation.3 | convolution fusion | flops 3623878656 | bytes 14548992 | tf_op jit(solution)/shard_map/tdr,dnr->tn/dot_general | solution.py:332
  156.9 3.4 fusion.40
  160.3 2.3 copy-done.8
  163.9 2.9 slice.196
  166.7 2.4 copy.38
  171.0 2.4 copy.35
  175.3 2.4 maximum_multiply_fusion.1
  177.7 3.5 copy.39
  181.2 2.5 copy.36
  183.8 6.7 %add_convert_fusion.1 = (bf16[1024,768]{1,0:T(8,128)(2,1)S(1)}, bf16[1024,768]{1,0:T(8,128)(2,1)S(1)}) fusion(f32[1024,768]{1,0:T(8,128)} %copy.39, f32[1024,768]{1,0:T(8,128)} %copy.34, f32[1024,2304]{1,0:T(8,128)} %copy-done.8, f32[1024,768]{1,0:T(8,128)} %copy.36), kind=kLoop, calls=%fused_computation.59 | loop fusion | flops 4718592 | bytes 18874368 | tf_op jit(solution)/shard_map/convert_element_type | solution.py:381
  192.5 4.6 collective-permute-start
  197.1 4.8 reshape_reshape.6
  201.9 6.5 %fusion.26 = f32[2,576,1024]{2,1,0:T(8,128)} fusion(bf16[2,768,576]{2,1,0:T(8,128)(2,1)} %reshape_reshape.6, bf16[1024,768]{1,0:T(8,128)(2,1)} %param.23), kind=kOutput, calls=%fused_computation.74 | convolution fusion | flops 1811939328 | bytes 8060928 | tf_op jit(solution)/shard_map/tn,dnr->tdr/dot_general | solution.py:336
  208.4 2.4 slice.186
  210.8 4.1 slice.198
  214.9 6.1 %copy.48 = f32[1024,1152]{1,0:T(8,128)} copy(f32[1024,1152]{0,1:T(8,128)} %bitcast.131) | data formatting | bytes 9437184 | tf_op jit(solution)/shard_map/reshape | solution.py:337
  221.8 5.8 copy.50
  227.6 2.4 copy.51
  230.0 5.3 pad_maximum_fusion.1.kv_ref
  235.3 20.9 %shard_map.161 = bf16[1024,768]{1,0:T(8,128)(2,1)S(1)} custom-call(bf16[1024,768]{1,0:T(8,128)(2,1)S(1)} %get-tuple-element.63.q_ref, bf16[1152,1536]{1,0:T(8,128)(2,1)} %pad_maximum_fusion.1.kv_ref, s32[1024,1]{1,0:T(8,128)S(1)} %copy-done, s32[1,1152]{1,0:T(1,128)S(1)} %reshape.236.tk_ref), custom_call_target="tpu_custom_call" | custom-call | tf_op jit(solution)/shard_map/pallas_call | solution.py:287
  258.2 3.6 fusion.43
  262.7 2.3 copy-done.11
  265.0 3.9 convolution_bitcast_fusion
  269.0 11.1 %fusion.28 = (f32[1024,1152]{1,0:T(8,128)}, f32[1024,1152]{1,0:T(8,128)S(1)}) fusion(f32[1024,1152]{1,0:T(8,128)S(1)} %bitcast.107, f32[1024,2304]{1,0:T(8,128)S(1)} %convolution_bitcast_fusion), kind=kLoop, calls=%fused_computation.76 | loop fusion | flops 76677120 | bytes 18874368 | tf_op jit(solution)/shard_map/transpose(jvp())/mul | solution.py:80
  280.1 3.5 multiply_add_fusion
  283.7 7.6 %multiply_reduce_fusion = (f32[768]{0:T(1024)S(1)}, f32[1024]{0:T(1024)S(1)}, f32[1024]{0:T(1024)S(1)}, f32[1024,768]{0,1:T(8,128)S(1)}) fusion(f32[1024,768]{0,1:T(8,128)S(1)} %get-tuple-element.96, f32[1024]{0:T(1024)S(1)} %add_rsqrt_fusion, f32[1024]{0:T(1024)S(1)} %broadcast_multiply_fusion.4, f32[768]{0:T(1024)S(1)} %reshape.256, ...), kind=kOutput, calls=%fused_computation.52 | convolution fusion | flops 3634885888 | bytes 19290112 | tf_op jit(solution)/shard_map/tn,dnr->tdr/dot_general | solution.py:336
  294.1 55.1 %shard_map.162 = (f32[1024,768]{1,0:T(8,128)}, f32[1152,1536]{1,0:T(8,128)}) custom-call(bf16[1024,768]{1,0:T(8,128)(2,1)S(1)} %get-tuple-element.63.q_ref, bf16[1152,1536]{1,0:T(8,128)(2,1)} %pad_maximum_fusion.1.kv_ref, s32[1024,1]{1,0:T(8,128)S(1)} %copy-done.1, s32[1,1152]{1,0:T(1,128)S(1)} %reshape.236.tk_ref, ...), custom_call_target="tpu_custom_call" | custom-call | tf_op jit(solution)/shard_map/pallas_call | solution.py:299
  349.2 6.6 %slice.171 = f32[1024,1536]{1,0:T(8,128)} slice(f32[1152,1536]{1,0:T(8,128)} %get-tuple-element.35), slice={[64:1088], [0:1536]} | slice | bytes 12582912 | tf_op jit(solution)/shard_map/slice | solution.py:416
  355.8 2.2 convert.21
  359.2 2.8 convolution_bitcast_fusion.5
  362.0 5.9 convolution_bitcast_fusion.3
  367.9 4.4 copy.43
  374.2 4.9 collective-permute-start.4
  380.3 2.5 copy.54
  382.9 4.0 slice_negate_fusion.1
  390.6 8.0 %copy.63 = f32[2,2304,384]{2,1,0:T(8,128)} copy(f32[2,2304,384]{1,2,0:T(8,128)} %convolution_bitcast_fusion.3) | data formatting | bytes 14155776 | tf_op jit(solution)/shard_map/tn,tdr->dnr/transpose | solution.py:341
  398.6 4.1 convolution_bitcast_fusion.4
  402.7 3.2 copy.64
  405.9 5.7 reshape_reshape.7
  411.7 6.8 %constant_dynamic-update-slice_fusion.2 = f32[2,16,424,384]{3,2,1,0:T(8,128)} fusion(f32[2,16,424,384]{3,2,1,0:T(8,128)} %constant_dynamic-update-slice_fusion.3, f32[2,16,144,384]{3,2,1,0:T(8,128)} %bitcast.110), kind=kLoop, calls=%fused_computation.99 | loop fusion | bytes 14155776
  428.6 2.4 copy.57
  432.9 2.4 maximum_multiply_fusion.2
  435.3 2.3 copy.55
  437.6 3.7 copy.58
  441.3 6.1 %subtract_convert_fusion.1 = (bf16[1024,768]{1,0:T(8,128)(2,1)S(1)}, bf16[1024,768]{1,0:T(8,128)(2,1)S(1)}) fusion(f32[1024,768]{1,0:T(8,128)} %copy.55, f32[1024,768]{1,0:T(8,128)} %get-tuple-element.34, f32[1024,768]{1,0:T(8,128)S(1)} %copy-done.5, f32[1024,768]{1,0:T(8,128)} %copy.58, f32[1024,1536]{1,0:T(8,128)} %copy-done.4), kind=kLoop, calls=%fused_computation.54 | loop fusion | flops 4718592 | bytes 18874368 | tf_op jit(solution)/shard_map/convert.2
  447.5 6.2 %convolution_bitcast_fusion.2 = f32[2,2304,384]{1,2,0:T(8,128)} fusion(bf16[1024,2,384]{0,2,1:T(8,128)(2,1)S(1)} %bitcast.143, bf16[1024,768]{1,0:T(8,128)(2,1)S(1)} %copy-done.27, bf16[1024,768]{1,0:T(8,128)(2,1)S(1)} %get-tuple-element.69, bf16[1024,768]{1,0:T(8,128)(2,1)S(1)} %get-tuple-element.68), kind=kOutput, calls=%fused_computation.4 | convolution fusion | flops 3638034432 | bytes 13369344 | tf_op jit(solution)/shard_map/tn,tdr->dnr/dot_general | solution.py:341
  453.7 6.7 %fusion.20 = (f32[768]{0:T(1024)S(1)}, f32[1024]{0:T(1024)}, f32[1024]{0:T(1024)S(1)}, f32[1024,768]{0,1:T(8,128)}) fusion(bf16[1024,768]{0,1:T(8,128)(2,1)S(1)} %copy-done.3, f32[1024]{0:T(1024)S(1)} %copy-done.34, f32[1024]{0:T(1024)S(1)} %copy-done.30, f32[768]{0:T(1024)S(1)} %copy-done.32, bf16[768,2304]{1,0:T(8,128)(2,1)S(1)} %bitcast.136, ...), kind=kOutput, calls=%fused_computation.42 | convolution fusion | flops 3645109504 | bytes 12998656 | tf_op jit(solution)/shard_map/tn,dnr->tdr/dot_general | solution.py:336
  460.4 8.0 %copy.66 = f32[2,2304,384]{2,1,0:T(8,128)} copy(f32[2,2304,384]{1,2,0:T(8,128)} %convolution_bitcast_fusion.2) | data formatting | bytes 14155776 | tf_op jit(solution)/shard_map/tn,tdr->dnr/transpose | solution.py:341
  468.6 6.4 %constant_dynamic-update-slice_fusion = f32[2,16,424,384]{3,2,1,0:T(8,128)} fusion(f32[2,16,424,384]{3,2,1,0:T(8,128)} %broadcast_dynamic-update-slice_fusion.1, f32[2,16,144,384]{3,2,1,0:T(8,128)} %bitcast.111), kind=kLoop, calls=%fused_computation.97 | loop fusion | bytes 14155776
  475.8 15.7 %pad.36 = f32[2,16,448,384]{3,2,1,0:T(8,128)} pad(f32[2,16,424,384]{3,2,1,0:T(8,128)} %broadcast_dynamic-update-slice_fusion, f32[]{:T(128)} %constant.111.clone.1), padding=0_0x0_0x0_24x0_0 | pad | bytes 42860548 | tf_op jit(solution)/shard_map/jit(_pad)/pad | solution.py:449
  493.0 6.0 fusion.22
  499.0 2.8 copy.68
  501.8 7.3 %fusion.19 = f32[1024,768]{0,1:T(8,128)} fusion(f32[1024,768]{0,1:T(8,128)} %copy-done.13, bf16[1024,768]{0,1:T(8,128)(2,1)S(1)} %copy-done.3, f32[1024,768]{0,1:T(8,128)} %get-tuple-element.98, f32[1024]{0:T(1024)S(1)} %broadcast_multiply_fusion, f32[1024]{0:T(1024)S(1)} %broadcast_multiply_fusion.1, f32[768]{0:T(1024)S(1)} %copy-done.32, ...), kind=kLoop, calls=%fused_computation.41 | loop fusion | flops 7077888 | bytes 11029504 | tf_op jit(solution)/shard_map/add | solution.py:431
  509.1 4.2 copy.69
  513.3 11.6 %reduce-scatter.2.cloned.1.call-done = f32[1,7168,384]{2,1,0:T(8,128)} async-done(((f32[2,7168,384]{2,1,0:T(8,128)}), f32[1,7168,384]{2,1,0:T(8,128)}) %reduce-scatter.2.cloned.1.call-update) | async-done | bytes 11010064 | tf_op jit(solution)/shard_map/reduce_scatter | solution.py:451
  525.0 71.1 %shard_map.163 = f32[448,384]{1,0:T(8,128)S(1)} custom-call(f32[16,448,384]{2,1,0:T(8,128)} %bitcast.125), custom_call_target="tpu_custom_call" | custom-call | tf_op jit(solution)/shard_map/pallas_call | solution.py:194
  (164 shorter events, 52.5 us)
Async XLA Ops:
  7.2 67.7 %all-gather.3.cloned.1.call-start = ((), (), s32[]{:S(2)}) async-start(), calls=%async_computation.1 | async-start | bytes 3852288 | tf_op jit(solution)/shard_map/all_gather | solution.py:317
  9.5 138.9 %all-gather.5.cloned.1.call-start = ((), (), s32[]{:S(2)}) async-start(), calls=%async_computation.2 | async-start | bytes 6893568 | tf_op jit(solution)/shard_map/all_gather | solution.py:317
  15.4 509.6 %reduce-scatter.2.cloned.1.call-start = ((), (), s32[]{:S(2)}) async-start(), calls=%async_computation.3 | async-start | bytes 33030144 | tf_op jit(solution)/shard_map/reduce_scatter | solution.py:451
  16.2 17.5 %collective-permute-start.2 = (s32[64]{0:T(128)S(1)}, s32[64]{0:T(128)S(1)}, u32[]{:S(2)}, u32[]{:S(2)}) collective-permute-start(s32[64]{0:T(128)S(1)} %get-tuple-element.91), channel_id=1, source_target_pairs={{0,1},{1,2},{2,3},{3,4},{4,5},{5,6},{6,7},{7,8},{8,9},{9,10},{10,1... | collective-permute-start | bytes 776 | tf_op jit(solution)/shard_map/ppermute | solution.py:25
  21.0 12.7 %collective-permute-start.3 = (s32[64]{0:T(128)S(1)}, s32[64]{0:T(128)S(1)}, u32[]{:S(2)}, u32[]{:S(2)}) collective-permute-start(s32[64]{0:T(128)S(1)} %get-tuple-element.90), channel_id=1, source_target_pairs={{1,0},{2,1},{3,2},{4,3},{5,4},{6,5},{7,6},{8,7},{9,8},{10,9},{11,1... | collective-permute-start | bytes 776 | tf_op jit(solution)/shard_map/ppermute | solution.py:26
  24.1 125.8 %copy-start.2 = (bf16[1024,768]{0,1:T(8,128)(2,1)}, bf16[1024,768]{0,1:T(8,128)(2,1)S(1)}, u32[]{:S(2)}) copy-start(bf16[1024,768]{0,1:T(8,128)(2,1)S(1)} %copy.32) | copy-start | bytes 4718596
  24.7 149.2 %copy-start.20 = (f32[1024,64]{0,1:T(8,128)}, f32[1024,64]{0,1:T(8,128)S(1)}, u32[]{:S(2)}) copy-start(f32[1024,64]{0,1:T(8,128)S(1)} %get-tuple-element.102) | copy-start | bytes 786436
  30.3 1.8 copy-start.23
  30.6 119.3 %copy-start.29 = (f32[1024]{0:T(1024)}, f32[1024]{0:T(1024)S(1)}, u32[]{:S(2)}) copy-start(f32[1024]{0:T(1024)S(1)} %broadcast_multiply_fusion.5) | copy-start | bytes 12292
  31.0 118.8 %copy-start.33 = (f32[1024]{0:T(1024)}, f32[1024]{0:T(1024)S(1)}, u32[]{:S(2)}) copy-start(f32[1024]{0:T(1024)S(1)} %add_rsqrt_fusion.1) | copy-start | bytes 12292
  149.8 7.0 %copy-start.31 = (f32[768]{0:T(1024)}, f32[768]{0:T(1024)S(1)}, u32[]{:S(2)}) copy-start(f32[768]{0:T(1024)S(1)} %reshape.255) | copy-start | bytes 9220
  150.4 6.5 %copy-start.24 = (bf16[1024,768]{0,1:T(8,128)(2,1)}, bf16[1024,768]{0,1:T(8,128)(2,1)S(1)}, u32[]{:S(2)}) copy-start(bf16[1024,768]{0,1:T(8,128)(2,1)S(1)} %fusion.15) | copy-start | bytes 4718596
  156.9 5.6 copy-start.8
  173.4 1.4 copy-start.17
  173.4 1.9 copy-start.18
  183.8 6.7 %copy-start.10 = (bf16[1024,768]{1,0:T(8,128)(2,1)S(1)}, bf16[1024,768]{1,0:T(8,128)(2,1)}, u32[]{:S(2)}) copy-start(bf16[1024,768]{1,0:T(8,128)(2,1)} %slice.251) | copy-start | bytes 4718596
  191.2 38.7 %collective-permute-start.1 = (bf16[64,1536]{1,0:T(8,128)(2,1)}, bf16[64,1536]{1,0:T(8,128)(2,1)S(1)}, u32[]{:S(2)}, u32[]{:S(2)}) collective-permute-start(bf16[64,1536]{1,0:T(8,128)(2,1)} %get-tuple-element.75), channel_id=1, source_target_pairs={{1,0},{2,1},{3,2},{4,3},{5,4},{6,5},{7,6},{8,7},{9,8},{10,9},{11,1... | collective-permute-start | bytes 589832 | tf_op jit(solution)/shard_map/ppermute | solution.py:26
  192.5 37.5 %collective-permute-start = (bf16[64,1536]{1,0:T(8,128)(2,1)}, bf16[64,1536]{1,0:T(8,128)(2,1)S(1)}, u32[]{:S(2)}, u32[]{:S(2)}) collective-permute-start(bf16[64,1536]{1,0:T(8,128)(2,1)} %get-tuple-element.74), channel_id=1, source_target_pairs={{0,1},{1,2},{2,3},{3,4},{4,5},{5,6},{6,7},{7,8},{8,9},{9,10},{10,1... | collective-permute-start | bytes 589832 | tf_op jit(solution)/shard_map/ppermute | solution.py:25
  230.0 5.3 copy-start
  261.9 29.5 %copy-start.6 = (f32[1024,768]{0,1:T(8,128)}, f32[1024,768]{0,1:T(8,128)S(1)}, u32[]{:S(2)}) copy-start(f32[1024,768]{0,1:T(8,128)S(1)} %get-tuple-element.96) | copy-start | bytes 9437188
  262.3 2.7 copy-start.11
  262.3 6.6 %slice-start = ((s8[4718592]{0:T(1024)(128)(4,1)}), s8[4194304]{0:T(1024)(128)(4,1)S(1)}, s32[]{:S(2)}) async-start(s8[4718592]{0:T(1024)(128)(4,1)} %bitcast.106), calls=%async_computation.4 | async-start | bytes 8388608
  265.0 4.0 slice-start.1
  283.7 7.7 %copy-start.14 = (bf16[1024,768]{0,1:T(8,128)(2,1)S(1)}, bf16[1024,768]{0,1:T(8,128)(2,1)}, u32[]{:S(2)}) copy-start(bf16[1024,768]{0,1:T(8,128)(2,1)} %copy.46) | copy-start | bytes 4718596
  291.4 1.3 copy-start.28
  292.4 65.7 %copy-start.13 = (f32[1024,768]{0,1:T(8,128)}, f32[1024,768]{0,1:T(8,128)S(1)}, u32[]{:S(2)}) copy-start(f32[1024,768]{0,1:T(8,128)S(1)} %multiply_add_fusion.1) | copy-start | bytes 9437188
  292.6 1.5 copy-start.1
  349.2 6.6 %copy-start.7 = (f32[1152,1536]{1,0:T(8,128)S(1)}, f32[1152,1536]{1,0:T(8,128)}, u32[]{:S(2)}) copy-start(f32[1152,1536]{1,0:T(8,128)} %get-tuple-element.35) | copy-start | bytes 21233668
  349.2 12.8 %slice-start.4 = ((s8[4718592]{0:T(1024)(128)(4,1)}), s8[4194304]{0:T(1024)(128)(4,1)S(1)}, s32[]{:S(2)}) async-start(s8[4718592]{0:T(1024)(128)(4,1)} %bitcast.134), calls=%async_computation.8 | async-start | bytes 8388608
  355.8 3.4 copy-start.26
  355.8 6.2 %slice-start.5 = ((s8[4718592]{0:T(1024)(128)(4,1)}), s8[524288]{0:T(1024)(128)(4,1)S(1)}, s32[]{:S(2)}) async-start(s8[4718592]{0:T(1024)(128)(4,1)} %bitcast.134), calls=%async_computation.9 | async-start | bytes 1048576
  367.9 12.4 %copy-start.12 = (f32[1024,768]{1,0:T(8,128)S(1)}, f32[1024,768]{1,0:T(8,128)}, u32[]{:S(2)}) copy-start(f32[1024,768]{1,0:T(8,128)} %get-tuple-element.34) | copy-start | bytes 9437188
  374.2 47.2 %collective-permute-start.4 = (bf16[64,1536]{1,0:T(8,128)(2,1)}, bf16[64,1536]{1,0:T(8,128)(2,1)}, u32[]{:S(2)}, u32[]{:S(2)}) collective-permute-start(bf16[64,1536]{1,0:T(8,128)(2,1)} %get-tuple-element.67), channel_id=1, source_target_pairs={{0,1},{1,2},{2,3},{3,4},{4,5},{5,6},{6,7},{7,8},{8,9},{9,10},{10,1... | collective-permute-start | bytes 589832 | tf_op jit(solution)/shard_map/ppermute | solution.py:34
  379.1 43.5 %collective-permute-start.5 = (bf16[64,1536]{1,0:T(8,128)(2,1)}, bf16[64,1536]{1,0:T(8,128)(2,1)}, u32[]{:S(2)}, u32[]{:S(2)}) collective-permute-start(bf16[64,1536]{1,0:T(8,128)(2,1)} %get-tuple-element.66), channel_id=1, source_target_pairs={{1,0},{2,1},{3,2},{4,3},{5,4},{6,5},{7,6},{8,7},{9,8},{10,9},{11,1... | collective-permute-start | bytes 589832 | tf_op jit(solution)/shard_map/ppermute | solution.py:34
  405.9 15.5 %slice-start.2 = ((s8[6291456]{0:T(1024)(128)(4,1)}), s8[2097152]{0:T(1024)(128)(4,1)S(1)}, s32[]{:S(2)}) async-start(s8[6291456]{0:T(1024)(128)(4,1)} %bitcast.108), calls=%async_computation.6 | async-start | bytes 4194304
  411.7 6.8 %copy-start.9 = (f32[2,16,72,384]{3,2,1,0:T(8,128)S(1)}, f32[2,16,72,384]{3,2,1,0:T(8,128)}, u32[]{:S(2)}) copy-start(f32[2,16,72,384]{3,2,1,0:T(8,128)} %reshape_reshape.7) | copy-start | bytes 10616836
  411.7 9.7 %slice-start.3 = ((s8[6291456]{0:T(1024)(128)(4,1)}), s8[4194304]{0:T(1024)(128)(4,1)S(1)}, s32[]{:S(2)}) async-start(s8[6291456]{0:T(1024)(128)(4,1)} %bitcast.108), calls=%async_computation.7 | async-start | bytes 8388608
  423.6 3.1 copy-start.4
  431.0 1.4 copy-start.15
  431.0 1.9 copy-start.16
  431.0 1.9 copy-start.21
  437.6 3.7 copy-start.5
  441.3 6.1 %copy-start.25 = (bf16[1024,768]{0,1:T(8,128)(2,1)S(1)}, bf16[1024,768]{0,1:T(8,128)(2,1)}, u32[]{:S(2)}) copy-start(bf16[1024,768]{0,1:T(8,128)(2,1)} %copy-done.24) | copy-start | bytes 4718596
  441.3 6.1 %copy-start.27 = (bf16[1024,768]{1,0:T(8,128)(2,1)S(1)}, bf16[1024,768]{1,0:T(8,128)(2,1)}, u32[]{:S(2)}) copy-start(bf16[1024,768]{1,0:T(8,128)(2,1)} %slice.250) | copy-start | bytes 4718596
  447.5 6.2 %copy-start.3 = (bf16[1024,768]{0,1:T(8,128)(2,1)S(1)}, bf16[1024,768]{0,1:T(8,128)(2,1)}, u32[]{:S(2)}) copy-start(bf16[1024,768]{0,1:T(8,128)(2,1)} %copy-done.2) | copy-start | bytes 4718596
  447.5 6.2 %copy-start.19 = (bf16[2,384,2304]{2,1,0:T(8,128)(2,1)S(1)}, bf16[2,384,2304]{2,1,0:T(8,128)(2,1)}, u32[]{:S(2)}) copy-start(bf16[2,384,2304]{2,1,0:T(8,128)(2,1)} %copy.59) | copy-start | bytes 10616836
  447.5 6.2 %copy-start.30 = (f32[1024]{0:T(1024)S(1)}, f32[1024]{0:T(1024)}, u32[]{:S(2)}) copy-start(f32[1024]{0:T(1024)} %copy-done.29) | copy-start | bytes 12292
  447.5 6.2 %copy-start.32 = (f32[768]{0:T(1024)S(1)}, f32[768]{0:T(1024)}, u32[]{:S(2)}) copy-start(f32[768]{0:T(1024)} %copy-done.31) | copy-start | bytes 9220
  447.5 6.2 %copy-start.34 = (f32[1024]{0:T(1024)S(1)}, f32[1024]{0:T(1024)}, u32[]{:S(2)}) copy-start(f32[1024]{0:T(1024)} %copy-done.33) | copy-start | bytes 12292
  491.5 1.5 copy-start.22
  499.0 2.8 copy-start.35
Sparse Core Ops, SparseCore 0:
  11.4 63.3 all-gather.2
  78.3 69.9 all-gather.4
  491.6 33.3 reduce-scatter.1

commit v7 on v6

--- a/solution.py
+++ b/solution.py
@@ -318,10 +318,10 @@
     return every.reshape(n_dp, n_seq, payload.shape[0], payload.shape[1])
 
 
-def gain_blocks(grad_gain, n_dp, n_seq, width):
+def gain_blocks(grad_gain, n_dp, n_seq, width, height=8):
     part = jnp.pad(grad_gain.reshape(n_seq, -1), ((0, 0), (0, width - grad_gain.shape[0] // n_seq)))
-    rows = jnp.concatenate([part[:, None], jnp.zeros((n_seq, 7, width), part.dtype)], 1)
-    return jnp.broadcast_to(rows[None], (n_dp, n_seq, 8, width))
+    rows = jnp.concatenate([part[:, None], jnp.zeros((n_seq, height - 1, width), part.dtype)], 1)
+    return jnp.broadcast_to(rows[None], (n_dp, n_seq, height, width))
 
 
 def front(value, n_dp):
@@ -358,18 +358,6 @@
     )
     full_qkv = first[:, :, :qkv_cols].reshape(n_dp, n_seq * qkv_cols, rows)
     gain_one = first[0, :, qkv_cols, : gain_attn.shape[0]].reshape(-1).astype(jnp.float32)
-    at = 0
-    full_out = second[:, :, at : at + out_cols].reshape(n_dp, n_seq * out_cols, rows)
-    at += out_cols
-    full_in = second[:, :, at : at + in_cols].reshape(n_dp, n_seq * in_cols, rows)
-    at += in_cols
-    full_down = (
-        second[:, :, at : at + down_lines]
-        .reshape(n_dp, n_seq, down_cols, down_rows)
-        .reshape(n_dp, n_seq * down_cols, down_rows)
-    )
-    at += down_lines
-    gain_two = second[0, :, at, : gain_mlp.shape[0]].reshape(-1).astype(jnp.float32)
     stream = tokens.astype(jnp.float32)
     normed_a, factor_a = layer_norm(stream)
     h_attn = (normed_a * gain_one).astype(jnp.bfloat16)
@@ -388,6 +376,19 @@
         padded(tag_key, ((("dp", "seq"), 0),), HALF),
     )
     attn_out = attn_fwd(query, wide_kv, tag_query, wide_tag)
+    attn_out, second = lax.optimization_barrier((attn_out, second))
+    at = 0
+    full_out = second[:, :, at : at + out_cols].reshape(n_dp, n_seq * out_cols, rows)
+    at += out_cols
+    full_in = second[:, :, at : at + in_cols].reshape(n_dp, n_seq * in_cols, rows)
+    at += in_cols
+    full_down = (
+        second[:, :, at : at + down_lines]
+        .reshape(n_dp, n_seq, down_cols, down_rows)
+        .reshape(n_dp, n_seq * down_cols, down_rows)
+    )
+    at += down_lines
+    gain_two = second[0, :, at, : gain_mlp.shape[0]].reshape(-1).astype(jnp.float32)
     mid = stream + apply_t(attn_out, full_out, n_dp)
     normed_m, factor_m = layer_norm(mid)
     h_mlp = (normed_m * gain_two).astype(jnp.bfloat16)
@@ -429,6 +430,8 @@
     grad_hattn = apply_back(grad_qkv, full_qkv)
     grad_gain_one = jnp.sum(grad_hattn * normed_a, axis=0)
     grad_tokens = grad_mid + norm_back(grad_hattn * gain_one, normed_a, factor_a)
+    height = out_cols + in_cols + down_lines + qkv_cols + 16
+    tail = 8 + (-height) % (2 * RING_WAYS * 16)
     blocks = jnp.concatenate(
         [
             grad_outw.reshape(n_dp, n_seq, out_cols, rows),
@@ -438,15 +441,10 @@
             ),
             gain_blocks(grad_gain_two, n_dp, n_seq, rows),
             grad_qkvw.reshape(n_dp, n_seq, qkv_cols, rows),
-            gain_blocks(grad_gain_one, n_dp, n_seq, rows),
+            gain_blocks(grad_gain_one, n_dp, n_seq, rows, tail),
         ],
         2,
     )
-    height = blocks.shape[2]
-    lanes_rows = 2 * RING_WAYS * 16
-    extra = (-height) % lanes_rows
-    if extra:
-        blocks = jnp.pad(blocks, ((0, 0), (0, 0), (0, extra), (0, 0)))
     depth = blocks.shape[2]
     half = lax.psum_scatter(
         blocks.reshape(n_dp, n_seq * depth, rows), "dp", scatter_dimension=0, tiled=True

time: 616 us -> 573 us (0.930)
  waiting for transfers between devices: 116 us -> 67.1 us
  other arithmetic: 64 us -> 71.3 us
  local copies, waits for them, and re-layouts: 184 us -> 177 us
    all_gather x2, waiting for transfers between devices: 105 us -> 50.7 us  [gather_rows(): every = lax.all_gather(payload, ('dp', 'seq'), axis=0, tiled=True)]
    pad x1 -> x0, local copies, waits for them, and re-layouts: 15.7 us -> none  [on_device(): blocks = jnp.pad(blocks, ((0, 0), (0, 0), (0, extra), (0, 0)))]
    unnamed x95 -> x85, local copies, waits for them, and re-layouts: 40.3 us -> 37.1 us
  transfers between devices with their start and end apart: 9 -> 9, of which waited for: 3 -> 4; matrix products, arithmetic and copies ran while one was open for 20% -> 25% of each run, Pallas kernels for 0% -> 4%
where the time goes in v7:
time: 573 us; the launch traced here: 562 us
  local copies, waits for them, and re-layouts  177 us (31%)
  Pallas kernels  147 us (26%)
  other arithmetic  71.3 us (12%)
  waiting for transfers between devices  67.1 us (12%)
  matrix products  66.2 us (12%)
  starting transfers between devices  18.6 us (3%)
  between operations  14.8 us (3%)
    pallas_call x1, Pallas kernels, ring_reduce(): pl.pallas_call(functools.partial(ring_kernel, tuple(order), per_way), out...  71.1 us
    pallas_call x1, Pallas kernels, attn_bwd(): pl.pallas_call(attn_bwd_kernel, out_shape=(jax.ShapeDtypeStruct((count, w...  55.1 us
    all_gather x2, waiting for transfers between devices, gather_rows(): every = lax.all_gather(payload, ('dp', 'seq'), axis=0, tiled=True)  50.7 us
    unnamed x85, local copies, waits for them, and re-layouts  37.1 us
    dot_general x4, matrix products, apply_back(): jnp.einsum('tn,dnr->tdr', grad, weight_t, preferred_element_type=jnp.floa...  25.9 us
    transpose x4, local copies, waits for them, and re-layouts, grad_t(): jnp.einsum('tn,tdr->dnr', grad, front(left, n_dp), preferred_element_type...  24.4 us
    pallas_call x1, Pallas kernels, attn_fwd(): pl.pallas_call(attn_fwd_kernel, out_shape=jax.ShapeDtypeStruct((count, wi...  20.9 us
    dot_general x4, matrix products, grad_t(): jnp.einsum('tn,tdr->dnr', grad, front(left, n_dp), preferred_element_type...  20.9 us
  transfers between devices with their start and end apart: 9, of which 4 were waited for; matrix products, arithmetic and copies ran while one was open for 25% of the time, Pallas kernels for 4%

profile of v7, /device:TPU:0, one launch (start us, length us, event | category | flops | bytes accessed | tf_op | source)
XLA Modules:
  0.0 562.0 jit_solution(8556700548319479778)
XLA Ops:
  11.2 4.2 concatenate.58
  19.9 3.5 copy.34
  24.2 50.7 %all-gather.3.cloned.1.call-done = bf16[4864,384]{1,0:T(8,128)(2,1)} async-done(((bf16[152,384]{1,0:T(8,128)(2,1)}), bf16[4864,384]{1,0:T(8,128)(2,1)}) %all-gather.3.cloned.1.call-update) | async-done | bytes 3735568 | tf_op jit(solution)/shard_map/all_gather | solution.py:317
  74.8 4.1 slice.187
  80.4 6.5 %convolution_bitcast_fusion.1 = f32[1024,2304]{1,0:T(8,128)S(1)} fusion(bf16[1024,2,384]{0,2,1:T(8,128)(2,1)S(1)} %bitcast.142, bf16[2,2304,384]{2,1,0:T(8,128)(2,1)} %bitcast.110), kind=kOutput, calls=%fused_computation.3 | convolution fusion | flops 3623878656 | bytes 14548992 | tf_op jit(solution)/shard_map/tdr,dnr->tn/dot_general | solution.py:332
  88.3 3.7 fusion.39
  95.4 3.5 copy.35
  98.9 2.7 slice_negate_fusion.2
  101.6 2.5 maximum_multiply_fusion.1
  104.1 3.6 copy.39
  110.0 6.7 %add_convert_fusion.1 = (bf16[1024,768]{1,0:T(8,128)(2,1)S(1)}, bf16[1024,768]{1,0:T(8,128)(2,1)S(1)}) fusion(f32[1024,768]{1,0:T(8,128)} %copy.39, f32[1024,768]{1,0:T(8,128)} %copy.34, f32[1024,2304]{1,0:T(8,128)} %copy-done.6, f32[1024,768]{1,0:T(8,128)} %copy.36), kind=kLoop, calls=%fused_computation.59 | loop fusion | flops 4718592 | bytes 18874368 | tf_op jit(solution)/shard_map/convert_element_type | solution.py:369
  119.0 5.0 collective-permute-start
  124.1 3.5 collective-permute-start.2
  129.9 2.6 copy.46
  132.5 2.5 collective-permute-done.2
  137.2 5.8 %copy.59 = bf16[2,384,2304]{2,1,0:T(8,128)(2,1)} copy(bf16[2,384,2304]{1,2,0:T(8,128)(2,1)} %bitcast.111) | data formatting | bytes 7077888 | tf_op jit(solution)/shard_map/tn,dnr->tdr/dot_general | solution.py:336
  143.0 3.5 pad_maximum_fusion.1.kv_ref
  146.6 20.9 %shard_map.161 = bf16[1024,768]{1,0:T(8,128)(2,1)S(1)} custom-call(bf16[1024,768]{1,0:T(8,128)(2,1)S(1)} %get-tuple-element.67.q_ref, bf16[1152,1536]{1,0:T(8,128)(2,1)} %pad_maximum_fusion.1.kv_ref, s32[1024,1]{1,0:T(8,128)S(1)} %copy-done, s32[1,1152]{1,0:T(1,128)S(1)} %reshape.236.tk_ref), custom_call_target="tpu_custom_call" | custom-call | tf_op jit(solution)/shard_map/pallas_call | solution.py:287
  167.5 2.4 slice.163
  169.9 2.9 slice.168
  173.6 4.2 slice.165
  179.4 4.9 reshape_reshape.6
  184.3 6.1 %fusion.26 = f32[2,576,1024]{2,1,0:T(8,128)} fusion(bf16[2,768,576]{2,1,0:T(8,128)(2,1)} %reshape_reshape.6, bf16[1024,768]{1,0:T(8,128)(2,1)S(1)} %copy-done.14), kind=kOutput, calls=%fused_computation.74 | convolution fusion | flops 1811939328 | bytes 8060928 | tf_op jit(solution)/shard_map/tn,dnr->tdr/dot_general | solution.py:336
  190.4 6.6 %copy.48 = f32[1024,1152]{1,0:T(8,128)} copy(f32[1024,1152]{0,1:T(8,128)} %bitcast.131) | data formatting | bytes 9437184 | tf_op jit(solution)/shard_map/reshape | solution.py:337
  197.0 3.2 fusion.42
  203.9 3.9 convolution_bitcast_fusion
  207.8 11.1 %fusion.28 = (f32[1024,1152]{1,0:T(8,128)}, f32[1024,1152]{1,0:T(8,128)S(1)}) fusion(f32[1024,1152]{1,0:T(8,128)S(1)} %bitcast.106, f32[1024,2304]{1,0:T(8,128)S(1)} %convolution_bitcast_fusion), kind=kLoop, calls=%fused_computation.76 | loop fusion | flops 76677120 | bytes 18874368 | tf_op jit(solution)/shard_map/transpose(jvp())/mul | solution.py:80
  219.0 4.3 multiply_add_fusion
  223.3 5.8 %copy.50 = bf16[2,384,2304]{2,1,0:T(8,128)(2,1)} copy(bf16[2,384,2304]{1,2,0:T(8,128)(2,1)} %bitcast.112) | data formatting | bytes 7077888 | tf_op jit(solution)/shard_map/tn,dnr->tdr/dot_general | solution.py:336
  229.1 11.5 %multiply_reduce_fusion = (f32[768]{0:T(1024)S(1)}, f32[1024]{0:T(1024)S(1)}, f32[1024]{0:T(1024)S(1)}, f32[1024,768]{0,1:T(8,128)}) fusion(f32[1024,768]{0,1:T(8,128)} %copy-done.4, f32[1024]{0:T(1024)S(1)} %add_rsqrt_fusion, f32[1024]{0:T(1024)S(1)} %broadcast_multiply_fusion.4, f32[768]{0:T(1024)S(1)} %reshape.256, bf16[768,2304]{1,0:T(8,128)(2,1)} %bitcast.137, ...), kind=kOutput, calls=%fused_computation.52 | convolution fusion | flops 3634885888 | bytes 19290112 | tf_op jit(solution)/shard_map/tn,dnr->tdr/dot_general | solution.py:336
  240.7 2.6 copy.51
  243.2 4.4 multiply_add_fusion.1
  249.1 55.1 %shard_map.162 = (f32[1024,768]{1,0:T(8,128)}, f32[1152,1536]{1,0:T(8,128)}) custom-call(bf16[1024,768]{1,0:T(8,128)(2,1)S(1)} %get-tuple-element.67.q_ref, bf16[1152,1536]{1,0:T(8,128)(2,1)} %pad_maximum_fusion.1.kv_ref, s32[1024,1]{1,0:T(8,128)S(1)} %copy-done.1, s32[1,1152]{1,0:T(1,128)S(1)} %reshape.236.tk_ref, ...), custom_call_target="tpu_custom_call" | custom-call | tf_op jit(solution)/shard_map/pallas_call | solution.py:299
  304.2 6.6 %slice.171 = f32[1024,1536]{1,0:T(8,128)} slice(f32[1152,1536]{1,0:T(8,128)} %get-tuple-element.39), slice={[64:1088], [0:1536]} | slice | bytes 12582912 | tf_op jit(solution)/shard_map/slice | solution.py:417
  314.3 2.8 convolution_bitcast_fusion.5
  317.2 5.9 %convolution_bitcast_fusion.3 = f32[2,2304,384]{1,2,0:T(8,128)} fusion(bf16[1024,2,384]{0,2,1:T(8,128)(2,1)S(1)} %bitcast.147, f32[1024,1152]{1,0:T(8,128)S(1)} %bitcast.130, f32[1024,1152]{1,0:T(8,128)S(1)} %bitcast.135), kind=kOutput, calls=%fused_computation.5 | convolution fusion | flops 3628597248 | bytes 18087936 | tf_op jit(solution)/shard_map/tn,tdr->dnr/dot_general | solution.py:341
  323.1 4.3 copy.43
  329.2 5.9 %collective-permute-start.4 = (bf16[64,1536]{1,0:T(8,128)(2,1)}, bf16[64,1536]{1,0:T(8,128)(2,1)}, u32[]{:S(2)}, u32[]{:S(2)}) collective-permute-start(bf16[64,1536]{1,0:T(8,128)(2,1)} %get-tuple-element.71), channel_id=1, source_target_pairs={{0,1},{1,2},{2,3},{3,4},{4,5},{5,6},{6,7},{7,8},{8,9},{9,10},{10,1... | collective-permute-start | bytes 589832 | tf_op jit(solution)/shard_map/ppermute | solution.py:34
  336.3 3.7 copy.54
  340.1 3.4 slice_negate_fusion.1
  343.5 3.1 copy.62
  346.5 3.2 constant_dynamic-update-slice_fusion.3
  349.8 8.0 %copy.63 = f32[2,2304,384]{2,1,0:T(8,128)} copy(f32[2,2304,384]{1,2,0:T(8,128)} %convolution_bitcast_fusion.3) | data formatting | bytes 14155776 | tf_op jit(solution)/shard_map/tn,tdr->dnr/transpose | solution.py:341
  357.8 5.9 %convolution_bitcast_fusion.4 = f32[2,768,576]{1,2,0:T(8,128)} fusion(bf16[1024,2,576]{0,2,1:T(8,128)(2,1)} %bitcast.140, bf16[1024,768]{1,0:T(8,128)(2,1)} %param.23), kind=kOutput, calls=%fused_computation.64 | convolution fusion | flops 1811939328 | bytes 7471104 | tf_op jit(solution)/shard_map/tn,tdr->dnr/dot_general | solution.py:341
  363.7 5.3 copy.64
  369.0 5.5 reshape_reshape.7
  374.7 6.5 %constant_dynamic-update-slice_fusion.2 = f32[2,16,448,384]{3,2,1,0:T(8,128)} fusion(f32[2,16,448,384]{3,2,1,0:T(8,128)} %constant_dynamic-update-slice_fusion.3, f32[2,16,144,384]{3,2,1,0:T(8,128)} %bitcast.107), kind=kLoop, calls=%fused_computation.99 | loop fusion | bytes 14155776
  387.9 3.2 slice.244
  391.1 3.7 slice.202
  394.8 3.6 copy.57
  400.8 3.4 maximum_multiply_fusion.2
  404.2 3.5 copy.55
  407.8 3.6 copy.58
  411.4 7.0 %subtract_convert_fusion.1 = (bf16[1024,768]{1,0:T(8,128)(2,1)S(1)}, bf16[1024,768]{1,0:T(8,128)(2,1)S(1)}) fusion(f32[1024,768]{1,0:T(8,128)} %copy.55, f32[1024,768]{1,0:T(8,128)} %get-tuple-element.38, f32[1024,768]{1,0:T(8,128)} %copy.34, f32[1024,768]{1,0:T(8,128)} %copy.58, f32[1024,1536]{1,0:T(8,128)} %fusion.32), kind=kLoop, calls=%fused_computation.54 | loop fusion | flops 4718592 | bytes 18874368 | tf_op jit(solution)/shard_map/convert.2
  418.5 6.2 %convolution_bitcast_fusion.2 = f32[2,2304,384]{1,2,0:T(8,128)} fusion(bf16[1024,2,384]{0,2,1:T(8,128)(2,1)S(1)} %bitcast.143, bf16[1024,768]{1,0:T(8,128)(2,1)S(1)} %copy-done.18, bf16[1024,768]{1,0:T(8,128)(2,1)S(1)} %get-tuple-element.73, bf16[1024,768]{1,0:T(8,128)(2,1)S(1)} %get-tuple-element.72), kind=kOutput, calls=%fused_computation.4 | convolution fusion | flops 3638034432 | bytes 13369344 | tf_op jit(solution)/shard_map/tn,tdr->dnr/dot_general | solution.py:341
  424.7 6.8 %fusion.20 = (f32[768]{0:T(1024)S(1)}, f32[1024]{0:T(1024)}, f32[1024]{0:T(1024)S(1)}, f32[1024,768]{0,1:T(8,128)}) fusion(bf16[1024,768]{0,1:T(8,128)(2,1)S(1)} %copy-done.3, f32[1024]{0:T(1024)S(1)} %copy-done.27, f32[1024]{0:T(1024)S(1)} %copy-done.23, f32[768]{0:T(1024)S(1)} %copy-done.25, bf16[768,2304]{1,0:T(8,128)(2,1)S(1)} %bitcast.136, ...), kind=kOutput, calls=%fused_computation.42 | convolution fusion | flops 3645109504 | bytes 12998656 | tf_op jit(solution)/shard_map/tn,dnr->tdr/dot_general | solution.py:336
  431.5 8.0 %copy.66 = f32[2,2304,384]{2,1,0:T(8,128)} copy(f32[2,2304,384]{1,2,0:T(8,128)} %convolution_bitcast_fusion.2) | data formatting | bytes 14155776 | tf_op jit(solution)/shard_map/tn,tdr->dnr/transpose | solution.py:341
  439.7 6.4 %constant_dynamic-update-slice_fusion = f32[2,16,448,384]{3,2,1,0:T(8,128)} fusion(f32[2,16,448,384]{3,2,1,0:T(8,128)} %broadcast_dynamic-update-slice_fusion.1, f32[2,16,144,384]{3,2,1,0:T(8,128)} %bitcast.108), kind=kLoop, calls=%fused_computation.97 | loop fusion | bytes 14155776
  449.0 5.9 %fusion.22 = bf16[1024,768]{0,1:T(8,128)(2,1)} fusion(f32[1024,768]{0,1:T(8,128)} %copy-done.4, bf16[2,768,576]{2,1,0:T(8,128)(2,1)S(1)} %copy-done.13, bf16[1024,2,576]{0,2,1:T(8,128)(2,1)} %bitcast.141), kind=kOutput, calls=%fused_computation.51 | convolution fusion | flops 1813512192 | bytes 8847360 | tf_op jit(solution)/shard_map/tdr,dnr->tn/dot_general | solution.py:332
  455.0 2.8 copy.68
  457.8 7.4 %fusion.19 = f32[1024,768]{0,1:T(8,128)} fusion(f32[1024,768]{0,1:T(8,128)} %copy-done.10, bf16[1024,768]{0,1:T(8,128)(2,1)S(1)} %copy-done.3, f32[1024,768]{0,1:T(8,128)} %get-tuple-element.102, f32[1024]{0:T(1024)S(1)} %broadcast_multiply_fusion, f32[1024]{0:T(1024)S(1)} %broadcast_multiply_fusion.1, f32[768]{0:T(1024)S(1)} %copy-done.25, ...), kind=kLoop, calls=%fused_computation.41 | loop fusion | flops 7077888 | bytes 11029504 | tf_op jit(solution)/shard_map/add | solution.py:432
  465.2 4.2 copy.69
  469.5 11.8 %reduce-scatter.2.cloned.1.call-done = f32[1,7168,384]{2,1,0:T(8,128)} async-done(((f32[2,7168,384]{2,1,0:T(8,128)}), f32[1,7168,384]{2,1,0:T(8,128)}) %reduce-scatter.2.cloned.1.call-update) | async-done | bytes 11010064 | tf_op jit(solution)/shard_map/reduce_scatter | solution.py:449
  481.2 71.1 %shard_map.163 = f32[448,384]{1,0:T(8,128)S(1)} custom-call(f32[16,448,384]{2,1,0:T(8,128)} %bitcast.123), custom_call_target="tpu_custom_call" | custom-call | tf_op jit(solution)/shard_map/pallas_call | solution.py:194
  (153 shorter events, 53.7 us)
Async XLA Ops:
  7.2 10.0 %copy-start.29 = (s32[1024]{0:T(1024)S(1)}, s32[1024]{0:T(1024)}, u32[]{:S(2)}) copy-start(s32[1024]{0:T(1024)} %param.16) | copy-start | bytes 12292
  7.2 10.0 %copy-start.30 = (s32[1024]{0:T(1024)S(1)}, s32[1024]{0:T(1024)}, u32[]{:S(2)}) copy-start(s32[1024]{0:T(1024)} %param.15) | copy-start | bytes 12292
  7.2 67.7 %all-gather.3.cloned.1.call-start = ((), (), s32[]{:S(2)}) async-start(), calls=%async_computation.1 | async-start | bytes 3852288 | tf_op jit(solution)/shard_map/all_gather | solution.py:317
  9.5 158.0 %all-gather.5.cloned.1.call-start = ((), (), s32[]{:S(2)}) async-start(), calls=%async_computation.2 | async-start | bytes 6893568 | tf_op jit(solution)/shard_map/all_gather | solution.py:317
  15.4 465.8 %reduce-scatter.2.cloned.1.call-start = ((), (), s32[]{:S(2)}) async-start(), calls=%async_computation.3 | async-start | bytes 33030144 | tf_op jit(solution)/shard_map/reduce_scatter | solution.py:449
  17.2 62.7 %copy-start.2 = (bf16[1024,768]{0,1:T(8,128)(2,1)}, bf16[1024,768]{0,1:T(8,128)(2,1)S(1)}, u32[]{:S(2)}) copy-start(bf16[1024,768]{0,1:T(8,128)(2,1)S(1)} %copy.32) | copy-start | bytes 4718596
  23.7 56.1 %copy-start.22 = (f32[1024]{0:T(1024)}, f32[1024]{0:T(1024)S(1)}, u32[]{:S(2)}) copy-start(f32[1024]{0:T(1024)S(1)} %broadcast_multiply_fusion.5) | copy-start | bytes 12292
  24.2 55.7 %copy-start.26 = (f32[1024]{0:T(1024)}, f32[1024]{0:T(1024)S(1)}, u32[]{:S(2)}) copy-start(f32[1024]{0:T(1024)S(1)} %add_rsqrt_fusion.1) | copy-start | bytes 12292
  79.8 7.0 %copy-start.24 = (f32[768]{0:T(1024)}, f32[768]{0:T(1024)S(1)}, u32[]{:S(2)}) copy-start(f32[768]{0:T(1024)S(1)} %reshape.255) | copy-start | bytes 9220
  80.3 6.5 %copy-start.15 = (bf16[1024,768]{0,1:T(8,128)(2,1)}, bf16[1024,768]{0,1:T(8,128)(2,1)S(1)}, u32[]{:S(2)}) copy-start(bf16[1024,768]{0,1:T(8,128)(2,1)S(1)} %fusion.15) | copy-start | bytes 4718596
  86.9 6.1 %copy-start.6 = (f32[1024,2304]{1,0:T(8,128)}, f32[1024,2304]{1,0:T(8,128)S(1)}, u32[]{:S(2)}) copy-start(f32[1024,2304]{1,0:T(8,128)S(1)} %convolution_bitcast_fusion.1) | copy-start | bytes 28311556
  110.0 6.7 %copy-start.8 = (bf16[1024,768]{1,0:T(8,128)(2,1)S(1)}, bf16[1024,768]{1,0:T(8,128)(2,1)}, u32[]{:S(2)}) copy-start(bf16[1024,768]{1,0:T(8,128)(2,1)} %slice.245) | copy-start | bytes 4718596
  117.5 25.5 %collective-permute-start.1 = (bf16[64,1536]{1,0:T(8,128)(2,1)}, bf16[64,1536]{1,0:T(8,128)(2,1)}, u32[]{:S(2)}, u32[]{:S(2)}) collective-permute-start(bf16[64,1536]{1,0:T(8,128)(2,1)} %get-tuple-element.79), channel_id=1, source_target_pairs={{1,0},{2,1},{3,2},{4,3},{5,4},{6,5},{7,6},{8,7},{9,8},{10,9},{11,1... | collective-permute-start | bytes 589832 | tf_op jit(solution)/shard_map/ppermute | solution.py:26
  119.0 24.1 %collective-permute-start = (bf16[64,1536]{1,0:T(8,128)(2,1)}, bf16[64,1536]{1,0:T(8,128)(2,1)}, u32[]{:S(2)}, u32[]{:S(2)}) collective-permute-start(bf16[64,1536]{1,0:T(8,128)(2,1)} %get-tuple-element.78), channel_id=1, source_target_pairs={{0,1},{1,2},{2,3},{3,4},{4,5},{5,6},{6,7},{7,8},{8,9},{9,10},{10,1... | collective-permute-start | bytes 589832 | tf_op jit(solution)/shard_map/ppermute | solution.py:25
  124.1 10.9 %collective-permute-start.2 = (s32[64]{0:T(128)S(1)}, s32[64]{0:T(128)S(1)}, u32[]{:S(2)}, u32[]{:S(2)}) collective-permute-start(s32[64]{0:T(128)S(1)} %get-tuple-element.95), channel_id=1, source_target_pairs={{0,1},{1,2},{2,3},{3,4},{4,5},{5,6},{6,7},{7,8},{8,9},{9,10},{10,1... | collective-permute-start | bytes 776 | tf_op jit(solution)/shard_map/ppermute | solution.py:25
  127.6 9.5 %collective-permute-start.3 = (s32[64]{0:T(128)S(1)}, s32[64]{0:T(128)S(1)}, u32[]{:S(2)}, u32[]{:S(2)}) collective-permute-start(s32[64]{0:T(128)S(1)} %get-tuple-element.94), channel_id=1, source_target_pairs={{1,0},{2,1},{3,2},{4,3},{5,4},{6,5},{7,6},{8,7},{9,8},{10,9},{11,1... | collective-permute-start | bytes 776 | tf_op jit(solution)/shard_map/ppermute | solution.py:26
  143.0 3.5 copy-start
  179.4 4.9 copy-start.14
  190.4 6.7 %copy-start.3 = (bf16[1024,768]{0,1:T(8,128)(2,1)S(1)}, bf16[1024,768]{0,1:T(8,128)(2,1)}, u32[]{:S(2)}) copy-start(bf16[1024,768]{0,1:T(8,128)(2,1)} %copy-done.2) | copy-start | bytes 4718596
  200.2 1.7 copy-start.4
  200.6 3.3 copy-start.9
  200.6 7.2 %slice-start = ((s8[4718592]{0:T(1024)(128)(4,1)}), s8[4194304]{0:T(1024)(128)(4,1)S(1)}, s32[]{:S(2)}) async-start(s8[4718592]{0:T(1024)(128)(4,1)} %bitcast.105), calls=%async_computation.4 | async-start | bytes 8388608
  201.9 5.9 %copy-start.19 = (bf16[1024,768]{0,1:T(8,128)(2,1)}, bf16[1024,768]{0,1:T(8,128)(2,1)S(1)}, u32[]{:S(2)}) copy-start(bf16[1024,768]{0,1:T(8,128)(2,1)S(1)} %multiply_convert_fusion.1) | copy-start | bytes 4718596
  203.9 3.9 slice-start.1
  243.2 4.4 copy-start.21
  247.6 65.5 %copy-start.10 = (f32[1024,768]{0,1:T(8,128)}, f32[1024,768]{0,1:T(8,128)S(1)}, u32[]{:S(2)}) copy-start(f32[1024,768]{0,1:T(8,128)S(1)} %multiply_add_fusion.1) | copy-start | bytes 9437188
  247.6 1.5 copy-start.1
  304.2 6.6 %copy-start.5 = (f32[1152,1536]{1,0:T(8,128)S(1)}, f32[1152,1536]{1,0:T(8,128)}, u32[]{:S(2)}) copy-start(f32[1152,1536]{1,0:T(8,128)} %get-tuple-element.39) | copy-start | bytes 21233668
  304.2 13.0 %slice-start.2 = ((s8[4718592]{0:T(1024)(128)(4,1)}), s8[4194304]{0:T(1024)(128)(4,1)S(1)}, s32[]{:S(2)}) async-start(s8[4718592]{0:T(1024)(128)(4,1)} %bitcast.129), calls=%async_computation.6 | async-start | bytes 8388608
  304.2 13.0 %slice-start.4 = ((s8[4718592]{0:T(1024)(128)(4,1)}), s8[4194304]{0:T(1024)(128)(4,1)S(1)}, s32[]{:S(2)}) async-start(s8[4718592]{0:T(1024)(128)(4,1)} %bitcast.134), calls=%async_computation.8 | async-start | bytes 8388608
  310.8 3.5 copy-start.17
  310.8 6.4 %slice-start.3 = ((s8[4718592]{0:T(1024)(128)(4,1)}), s8[524288]{0:T(1024)(128)(4,1)S(1)}, s32[]{:S(2)}) async-start(s8[4718592]{0:T(1024)(128)(4,1)} %bitcast.129), calls=%async_computation.7 | async-start | bytes 1048576
  310.8 6.4 %slice-start.5 = ((s8[4718592]{0:T(1024)(128)(4,1)}), s8[524288]{0:T(1024)(128)(4,1)S(1)}, s32[]{:S(2)}) async-start(s8[4718592]{0:T(1024)(128)(4,1)} %bitcast.134), calls=%async_computation.9 | async-start | bytes 1048576
  314.3 2.9 copy-start.20
  329.2 55.0 %collective-permute-start.4 = (bf16[64,1536]{1,0:T(8,128)(2,1)}, bf16[64,1536]{1,0:T(8,128)(2,1)}, u32[]{:S(2)}, u32[]{:S(2)}) collective-permute-start(bf16[64,1536]{1,0:T(8,128)(2,1)} %get-tuple-element.71), channel_id=1, source_target_pairs={{0,1},{1,2},{2,3},{3,4},{4,5},{5,6},{6,7},{7,8},{8,9},{9,10},{10,1... | collective-permute-start | bytes 589832 | tf_op jit(solution)/shard_map/ppermute | solution.py:34
  335.0 51.0 %collective-permute-start.5 = (bf16[64,1536]{1,0:T(8,128)(2,1)}, bf16[64,1536]{1,0:T(8,128)(2,1)}, u32[]{:S(2)}, u32[]{:S(2)}) collective-permute-start(bf16[64,1536]{1,0:T(8,128)(2,1)} %get-tuple-element.70), channel_id=1, source_target_pairs={{1,0},{2,1},{3,2},{4,3},{5,4},{6,5},{7,6},{8,7},{9,8},{10,9},{11,1... | collective-permute-start | bytes 589832 | tf_op jit(solution)/shard_map/ppermute | solution.py:34
  374.7 6.5 %copy-start.7 = (f32[2,16,72,384]{3,2,1,0:T(8,128)S(1)}, f32[2,16,72,384]{3,2,1,0:T(8,128)}, u32[]{:S(2)}) copy-start(f32[2,16,72,384]{3,2,1,0:T(8,128)} %reshape_reshape.7) | copy-start | bytes 10616836
  398.4 2.4 copy-start.11
  411.4 7.0 %copy-start.16 = (bf16[1024,768]{0,1:T(8,128)(2,1)S(1)}, bf16[1024,768]{0,1:T(8,128)(2,1)}, u32[]{:S(2)}) copy-start(bf16[1024,768]{0,1:T(8,128)(2,1)} %copy-done.15) | copy-start | bytes 4718596
  411.4 7.0 %copy-start.18 = (bf16[1024,768]{1,0:T(8,128)(2,1)S(1)}, bf16[1024,768]{1,0:T(8,128)(2,1)}, u32[]{:S(2)}) copy-start(bf16[1024,768]{1,0:T(8,128)(2,1)} %slice.244) | copy-start | bytes 4718596
  418.4 6.3 %copy-start.12 = (bf16[2,384,2304]{2,1,0:T(8,128)(2,1)S(1)}, bf16[2,384,2304]{2,1,0:T(8,128)(2,1)}, u32[]{:S(2)}) copy-start(bf16[2,384,2304]{2,1,0:T(8,128)(2,1)} %copy.59) | copy-start | bytes 10616836
  418.4 6.3 %copy-start.23 = (f32[1024]{0:T(1024)S(1)}, f32[1024]{0:T(1024)}, u32[]{:S(2)}) copy-start(f32[1024]{0:T(1024)} %copy-done.22) | copy-start | bytes 12292
  418.5 6.3 %copy-start.25 = (f32[768]{0:T(1024)S(1)}, f32[768]{0:T(1024)}, u32[]{:S(2)}) copy-start(f32[768]{0:T(1024)} %copy-done.24) | copy-start | bytes 9220
  418.5 6.3 %copy-start.27 = (f32[1024]{0:T(1024)S(1)}, f32[1024]{0:T(1024)}, u32[]{:S(2)}) copy-start(f32[1024]{0:T(1024)} %copy-done.26) | copy-start | bytes 12292
  447.5 1.5 copy-start.13
  455.0 2.8 copy-start.28
Sparse Core Ops, SparseCore 0:
  11.4 63.3 all-gather.2
  78.3 75.0 all-gather.4
  447.6 33.5 reduce-scatter.1

commit v8 on v7

--- a/solution.py
+++ b/solution.py
@@ -338,7 +338,16 @@
 
 
 def grad_t(grad, left, n_dp):
-    return jnp.einsum("tn,tdr->dnr", grad, front(left, n_dp), preferred_element_type=jnp.float32)
+    width = left.shape[1] // n_dp
+    return [
+        lax.dot_general(
+            grad,
+            left[:, d * width : (d + 1) * width],
+            (((0,), (0,)), ((), ())),
+            preferred_element_type=jnp.float32,
+        )
+        for d in range(n_dp)
+    ]
 
 
 def on_device(order, tokens, doc_start, real, w_qkv, w_out, w_in, w_down, gain_attn, gain_mlp, cotangent):
@@ -432,18 +441,23 @@
     grad_tokens = grad_mid + norm_back(grad_hattn * gain_one, normed_a, factor_a)
     height = out_cols + in_cols + down_lines + qkv_cols + 16
     tail = 8 + (-height) % (2 * RING_WAYS * 16)
-    blocks = jnp.concatenate(
+    gain_two_rows = gain_blocks(grad_gain_two, 1, n_seq, rows)[0]
+    gain_one_rows = gain_blocks(grad_gain_one, 1, n_seq, rows, tail)[0]
+    blocks = jnp.stack(
         [
-            grad_outw.reshape(n_dp, n_seq, out_cols, rows),
-            grad_inw.reshape(n_dp, n_seq, in_cols, rows),
-            grad_down.reshape(n_dp, n_seq, down_cols, down_rows).reshape(
-                n_dp, n_seq, down_lines, rows
-            ),
-            gain_blocks(grad_gain_two, n_dp, n_seq, rows),
-            grad_qkvw.reshape(n_dp, n_seq, qkv_cols, rows),
-            gain_blocks(grad_gain_one, n_dp, n_seq, rows, tail),
-        ],
-        2,
+            jnp.concatenate(
+                [
+                    grad_outw[d].reshape(n_seq, out_cols, rows),
+                    grad_inw[d].reshape(n_seq, in_cols, rows),
+                    grad_down[d].reshape(n_seq, down_cols, down_rows).reshape(n_seq, down_lines, rows),
+                    gain_two_rows,
+                    grad_qkvw[d].reshape(n_seq, qkv_cols, rows),
+                    gain_one_rows,
+                ],
+                1,
+            )
+            for d in range(n_dp)
+        ]
     )
     depth = blocks.shape[2]
     half = lax.psum_scatter(

time: 573 us -> 611 us (1.066)
  local copies, waits for them, and re-layouts: 177 us -> 202 us
  other arithmetic: 71.3 us -> 81.2 us
    concatenate x3 -> x2, local copies, waits for them, and re-layouts: 1.49 us -> 68.3 us  [on_device(): jnp.concatenate([grad_outw[d].reshape(n_seq, out_cols, rows), grad_inw[d]...]
    transpose x4 -> x0, local copies, waits for them, and re-layouts: 24.4 us -> none  [grad_t(): jnp.einsum('tn,tdr->dnr', grad, front(left, n_dp), preferred_element_type...]
    unnamed x85 -> x86, local copies, waits for them, and re-layouts: 37.1 us -> 19.4 us
    another operation x2 -> x3, other arithmetic: 9.25 us -> 24.6 us  [the longest x1 16.2 us: on_device(): jnp.stack([jnp.concatenate([grad_outw[d].reshape(n_seq, out_cols, rows),...]
    dot_general x4 -> x8, matrix products: 20.9 us -> 26.4 us  [grad_t(): lax.dot_general(grad, left[:, d * width:(d + 1) * width], (((0,), (0,)),...]
  transfers between devices with their start and end apart: 9 -> 9, of which waited for: 4 -> 4; matrix products, arithmetic and copies ran while one was open for 25% -> 18% of each run, Pallas kernels for 4% -> 3%
where the time goes in v8:
time: 611 us; the launch traced here: 599 us
  local copies, waits for them, and re-layouts  202 us (33%)
  Pallas kernels  147 us (24%)
  other arithmetic  81.2 us (13%)
  matrix products  71.2 us (12%)
  waiting for transfers between devices  63.9 us (10%)
  starting transfers between devices  18.7 us (3%)
  between operations  14.8 us (2%)
    pallas_call x1, Pallas kernels, ring_reduce(): pl.pallas_call(functools.partial(ring_kernel, tuple(order), per_way), out...  71 us
    concatenate x2, local copies, waits for them, and re-layouts, on_device(): jnp.concatenate([grad_outw[d].reshape(n_seq, out_cols, rows), grad_inw[d]...  68.3 us
    pallas_call x1, Pallas kernels, attn_bwd(): pl.pallas_call(attn_bwd_kernel, out_shape=(jax.ShapeDtypeStruct((count, w...  55.3 us
    all_gather x2, waiting for transfers between devices, gather_rows(): every = lax.all_gather(payload, ('dp', 'seq'), axis=0, tiled=True)  50.7 us
    dot_general x8, matrix products, grad_t(): lax.dot_general(grad, left[:, d * width:(d + 1) * width], (((0,), (0,)),...  26.4 us
    dot_general x4, matrix products, apply_back(): jnp.einsum('tn,dnr->tdr', grad, weight_t, preferred_element_type=jnp.floa...  25.6 us
    pallas_call x1, Pallas kernels, attn_fwd(): pl.pallas_call(attn_fwd_kernel, out_shape=jax.ShapeDtypeStruct((count, wi...  20.9 us
    unnamed x86, local copies, waits for them, and re-layouts  19.4 us
  transfers between devices with their start and end apart: 9, of which 4 were waited for; matrix products, arithmetic and copies ran while one was open for 18% of the time, Pallas kernels for 3%

profile of v8, /device:TPU:0, one launch (start us, length us, event | category | flops | bytes accessed | tf_op | source)
XLA Modules:
  0.0 598.8 jit_solution(3614023589784350665)
XLA Ops:
  11.2 4.2 concatenate.60
  19.9 3.6 copy.30
  24.2 50.7 %all-gather.3.cloned.1.call-done = bf16[4864,384]{1,0:T(8,128)(2,1)} async-done(((bf16[152,384]{1,0:T(8,128)(2,1)}), bf16[4864,384]{1,0:T(8,128)(2,1)}) %all-gather.3.cloned.1.call-update) | async-done | bytes 3735568 | tf_op jit(solution)/shard_map/all_gather | solution.py:317
  74.9 4.1 slice.219
  80.4 6.5 %convolution_bitcast_fusion.1 = f32[1024,2304]{1,0:T(8,128)S(1)} fusion(bf16[1024,2,384]{0,2,1:T(8,128)(2,1)S(1)} %bitcast.133, bf16[2,2304,384]{2,1,0:T(8,128)(2,1)} %bitcast.97), kind=kOutput, calls=%fused_computation.4 | convolution fusion | flops 3623878656 | bytes 14548992 | tf_op jit(solution)/shard_map/tdr,dnr->tn/dot_general | solution.py:332
  88.3 3.7 fusion.48
  93.0 2.4 copy.34
  95.3 3.5 copy.31
  98.9 2.7 slice_negate_fusion.2
  101.6 2.5 maximum_multiply_fusion.1
  104.0 3.6 copy.35
  107.6 2.4 copy.32
  110.0 6.7 %add_convert_fusion.1 = (bf16[1024,768]{1,0:T(8,128)(2,1)S(1)}, bf16[1024,768]{1,0:T(8,128)(2,1)S(1)}) fusion(f32[1024,768]{1,0:T(8,128)} %copy.35, f32[1024,768]{1,0:T(8,128)} %copy.30, f32[1024,2304]{1,0:T(8,128)} %copy-done.10, f32[1024,768]{1,0:T(8,128)} %copy.32), kind=kLoop, calls=%fused_computation.56 | loop fusion | flops 4718592 | bytes 18874368 | tf_op jit(solution)/shard_map/convert_element_type | solution.py:378
  118.9 5.1 collective-permute-start
  124.0 3.5 collective-permute-start.2
  130.0 2.6 copy.42
  132.5 2.4 collective-permute-done.2
  137.1 5.8 copy.55
  143.0 3.6 pad_maximum_fusion.2.kv_ref
  146.6 20.9 %shard_map.161 = bf16[1024,768]{1,0:T(8,128)(2,1)S(1)} custom-call(bf16[1024,768]{1,0:T(8,128)(2,1)S(1)} %get-tuple-element.67.q_ref, bf16[1152,1536]{1,0:T(8,128)(2,1)} %pad_maximum_fusion.2.kv_ref, s32[1024,1]{1,0:T(8,128)S(1)} %copy-done, s32[1,1152]{1,0:T(1,128)S(1)} %reshape.241.tk_ref), custom_call_target="tpu_custom_call" | custom-call | tf_op jit(solution)/shard_map/pallas_call | solution.py:287
  167.5 2.4 slice.187
  169.9 2.9 slice.192
  173.5 4.1 slice.189
  177.7 4.8 reshape_reshape.9
  182.5 6.5 %fusion.23 = f32[2,576,1024]{2,1,0:T(8,128)} fusion(bf16[2,768,576]{2,1,0:T(8,128)(2,1)} %reshape_reshape.9, bf16[1024,768]{1,0:T(8,128)(2,1)} %param.23), kind=kOutput, calls=%fused_computation.68 | convolution fusion | flops 1811939328 | bytes 8060928 | tf_op jit(solution)/shard_map/tn,dnr->tdr/dot_general | solution.py:336
  189.0 6.3 %copy.44 = f32[1024,1152]{1,0:T(8,128)} copy(f32[1024,1152]{0,1:T(8,128)} %bitcast.119) | data formatting | bytes 9437184 | tf_op jit(solution)/shard_map/reshape | solution.py:337
  195.3 3.2 fusion.51
  202.2 3.9 convolution_bitcast_fusion
  206.2 11.1 %fusion.25 = (f32[1024,1152]{1,0:T(8,128)}, f32[1024,1152]{1,0:T(8,128)S(1)}) fusion(f32[1024,1152]{1,0:T(8,128)S(1)} %bitcast.96, f32[1024,2304]{1,0:T(8,128)S(1)} %convolution_bitcast_fusion), kind=kLoop, calls=%fused_computation.72 | loop fusion | flops 76677120 | bytes 18874368 | tf_op jit(solution)/shard_map/transpose(jvp())/mul | solution.py:80
  217.3 4.3 multiply_add_fusion
  221.6 5.8 copy.46
  227.3 11.5 %multiply_reduce_fusion = (f32[768]{0:T(1024)S(1)}, f32[1024]{0:T(1024)S(1)}, f32[1024]{0:T(1024)S(1)}, f32[1024,768]{0,1:T(8,128)}) fusion(f32[1024,768]{0,1:T(8,128)} %copy-done.7, f32[1024]{0:T(1024)S(1)} %add_rsqrt_fusion, f32[1024]{0:T(1024)S(1)} %broadcast_multiply_fusion.4, f32[768]{0:T(1024)S(1)} %reshape.263, bf16[768,2304]{1,0:T(8,128)(2,1)} %bitcast.129, ...), kind=kOutput, calls=%fused_computation.49 | convolution fusion | flops 3634885888 | bytes 19290112 | tf_op jit(solution)/shard_map/tn,dnr->tdr/dot_general | solution.py:336
  238.8 2.8 copy.47
  241.6 4.4 multiply_add_fusion.1
  247.5 55.3 %shard_map.162 = (f32[1024,768]{1,0:T(8,128)}, f32[1152,1536]{1,0:T(8,128)}) custom-call(bf16[1024,768]{1,0:T(8,128)(2,1)S(1)} %get-tuple-element.67.q_ref, bf16[1152,1536]{1,0:T(8,128)(2,1)} %pad_maximum_fusion.2.kv_ref, s32[1024,1]{1,0:T(8,128)S(1)} %copy-done.1, s32[1,1152]{1,0:T(1,128)S(1)} %reshape.241.tk_ref, ...), custom_call_target="tpu_custom_call" | custom-call | tf_op jit(solution)/shard_map/pallas_call | solution.py:299
  302.8 6.6 %slice.195 = f32[1024,1536]{1,0:T(8,128)} slice(f32[1152,1536]{1,0:T(8,128)} %get-tuple-element.39), slice={[64:1088], [0:1536]} | slice | bytes 12582912 | tf_op jit(solution)/shard_map/slice | solution.py:426
  314.7 4.5 fusion.30
  321.2 4.5 fusion.34
  325.7 2.7 convolution_bitcast_fusion.2
  332.5 6.0 collective-permute-start.4
  339.8 2.7 copy.50
  344.3 2.4 reshape_reshape.11
  346.8 3.0 copy.56
  349.8 3.4 reshape_reshape.10
  358.9 3.2 slice.298
  362.1 3.8 slice.234
  365.9 2.4 copy.53
  370.2 2.5 maximum_multiply_fusion.2
  372.6 2.4 copy.51
  375.1 3.7 copy.54
  378.8 6.1 %subtract_convert_fusion.1 = (bf16[1024,768]{1,0:T(8,128)(2,1)S(1)}, bf16[1024,768]{1,0:T(8,128)(2,1)S(1)}) fusion(f32[1024,768]{1,0:T(8,128)} %copy.51, f32[1024,768]{1,0:T(8,128)} %get-tuple-element.38, f32[1024,768]{1,0:T(8,128)S(1)} %copy-done.6, f32[1024,768]{1,0:T(8,128)} %copy.54, f32[1024,1536]{1,0:T(8,128)} %fusion.40), kind=kLoop, calls=%fused_computation.51 | loop fusion | flops 4718592 | bytes 18874368 | tf_op jit(solution)/shard_map/convert.2
  384.9 4.2 fusion.28
  389.2 4.2 fusion.32
  393.4 6.1 %fusion.18 = (f32[768]{0:T(1024)S(1)}, f32[1024]{0:T(1024)S(1)}, f32[1024]{0:T(1024)S(1)}, f32[1024,768]{0,1:T(8,128)}) fusion(bf16[1024,768]{0,1:T(8,128)(2,1)S(1)} %copy-done.5, f32[1024]{0:T(1024)S(1)} %copy-done.32, f32[1024]{0:T(1024)S(1)} %copy-done.28, f32[768]{0:T(1024)S(1)} %copy-done.30, bf16[768,2304]{1,0:T(8,128)(2,1)S(1)} %bitcast.124, ...), kind=kOutput, calls=%fused_computation.39 | convolution fusion | flops 3645109504 | bytes 12998656 | tf_op jit(solution)/shard_map/tn,dnr->tdr/dot_general | solution.py:336
  399.8 32.9 %concatenate.65 = f32[16,448,384]{2,1,0:T(8,128)} concatenate(f32[16,48,384]{2,1,0:T(8,128)} %bitcast.116, f32[16,144,384]{2,1,0:T(8,128)} %bitcast.126, f32[16,72,384]{2,1,0:T(8,128)S(1)} %copy-done.16, f32[16,1,384]{2,1,0:T(1,128)S(1)} %broadcast_in_dim.19, f32[16,7,384]{2,1,0:T(8,128)S(1)} %broadcast_in_dim.20, f32[16,144,384]{2,1,0:T(8,128)} %bitcast.128, ...), dimensions={1} | concatenate | bytes 22020096 | tf_op jit(solution)/shard_map/concatenate | solution.py:448
  432.7 35.4 %concatenate.64 = f32[16,448,384]{2,1,0:T(8,128)} concatenate(f32[16,48,384]{2,1,0:T(8,128)} %bitcast.115, f32[16,144,384]{2,1,0:T(8,128)} %bitcast.125, f32[16,72,384]{2,1,0:T(8,128)} %reshape_reshape.10, f32[16,1,384]{2,1,0:T(1,128)S(1)} %broadcast_in_dim.19, f32[16,7,384]{2,1,0:T(8,128)S(1)} %broadcast_in_dim.20, f32[16,144,384]{2,1,0:T(8,128)} %bitcast.127, ...), dimensions={1} | concatenate | bytes 22020096 | tf_op jit(solution)/shard_map/concatenate | solution.py:448
  468.1 16.2 %pad_maximum_fusion = f32[2,7168,384]{2,1,0:T(8,128)} fusion(f32[1,7168,384]{2,1,0:T(8,128)} %bitcast.93, f32[1,7168,384]{2,1,0:T(8,128)} %bitcast.94), kind=kLoop, calls=%fused_computation | loop fusion | flops 5505024 | bytes 44040192 | tf_op jit(solution)/shard_map/stack | solution.py:446
  484.3 4.4 copy.39
  488.7 5.6 fusion.20
  494.3 3.1 copy.58
  498.6 6.5 %fusion.17 = f32[1024,768]{0,1:T(8,128)} fusion(f32[1024,768]{0,1:T(8,128)S(1)} %copy-done.3, bf16[1024,768]{0,1:T(8,128)(2,1)} %copy-done.4, f32[1024,768]{0,1:T(8,128)} %get-tuple-element.102, f32[1024]{0:T(1024)S(1)} %broadcast_multiply_fusion, f32[1024]{0:T(1024)S(1)} %broadcast_multiply_fusion.1, f32[768]{0:T(1024)S(1)} %copy-done.30, ...), kind=kLoop, calls=%fused_computation.38 | loop fusion | flops 7077888 | bytes 11029504 | tf_op jit(solution)/shard_map/add | solution.py:441
  505.1 4.2 copy.59
  509.4 8.7 %reduce-scatter.2.cloned.1.call-done = f32[1,7168,384]{2,1,0:T(8,128)} async-done(((f32[2,7168,384]{2,1,0:T(8,128)}), f32[1,7168,384]{2,1,0:T(8,128)}) %reduce-scatter.2.cloned.1.call-update) | async-done | bytes 11010064 | tf_op jit(solution)/shard_map/reduce_scatter | solution.py:463
  518.0 71.0 %shard_map.163 = f32[448,384]{1,0:T(8,128)S(1)} custom-call(f32[16,448,384]{2,1,0:T(8,128)} %bitcast.110), custom_call_target="tpu_custom_call" | custom-call | tf_op jit(solution)/shard_map/pallas_call | solution.py:194
  (160 shorter events, 52.1 us)
Async XLA Ops:
  7.2 10.0 %copy-start.33 = (s32[1024]{0:T(1024)S(1)}, s32[1024]{0:T(1024)}, u32[]{:S(2)}) copy-start(s32[1024]{0:T(1024)} %param.16) | copy-start | bytes 12292
  7.2 10.0 %copy-start.34 = (s32[1024]{0:T(1024)S(1)}, s32[1024]{0:T(1024)}, u32[]{:S(2)}) copy-start(s32[1024]{0:T(1024)} %param.15) | copy-start | bytes 12292
  7.2 67.7 %all-gather.3.cloned.1.call-start = ((), (), s32[]{:S(2)}) async-start(), calls=%async_computation.1 | async-start | bytes 3852288 | tf_op jit(solution)/shard_map/all_gather | solution.py:317
  9.5 158.0 %all-gather.5.cloned.1.call-start = ((), (), s32[]{:S(2)}) async-start(), calls=%async_computation.2 | async-start | bytes 6893568 | tf_op jit(solution)/shard_map/all_gather | solution.py:317
  15.4 502.7 %reduce-scatter.2.cloned.1.call-start = ((), (), s32[]{:S(2)}) async-start(), calls=%async_computation.3 | async-start | bytes 33030144 | tf_op jit(solution)/shard_map/reduce_scatter | solution.py:463
  17.2 62.7 %copy-start.4 = (bf16[1024,768]{0,1:T(8,128)(2,1)}, bf16[1024,768]{0,1:T(8,128)(2,1)S(1)}, u32[]{:S(2)}) copy-start(bf16[1024,768]{0,1:T(8,128)(2,1)S(1)} %copy.28) | copy-start | bytes 4718596
  23.7 56.1 %copy-start.27 = (f32[1024]{0:T(1024)}, f32[1024]{0:T(1024)S(1)}, u32[]{:S(2)}) copy-start(f32[1024]{0:T(1024)S(1)} %broadcast_multiply_fusion.5) | copy-start | bytes 12292
  24.2 55.7 %copy-start.31 = (f32[1024]{0:T(1024)}, f32[1024]{0:T(1024)S(1)}, u32[]{:S(2)}) copy-start(f32[1024]{0:T(1024)S(1)} %add_rsqrt_fusion.1) | copy-start | bytes 12292
  79.8 7.0 %copy-start.29 = (f32[768]{0:T(1024)}, f32[768]{0:T(1024)S(1)}, u32[]{:S(2)}) copy-start(f32[768]{0:T(1024)S(1)} %reshape.262) | copy-start | bytes 9220
  80.3 6.5 %copy-start.21 = (bf16[1024,768]{0,1:T(8,128)(2,1)}, bf16[1024,768]{0,1:T(8,128)(2,1)S(1)}, u32[]{:S(2)}) copy-start(bf16[1024,768]{0,1:T(8,128)(2,1)S(1)} %fusion.13) | copy-start | bytes 4718596
  86.8 6.1 %copy-start.10 = (f32[1024,2304]{1,0:T(8,128)}, f32[1024,2304]{1,0:T(8,128)S(1)}, u32[]{:S(2)}) copy-start(f32[1024,2304]{1,0:T(8,128)S(1)} %convolution_bitcast_fusion.1) | copy-start | bytes 28311556
  110.0 6.7 %copy-start.11 = (bf16[1024,768]{1,0:T(8,128)(2,1)S(1)}, bf16[1024,768]{1,0:T(8,128)(2,1)}, u32[]{:S(2)}) copy-start(bf16[1024,768]{1,0:T(8,128)(2,1)} %slice.299) | copy-start | bytes 4718596
  117.5 25.5 %collective-permute-start.1 = (bf16[64,1536]{1,0:T(8,128)(2,1)}, bf16[64,1536]{1,0:T(8,128)(2,1)}, u32[]{:S(2)}, u32[]{:S(2)}) collective-permute-start(bf16[64,1536]{1,0:T(8,128)(2,1)} %get-tuple-element.79), channel_id=1, source_target_pairs={{1,0},{2,1},{3,2},{4,3},{5,4},{6,5},{7,6},{8,7},{9,8},{10,9},{11,1... | collective-permute-start | bytes 589832 | tf_op jit(solution)/shard_map/ppermute | solution.py:26
  118.9 24.1 %collective-permute-start = (bf16[64,1536]{1,0:T(8,128)(2,1)}, bf16[64,1536]{1,0:T(8,128)(2,1)}, u32[]{:S(2)}, u32[]{:S(2)}) collective-permute-start(bf16[64,1536]{1,0:T(8,128)(2,1)} %get-tuple-element.78), channel_id=1, source_target_pairs={{0,1},{1,2},{2,3},{3,4},{4,5},{5,6},{6,7},{7,8},{8,9},{9,10},{10,1... | collective-permute-start | bytes 589832 | tf_op jit(solution)/shard_map/ppermute | solution.py:25
  124.0 10.9 %collective-permute-start.2 = (s32[64]{0:T(128)S(1)}, s32[64]{0:T(128)S(1)}, u32[]{:S(2)}, u32[]{:S(2)}) collective-permute-start(s32[64]{0:T(128)S(1)} %get-tuple-element.95), channel_id=1, source_target_pairs={{0,1},{1,2},{2,3},{3,4},{4,5},{5,6},{6,7},{7,8},{8,9},{9,10},{10,1... | collective-permute-start | bytes 776 | tf_op jit(solution)/shard_map/ppermute | solution.py:25
  127.6 9.5 %collective-permute-start.3 = (s32[64]{0:T(128)S(1)}, s32[64]{0:T(128)S(1)}, u32[]{:S(2)}, u32[]{:S(2)}) collective-permute-start(s32[64]{0:T(128)S(1)} %get-tuple-element.94), channel_id=1, source_target_pairs={{1,0},{2,1},{3,2},{4,3},{5,4},{6,5},{7,6},{8,7},{9,8},{10,9},{11,1... | collective-permute-start | bytes 776 | tf_op jit(solution)/shard_map/ppermute | solution.py:26
  143.0 3.6 copy-start
  198.5 1.7 copy-start.7
  199.0 3.3 copy-start.12
  199.0 7.2 %slice-start = ((s8[4718592]{0:T(1024)(128)(4,1)}), s8[4194304]{0:T(1024)(128)(4,1)S(1)}, s32[]{:S(2)}) async-start(s8[4718592]{0:T(1024)(128)(4,1)} %bitcast.95), calls=%async_computation.4 | async-start | bytes 8388608
  200.2 5.9 copy-start.24
  202.2 3.9 slice-start.1
  241.6 4.4 copy-start.26
  246.0 73.2 %copy-start.2 = (f32[1024,768]{0,1:T(8,128)}, f32[1024,768]{0,1:T(8,128)S(1)}, u32[]{:S(2)}) copy-start(f32[1024,768]{0,1:T(8,128)S(1)} %multiply_add_fusion.1) | copy-start | bytes 9437188
  246.0 1.5 copy-start.1
  302.8 6.6 %copy-start.9 = (f32[1152,1536]{1,0:T(8,128)S(1)}, f32[1152,1536]{1,0:T(8,128)}, u32[]{:S(2)}) copy-start(f32[1152,1536]{1,0:T(8,128)} %get-tuple-element.39) | copy-start | bytes 21233668
  302.8 10.9 %slice-start.2 = ((s8[4718592]{0:T(1024)(128)(4,1)}), s8[4194304]{0:T(1024)(128)(4,1)S(1)}, s32[]{:S(2)}) async-start(s8[4718592]{0:T(1024)(128)(4,1)} %bitcast.117), calls=%async_computation.6 | async-start | bytes 8388608
  302.8 10.9 %slice-start.4 = ((s8[4718592]{0:T(1024)(128)(4,1)}), s8[4194304]{0:T(1024)(128)(4,1)S(1)}, s32[]{:S(2)}) async-start(s8[4718592]{0:T(1024)(128)(4,1)} %bitcast.122), calls=%async_computation.8 | async-start | bytes 8388608
  309.4 4.3 slice-start.3
  309.4 4.8 slice-start.5
  311.7 3.0 copy-start.25
  321.2 4.5 copy-start.15
  321.2 4.5 copy-start.20
  328.4 11.4 %copy-start.13 = (f32[1024,768]{1,0:T(8,128)S(1)}, f32[1024,768]{1,0:T(8,128)}, u32[]{:S(2)}) copy-start(f32[1024,768]{1,0:T(8,128)} %get-tuple-element.38) | copy-start | bytes 9437188
  332.5 22.6 %collective-permute-start.4 = (bf16[64,1536]{1,0:T(8,128)(2,1)}, bf16[64,1536]{1,0:T(8,128)(2,1)}, u32[]{:S(2)}, u32[]{:S(2)}) collective-permute-start(bf16[64,1536]{1,0:T(8,128)(2,1)} %get-tuple-element.71), channel_id=1, source_target_pairs={{0,1},{1,2},{2,3},{3,4},{4,5},{5,6},{6,7},{7,8},{8,9},{9,10},{10,1... | collective-permute-start | bytes 589832 | tf_op jit(solution)/shard_map/ppermute | solution.py:34
  338.5 18.6 %collective-permute-start.5 = (bf16[64,1536]{1,0:T(8,128)(2,1)}, bf16[64,1536]{1,0:T(8,128)(2,1)}, u32[]{:S(2)}, u32[]{:S(2)}) collective-permute-start(bf16[64,1536]{1,0:T(8,128)(2,1)} %get-tuple-element.70), channel_id=1, source_target_pairs={{1,0},{2,1},{3,2},{4,3},{5,4},{6,5},{7,6},{8,7},{9,8},{10,9},{11,1... | collective-permute-start | bytes 589832 | tf_op jit(solution)/shard_map/ppermute | solution.py:34
  346.8 6.4 %copy-start.14 = (f32[1024,768]{0,1:T(8,128)S(1)}, f32[1024,768]{0,1:T(8,128)}, u32[]{:S(2)}) copy-start(f32[1024,768]{0,1:T(8,128)} %copy.50) | copy-start | bytes 9437188
  368.3 1.4 copy-start.17
  368.3 1.9 copy-start.18
  375.1 3.7 copy-start.6
  378.8 6.1 %copy-start.22 = (bf16[1024,768]{0,1:T(8,128)(2,1)S(1)}, bf16[1024,768]{0,1:T(8,128)(2,1)}, u32[]{:S(2)}) copy-start(bf16[1024,768]{0,1:T(8,128)(2,1)} %copy-done.21) | copy-start | bytes 4718596
  378.8 6.1 %copy-start.23 = (bf16[1024,768]{1,0:T(8,128)(2,1)S(1)}, bf16[1024,768]{1,0:T(8,128)(2,1)}, u32[]{:S(2)}) copy-start(bf16[1024,768]{1,0:T(8,128)(2,1)} %slice.298) | copy-start | bytes 4718596
  389.2 4.2 copy-start.5
  389.2 4.2 copy-start.19
  389.2 4.2 copy-start.28
  389.2 4.2 copy-start.30
  389.2 4.2 copy-start.32
  393.4 6.4 %copy-start.16 = (f32[16,72,384]{2,1,0:T(8,128)S(1)}, f32[16,72,384]{2,1,0:T(8,128)}, u32[]{:S(2)}) copy-start(f32[16,72,384]{2,1,0:T(8,128)} %reshape_reshape.11) | copy-start | bytes 5308420
  484.3 4.5 copy-start.8
  494.3 4.3 copy-start.3
Sparse Core Ops, SparseCore 0:
  11.4 63.3 all-gather.2
  78.3 75.0 all-gather.4
  484.4 33.5 reduce-scatter.1

commit v9 on v8

--- a/solution.py
+++ b/solution.py
@@ -447,12 +447,18 @@
         [
             jnp.concatenate(
                 [
-                    grad_outw[d].reshape(n_seq, out_cols, rows),
-                    grad_inw[d].reshape(n_seq, in_cols, rows),
-                    grad_down[d].reshape(n_seq, down_cols, down_rows).reshape(n_seq, down_lines, rows),
-                    gain_two_rows,
-                    grad_qkvw[d].reshape(n_seq, qkv_cols, rows),
-                    gain_one_rows,
+                    *lax.optimization_barrier(
+                        (
+                            grad_outw[d].reshape(n_seq, out_cols, rows),
+                            grad_inw[d].reshape(n_seq, in_cols, rows),
+                            grad_down[d]
+                            .reshape(n_seq, down_cols, down_rows)
+                            .reshape(n_seq, down_lines, rows),
+                            gain_two_rows,
+                            grad_qkvw[d].reshape(n_seq, qkv_cols, rows),
+                            gain_one_rows,
+                        )
+                    ),
                 ],
                 1,
             )

time: 611 us -> 544 us (0.89)
  local copies, waits for them, and re-layouts: 202 us -> 138 us
    concatenate x2 -> x4, local copies, waits for them, and re-layouts: 68.3 us -> 0.89 us  [the longest x2 0.77 us: gain_blocks(): jnp.concatenate([part[:, None], jnp.zeros((n_seq, height - 1, width), par...]
    unnamed x86 -> x112, local copies, waits for them, and re-layouts: 19.4 us -> 29 us
  transfers between devices with their start and end apart: 9 -> 9, of which waited for: 4 -> 4; matrix products, arithmetic and copies ran while one was open for 18% -> 19% of each run, Pallas kernels for 3% -> 4%
where the time goes in v9:
time: 544 us; the launch traced here: 533 us
  Pallas kernels  147 us (27%)
  local copies, waits for them, and re-layouts  138 us (25%)
  other arithmetic  76 us (14%)
  matrix products  73.9 us (14%)
  waiting for transfers between devices  65.2 us (12%)
  starting transfers between devices  17.7 us (3%)
  between operations  15 us (3%)
    pallas_call x1, Pallas kernels, ring_reduce(): pl.pallas_call(functools.partial(ring_kernel, tuple(order), per_way), out...  71 us
    pallas_call x1, Pallas kernels, attn_bwd(): pl.pallas_call(attn_bwd_kernel, out_shape=(jax.ShapeDtypeStruct((count, w...  55.2 us
    all_gather x2, waiting for transfers between devices, gather_rows(): every = lax.all_gather(payload, ('dp', 'seq'), axis=0, tiled=True)  50.7 us
    unnamed x112, local copies, waits for them, and re-layouts  29 us
    dot_general x8, matrix products, grad_t(): lax.dot_general(grad, left[:, d * width:(d + 1) * width], (((0,), (0,)),...  26.6 us
    dot_general x4, matrix products, apply_back(): jnp.einsum('tn,dnr->tdr', grad, weight_t, preferred_element_type=jnp.floa...  25.4 us
    dot_general x4, matrix products, apply_t(): jnp.einsum('tdr,dnr->tn', front(left, n_dp), weight_t, preferred_element_...  21.9 us
    pallas_call x1, Pallas kernels, attn_fwd(): pl.pallas_call(attn_fwd_kernel, out_shape=jax.ShapeDtypeStruct((count, wi...  21 us
  transfers between devices with their start and end apart: 9, of which 4 were waited for; matrix products, arithmetic and copies ran while one was open for 19% of the time, Pallas kernels for 4%

profile of v9, /device:TPU:0, one launch (start us, length us, event | category | flops | bytes accessed | tf_op | source)
XLA Modules:
  0.0 533.4 jit_solution(6283818502488286230)
XLA Ops:
  11.2 4.2 concatenate.62
  19.9 3.6 copy.30
  24.2 50.7 %all-gather.3.cloned.1.call-done = bf16[4864,384]{1,0:T(8,128)(2,1)} async-done(((bf16[152,384]{1,0:T(8,128)(2,1)}), bf16[4864,384]{1,0:T(8,128)(2,1)}) %all-gather.3.cloned.1.call-update) | async-done | bytes 3735568 | tf_op jit(solution)/shard_map/all_gather | solution.py:317
  74.8 4.2 slice.219
  80.4 6.5 %convolution_bitcast_fusion.1 = f32[1024,2304]{1,0:T(8,128)S(1)} fusion(bf16[1024,2,384]{0,2,1:T(8,128)(2,1)S(1)} %bitcast.133, bf16[2,2304,384]{2,1,0:T(8,128)(2,1)} %bitcast.95), kind=kOutput, calls=%fused_computation.4 | convolution fusion | flops 3623878656 | bytes 14548992 | tf_op jit(solution)/shard_map/tdr,dnr->tn/dot_general | solution.py:332
  88.3 3.5 fusion.48
  92.9 2.4 copy.34
  95.3 3.5 copy.31
  98.8 2.7 slice_negate_fusion.2
  101.5 2.5 maximum_multiply_fusion.1
  104.0 3.6 copy.35
  107.5 2.4 copy.32
  109.9 6.7 %add_convert_fusion.1 = (bf16[1024,768]{1,0:T(8,128)(2,1)S(1)}, bf16[1024,768]{1,0:T(8,128)(2,1)S(1)}) fusion(f32[1024,768]{1,0:T(8,128)} %copy.35, f32[1024,768]{1,0:T(8,128)} %copy.30, f32[1024,2304]{1,0:T(8,128)} %copy-done.11, f32[1024,768]{1,0:T(8,128)} %copy.32), kind=kLoop, calls=%fused_computation.56 | loop fusion | flops 4718592 | bytes 18874368 | tf_op jit(solution)/shard_map/convert_element_type | solution.py:378
  117.4 4.0 collective-permute-start
  124.1 5.2 collective-permute-start.2
  130.3 2.6 copy.42
  132.9 6.1 %collective-permute-done.3 = s32[64]{0:T(128)S(1)} collective-permute-done((s32[64]{0:T(128)S(1)}, s32[64]{0:T(128)S(1)}, u32[]{:S(2)}, u32[]{:S(2)}) %collective-permute-start.3) | collective-permute-done | bytes 288 | tf_op jit(solution)/shard_map/ppermute | solution.py:26
  139.0 5.8 %copy.55 = bf16[2,384,2304]{2,1,0:T(8,128)(2,1)} copy(bf16[2,384,2304]{1,2,0:T(8,128)(2,1)} %bitcast.96) | data formatting | bytes 7077888 | tf_op jit(solution)/shard_map/tn,dnr->tdr/dot_general | solution.py:336
  144.9 3.6 pad_maximum_fusion.2.kv_ref
  148.4 21.0 %shard_map.161 = bf16[1024,768]{1,0:T(8,128)(2,1)S(1)} custom-call(bf16[1024,768]{1,0:T(8,128)(2,1)S(1)} %get-tuple-element.91.q_ref, bf16[1152,1536]{1,0:T(8,128)(2,1)} %pad_maximum_fusion.2.kv_ref, s32[1024,1]{1,0:T(8,128)S(1)} %copy-done, s32[1,1152]{1,0:T(1,128)S(1)} %reshape.241.tk_ref), custom_call_target="tpu_custom_call" | custom-call | tf_op jit(solution)/shard_map/pallas_call | solution.py:287
  170.2 2.4 slice.187
  172.7 2.9 slice.192
  175.5 4.1 slice.189
  179.8 4.8 reshape_reshape.9
  184.6 3.2 fusion.51
  189.8 5.8 %copy.46 = bf16[2,384,2304]{2,1,0:T(8,128)(2,1)} copy(bf16[2,384,2304]{1,2,0:T(8,128)(2,1)} %bitcast.97) | data formatting | bytes 7077888 | tf_op jit(solution)/shard_map/tn,dnr->tdr/dot_general | solution.py:336
  195.6 6.5 %fusion.23 = f32[2,576,1024]{2,1,0:T(8,128)} fusion(bf16[2,768,576]{2,1,0:T(8,128)(2,1)} %reshape_reshape.9, bf16[1024,768]{1,0:T(8,128)(2,1)} %param.23), kind=kOutput, calls=%fused_computation.68 | convolution fusion | flops 1811939328 | bytes 8060928 | tf_op jit(solution)/shard_map/tn,dnr->tdr/dot_general | solution.py:336
  202.1 6.3 %copy.44 = f32[1024,1152]{1,0:T(8,128)} copy(f32[1024,1152]{0,1:T(8,128)} %bitcast.119) | data formatting | bytes 9437184 | tf_op jit(solution)/shard_map/reshape | solution.py:337
  208.4 2.4 multiply_convert_fusion.1
  210.8 6.5 %convolution_bitcast_fusion = f32[1024,2304]{1,0:T(8,128)S(1)} fusion(bf16[1024,2,384]{0,2,1:T(8,128)(2,1)S(1)} %bitcast.134, bf16[2,2304,384]{2,1,0:T(8,128)(2,1)} %bitcast.98), kind=kOutput, calls=%fused_computation.3 | convolution fusion | flops 3623878656 | bytes 14548992 | tf_op jit(solution)/shard_map/tdr,dnr->tn/dot_general | solution.py:332
  217.4 11.2 %fusion.25 = (f32[1024,1152]{1,0:T(8,128)}, f32[1024,1152]{1,0:T(8,128)S(1)}) fusion(f32[1024,1152]{1,0:T(8,128)S(1)} %bitcast.94, f32[1024,2304]{1,0:T(8,128)S(1)} %convolution_bitcast_fusion), kind=kLoop, calls=%fused_computation.72 | loop fusion | flops 76677120 | bytes 18874368 | tf_op jit(solution)/shard_map/transpose(jvp())/mul | solution.py:80
  228.6 4.0 multiply_add_fusion
  232.6 9.4 %multiply_reduce_fusion = (f32[768]{0:T(1024)S(1)}, f32[1024]{0:T(1024)S(1)}, f32[1024]{0:T(1024)S(1)}, f32[1024,768]{0,1:T(8,128)S(1)}) fusion(f32[1024,768]{0,1:T(8,128)S(1)} %copy-done.8, f32[1024]{0:T(1024)S(1)} %add_rsqrt_fusion, f32[1024]{0:T(1024)S(1)} %broadcast_multiply_fusion.4, f32[768]{0:T(1024)S(1)} %reshape.263, ...), kind=kOutput, calls=%fused_computation.49 | convolution fusion | flops 3634885888 | bytes 19290112 | tf_op jit(solution)/shard_map/tn,dnr->tdr/dot_general | solution.py:336
  247.0 2.6 convolution_bitcast_fusion.2
  252.0 4.6 fusion.34
  256.6 4.6 fusion.30
  262.8 3.7 convolution_convert_fusion.do_ref
  266.5 55.2 %shard_map.162 = (f32[1024,768]{1,0:T(8,128)}, f32[1152,1536]{1,0:T(8,128)}) custom-call(bf16[1024,768]{1,0:T(8,128)(2,1)S(1)} %get-tuple-element.91.q_ref, bf16[1152,1536]{1,0:T(8,128)(2,1)} %pad_maximum_fusion.2.kv_ref, s32[1024,1]{1,0:T(8,128)S(1)} %copy-done.1, s32[1,1152]{1,0:T(1,128)S(1)} %reshape.241.tk_ref, ...), custom_call_target="tpu_custom_call" | custom-call | tf_op jit(solution)/shard_map/pallas_call | solution.py:299
  321.7 5.4 %convert.21 = bf16[1152,1536]{1,0:T(8,128)(2,1)} convert(f32[1152,1536]{1,0:T(8,128)} %get-tuple-element.51) | non-fusion elementwise | flops 1769472 | bytes 10616832 | tf_op jit(solution)/shard_map/convert.7
  327.8 3.0 slice.195
  333.4 2.4 reshape_reshape.11
  335.9 3.0 copy.56
  338.8 3.4 reshape_reshape.10
  346.9 4.6 collective-permute-start.4
  351.5 4.0 slice_negate_fusion.1
  355.5 3.1 collective-permute-done.4
  362.2 3.2 slice.298
  365.4 3.8 slice.234
  369.2 2.6 copy.53
  373.6 2.4 maximum_multiply_fusion.2
  376.0 2.4 copy.51
  378.4 3.8 copy.54
  382.2 6.1 %subtract_convert_fusion.1 = (bf16[1024,768]{1,0:T(8,128)(2,1)S(1)}, bf16[1024,768]{1,0:T(8,128)(2,1)S(1)}) fusion(f32[1024,768]{1,0:T(8,128)} %copy.51, f32[1024,768]{1,0:T(8,128)} %get-tuple-element.50, f32[1024,768]{1,0:T(8,128)S(1)} %copy-done.6, f32[1024,768]{1,0:T(8,128)} %copy.54, f32[1024,1536]{1,0:T(8,128)} %fusion.40), kind=kLoop, calls=%fused_computation.51 | loop fusion | flops 4718592 | bytes 18874368 | tf_op jit(solution)/shard_map/convert.2
  388.4 4.3 fusion.32
  392.7 4.2 fusion.28
  396.9 5.9 %fusion.18 = (f32[768]{0:T(1024)S(1)}, f32[1024]{0:T(1024)S(1)}, f32[1024]{0:T(1024)S(1)}, f32[1024,768]{0,1:T(8,128)}) fusion(bf16[1024,768]{0,1:T(8,128)(2,1)S(1)} %copy-done.5, f32[1024]{0:T(1024)S(1)} %copy-done.40, f32[1024]{0:T(1024)S(1)} %copy-done.36, f32[768]{0:T(1024)S(1)} %copy-done.38, bf16[768,2304]{1,0:T(8,128)(2,1)S(1)} %bitcast.124, ...), kind=kOutput, calls=%fused_computation.39 | convolution fusion | flops 3645109504 | bytes 12998656 | tf_op jit(solution)/shard_map/tn,dnr->tdr/dot_general | solution.py:336
  414.6 7.8 %pad_maximum_fusion = f32[2,7168,384]{2,1,0:T(8,128)} fusion(f32[1,7168,384]{2,1,0:T(8,128)S(1)} %bitcast.100, f32[1,7168,384]{2,1,0:T(8,128)S(1)} %bitcast.99), kind=kLoop, calls=%fused_computation | loop fusion | flops 5505024 | bytes 44040192 | tf_op jit(solution)/shard_map/stack | solution.py:446
  422.4 4.7 copy.39
  427.0 5.7 %fusion.20 = bf16[1024,768]{0,1:T(8,128)(2,1)} fusion(f32[1024,768]{0,1:T(8,128)S(1)} %copy-done.9, bf16[2,768,576]{2,1,0:T(8,128)(2,1)} %reshape_reshape.9, bf16[1024,2,576]{0,2,1:T(8,128)(2,1)} %bitcast.132), kind=kOutput, calls=%fused_computation.48 | convolution fusion | flops 1813512192 | bytes 8847360 | tf_op jit(solution)/shard_map/tdr,dnr->tn/dot_general | solution.py:332
  432.8 3.0 copy.58
  436.9 6.3 %fusion.17 = f32[1024,768]{0,1:T(8,128)} fusion(f32[1024,768]{0,1:T(8,128)S(1)} %copy-done.3, bf16[1024,768]{0,1:T(8,128)(2,1)} %copy-done.4, f32[1024,768]{0,1:T(8,128)} %get-tuple-element.126, f32[1024]{0:T(1024)S(1)} %broadcast_multiply_fusion, f32[1024]{0:T(1024)S(1)} %broadcast_multiply_fusion.1, f32[768]{0:T(1024)S(1)} %copy-done.38, ...), kind=kLoop, calls=%fused_computation.38 | loop fusion | flops 7077888 | bytes 11029504 | tf_op jit(solution)/shard_map/add | solution.py:441
  443.1 4.3 copy.59
  447.5 5.3 reduce-scatter.2.cloned.1.call-done
  452.7 71.0 %shard_map.163 = f32[448,384]{1,0:T(8,128)S(1)} custom-call(f32[16,448,384]{2,1,0:T(8,128)} %bitcast.110), custom_call_target="tpu_custom_call" | custom-call | tf_op jit(solution)/shard_map/pallas_call | solution.py:194
  (186 shorter events, 58.1 us)
Async XLA Ops:
  7.2 10.0 %copy-start.41 = (s32[1024]{0:T(1024)S(1)}, s32[1024]{0:T(1024)}, u32[]{:S(2)}) copy-start(s32[1024]{0:T(1024)} %param.16) | copy-start | bytes 12292
  7.2 10.0 %copy-start.42 = (s32[1024]{0:T(1024)S(1)}, s32[1024]{0:T(1024)}, u32[]{:S(2)}) copy-start(s32[1024]{0:T(1024)} %param.15) | copy-start | bytes 12292
  7.2 67.7 %all-gather.3.cloned.1.call-start = ((), (), s32[]{:S(2)}) async-start(), calls=%async_computation.1 | async-start | bytes 3852288 | tf_op jit(solution)/shard_map/all_gather | solution.py:317
  9.5 160.0 %all-gather.5.cloned.1.call-start = ((), (), s32[]{:S(2)}) async-start(), calls=%async_computation.2 | async-start | bytes 6893568 | tf_op jit(solution)/shard_map/all_gather | solution.py:317
  15.4 437.3 %reduce-scatter.2.cloned.1.call-start = ((), (), s32[]{:S(2)}) async-start(), calls=%async_computation.3 | async-start | bytes 33030144 | tf_op jit(solution)/shard_map/reduce_scatter | solution.py:469
  17.2 62.7 %copy-start.4 = (bf16[1024,768]{0,1:T(8,128)(2,1)}, bf16[1024,768]{0,1:T(8,128)(2,1)S(1)}, u32[]{:S(2)}) copy-start(bf16[1024,768]{0,1:T(8,128)(2,1)S(1)} %copy.28) | copy-start | bytes 4718596
  23.7 56.2 %copy-start.35 = (f32[1024]{0:T(1024)}, f32[1024]{0:T(1024)S(1)}, u32[]{:S(2)}) copy-start(f32[1024]{0:T(1024)S(1)} %broadcast_multiply_fusion.5) | copy-start | bytes 12292
  24.2 55.7 %copy-start.39 = (f32[1024]{0:T(1024)}, f32[1024]{0:T(1024)S(1)}, u32[]{:S(2)}) copy-start(f32[1024]{0:T(1024)S(1)} %add_rsqrt_fusion.1) | copy-start | bytes 12292
  79.9 7.0 %copy-start.37 = (f32[768]{0:T(1024)}, f32[768]{0:T(1024)S(1)}, u32[]{:S(2)}) copy-start(f32[768]{0:T(1024)S(1)} %reshape.262) | copy-start | bytes 9220
  80.4 6.5 %copy-start.30 = (bf16[1024,768]{0,1:T(8,128)(2,1)}, bf16[1024,768]{0,1:T(8,128)(2,1)S(1)}, u32[]{:S(2)}) copy-start(bf16[1024,768]{0,1:T(8,128)(2,1)S(1)} %fusion.13) | copy-start | bytes 4718596
  86.9 6.0 %copy-start.11 = (f32[1024,2304]{1,0:T(8,128)}, f32[1024,2304]{1,0:T(8,128)S(1)}, u32[]{:S(2)}) copy-start(f32[1024,2304]{1,0:T(8,128)S(1)} %convolution_bitcast_fusion.1) | copy-start | bytes 28311556
  109.9 6.7 %copy-start.12 = (bf16[1024,768]{1,0:T(8,128)(2,1)S(1)}, bf16[1024,768]{1,0:T(8,128)(2,1)}, u32[]{:S(2)}) copy-start(bf16[1024,768]{1,0:T(8,128)(2,1)} %slice.299) | copy-start | bytes 4718596
  117.4 27.5 %collective-permute-start = (bf16[64,1536]{1,0:T(8,128)(2,1)}, bf16[64,1536]{1,0:T(8,128)(2,1)}, u32[]{:S(2)}, u32[]{:S(2)}) collective-permute-start(bf16[64,1536]{1,0:T(8,128)(2,1)} %get-tuple-element.102), channel_id=1, source_target_pairs={{0,1},{1,2},{2,3},{3,4},{4,5},{5,6},{6,7},{7,8},{8,9},{9,10},{10,1... | collective-permute-start | bytes 589832 | tf_op jit(solution)/shard_map/ppermute | solution.py:25
  121.4 23.5 %collective-permute-start.1 = (bf16[64,1536]{1,0:T(8,128)(2,1)}, bf16[64,1536]{1,0:T(8,128)(2,1)}, u32[]{:S(2)}, u32[]{:S(2)}) collective-permute-start(bf16[64,1536]{1,0:T(8,128)(2,1)} %get-tuple-element.103), channel_id=1, source_target_pairs={{1,0},{2,1},{3,2},{4,3},{5,4},{6,5},{7,6},{8,7},{9,8},{10,9},{11,1... | collective-permute-start | bytes 589832 | tf_op jit(solution)/shard_map/ppermute | solution.py:26
  122.8 16.2 %collective-permute-start.3 = (s32[64]{0:T(128)S(1)}, s32[64]{0:T(128)S(1)}, u32[]{:S(2)}, u32[]{:S(2)}) collective-permute-start(s32[64]{0:T(128)S(1)} %get-tuple-element.118), channel_id=1, source_target_pairs={{1,0},{2,1},{3,2},{4,3},{5,4},{6,5},{7,6},{8,7},{9,8},{10,9},{11,1... | collective-permute-start | bytes 776 | tf_op jit(solution)/shard_map/ppermute | solution.py:26
  124.1 14.9 %collective-permute-start.2 = (s32[64]{0:T(128)S(1)}, s32[64]{0:T(128)S(1)}, u32[]{:S(2)}, u32[]{:S(2)}) collective-permute-start(s32[64]{0:T(128)S(1)} %get-tuple-element.119), channel_id=1, source_target_pairs={{0,1},{1,2},{2,3},{3,4},{4,5},{5,6},{6,7},{7,8},{8,9},{9,10},{10,1... | collective-permute-start | bytes 776 | tf_op jit(solution)/shard_map/ppermute | solution.py:25
  144.9 3.6 copy-start
  187.8 1.7 copy-start.7
  208.4 9.0 %slice-start = ((s8[4718592]{0:T(1024)(128)(4,1)}), s8[4194304]{0:T(1024)(128)(4,1)S(1)}, s32[]{:S(2)}) async-start(s8[4718592]{0:T(1024)(128)(4,1)} %bitcast.93), calls=%async_computation.4 | async-start | bytes 8388608
  210.8 6.5 %copy-start.33 = (bf16[1024,768]{0,1:T(8,128)(2,1)}, bf16[1024,768]{0,1:T(8,128)(2,1)S(1)}, u32[]{:S(2)}) copy-start(bf16[1024,768]{0,1:T(8,128)(2,1)S(1)} %multiply_convert_fusion.1) | copy-start | bytes 4718596
  210.8 6.5 %slice-start.1 = ((s8[4718592]{0:T(1024)(128)(4,1)}), s8[524288]{0:T(1024)(128)(4,1)S(1)}, s32[]{:S(2)}) async-start(s8[4718592]{0:T(1024)(128)(4,1)} %bitcast.93), calls=%async_computation.5 | async-start | bytes 1048576
  228.6 4.0 copy-start.8
  232.6 17.1 %copy-start.14 = (bf16[1024,1152]{1,0:T(8,128)(2,1)}, bf16[1024,1152]{1,0:T(8,128)(2,1)S(1)}, u32[]{:S(2)}) copy-start(bf16[1024,1152]{1,0:T(8,128)(2,1)S(1)} %get-tuple-element.89) | copy-start | bytes 7077892
  232.6 9.4 %copy-start.17 = (bf16[1024,768]{0,1:T(8,128)(2,1)S(1)}, bf16[1024,768]{0,1:T(8,128)(2,1)}, u32[]{:S(2)}) copy-start(bf16[1024,768]{0,1:T(8,128)(2,1)} %copy.42) | copy-start | bytes 4718596
  242.9 4.1 copy-start.2
  243.0 4.0 copy-start.29
  245.0 7.0 %slice-start.4 = ((s8[4718592]{0:T(1024)(128)(4,1)}), s8[4194304]{0:T(1024)(128)(4,1)S(1)}, s32[]{:S(2)}) async-start(s8[4718592]{0:T(1024)(128)(4,1)} %bitcast.122), calls=%async_computation.8 | async-start | bytes 8388608
  247.0 5.0 slice-start.2
  247.0 5.0 slice-start.5
  249.6 2.4 slice-start.3
  249.6 2.4 copy-start.34
  256.6 4.6 copy-start.22
  262.8 3.7 copy-start.1
  321.7 6.0 %copy-start.10 = (f32[1152,1536]{1,0:T(8,128)S(1)}, f32[1152,1536]{1,0:T(8,128)}, u32[]{:S(2)}) copy-start(f32[1152,1536]{1,0:T(8,128)} %get-tuple-element.51) | copy-start | bytes 21233668
  335.9 6.4 %copy-start.13 = (f32[1024,768]{1,0:T(8,128)S(1)}, f32[1024,768]{1,0:T(8,128)}, u32[]{:S(2)}) copy-start(f32[1024,768]{1,0:T(8,128)} %get-tuple-element.50) | copy-start | bytes 9437188
  345.6 14.8 %collective-permute-start.5 = (bf16[64,1536]{1,0:T(8,128)(2,1)S(1)}, bf16[64,1536]{1,0:T(8,128)(2,1)S(1)}, u32[]{:S(2)}, u32[]{:S(2)}) collective-permute-start(bf16[64,1536]{1,0:T(8,128)(2,1)S(1)} %get-tuple-element.94), channel_id=1, source_target_pairs={{1,0},{2,1},{3,2},{4,3},{5,4},{6,5},{7,6},{8,7},{9,8},{10,9},{11,1... | collective-permute-start | bytes 589832 | tf_op jit(solution)/shard_map/ppermute | solution.py:34
  346.9 11.7 %collective-permute-start.4 = (bf16[64,1536]{1,0:T(8,128)(2,1)S(1)}, bf16[64,1536]{1,0:T(8,128)(2,1)S(1)}, u32[]{:S(2)}, u32[]{:S(2)}) collective-permute-start(bf16[64,1536]{1,0:T(8,128)(2,1)S(1)} %get-tuple-element.95), channel_id=1, source_target_pairs={{0,1},{1,2},{2,3},{3,4},{4,5},{5,6},{6,7},{7,8},{8,9},{9,10},{10,1... | collective-permute-start | bytes 589832 | tf_op jit(solution)/shard_map/ppermute | solution.py:34
  371.7 1.4 copy-start.18
  371.8 1.9 copy-start.19
  378.4 3.8 copy-start.6
  382.2 6.1 %copy-start.31 = (bf16[1024,768]{0,1:T(8,128)(2,1)S(1)}, bf16[1024,768]{0,1:T(8,128)(2,1)}, u32[]{:S(2)}) copy-start(bf16[1024,768]{0,1:T(8,128)(2,1)} %copy-done.30) | copy-start | bytes 4718596
  382.2 6.1 %copy-start.32 = (bf16[1024,768]{1,0:T(8,128)(2,1)S(1)}, bf16[1024,768]{1,0:T(8,128)(2,1)}, u32[]{:S(2)}) copy-start(bf16[1024,768]{1,0:T(8,128)(2,1)} %slice.298) | copy-start | bytes 4718596
  392.7 4.2 copy-start.5
  392.7 4.2 copy-start.23
  392.7 4.2 copy-start.36
  392.7 4.2 copy-start.38
  392.7 4.2 copy-start.40
  396.9 6.1 %copy-start.21 = (f32[768,384]{1,0:T(8,128)S(1)}, f32[768,384]{1,0:T(8,128)}, u32[]{:S(2)}) copy-start(f32[768,384]{1,0:T(8,128)} %fusion.36) | copy-start | bytes 3538948
  402.8 1.3 copy-start.20
  402.9 2.3 copy-start.25
  405.2 1.5 copy-start.16
  405.2 1.7 copy-start.28
  406.7 2.0 copy-start.27
  408.7 2.0 copy-start.24
  410.7 1.5 copy-start.15
  412.1 2.0 copy-start.26
  422.3 4.7 copy-start.9
  432.8 4.1 copy-start.3
Sparse Core Ops, SparseCore 0:
  11.4 63.3 all-gather.2
  78.3 75.9 all-gather.4
  422.5 30.2 reduce-scatter.1

commit v10 on v9

--- a/solution.py
+++ b/solution.py
@@ -139,7 +139,9 @@
     pos = lookup(me, where)
     nxt = lookup(lax.rem(pos + 1, n), order)
     prv = lookup(lax.rem(pos + n - 1, n), order)
-    piece = out_ref.shape[0] // (2 * per_way)
+    piece = out_ref.shape[0] // per_way
+    ahead = (n - 1) // 2
+    behind = n - 1 - ahead
 
     barrier = pltpu.get_barrier_semaphore()
     pl.semaphore_signal(barrier, 1, device_id=(d, nxt), device_id_type=MESH)
@@ -147,23 +149,31 @@
     pl.semaphore_wait(barrier, 2)
 
     lanes = []
-    for li in range(2 * per_way):
-        forward = li % 2 == 0
-        lanes.append((recv.at[li], send.at[li], ssem.at[li], rsem.at[li], free.at[li],
-                      nxt if forward else prv, prv if forward else nxt,
-                      slice(li * piece, (li + 1) * piece), -1 if forward else 1))
+    for forward in (True, False):
+        for chunk in range(per_way):
+            li = len(lanes)
+            lanes.append((recv.at[li], send.at[li], ssem.at[li], rsem.at[li], free.at[li],
+                          nxt if forward else prv, prv if forward else nxt,
+                          slice(chunk * piece, (chunk + 1) * piece),
+                          ahead if forward else behind, forward))
     copies = {}
-    for step in range(n - 1):
+    for step in range(max(ahead, behind)):
         slot = step % 2
-        for li, (recv, send, ssem, rsem, free, to, frm, rows, sign) in enumerate(lanes):
-            q = lookup(lax.rem(pos + sign * (1 + step) + n * (step + 2), n), order)
+        for li, (recv, send, ssem, rsem, free, to, frm, rows, sends, forward) in enumerate(lanes):
+            if step >= sends:
+                continue
+            if forward:
+                target = pos + sends - step
+            else:
+                target = pos + n - sends + step
+            q = lookup(lax.rem(target, n), order)
             own = h_ref[q, rows, :]
             if step == 0:
                 part = own
             else:
                 copies[(li, step - 1)].wait_recv()
                 part = recv[1 - slot].astype(jnp.float32) + own
-                if step <= n - 3:
+                if step <= sends - 2:
                     pl.semaphore_signal(free, 1, device_id=(d, frm), device_id_type=MESH)
             if step >= 2:
                 copies[(li, step - 2)].wait_send()
@@ -175,13 +185,19 @@
                 device_id=(d, to), device_id_type=MESH)
             c.start()
             copies[(li, step)] = c
-    last = n - 2
-    for li, (recv, send, ssem, rsem, free, to, frm, rows, sign) in enumerate(lanes):
-        copies[(li, last)].wait_recv()
-        out_ref[rows, :] = recv[last % 2].astype(jnp.float32) + h_ref[me, rows, :]
-        if last >= 1:
-            copies[(li, last - 1)].wait_send()
-        copies[(li, last)].wait_send()
+    for chunk in range(per_way):
+        rows = lanes[chunk][7]
+        total = h_ref[me, rows, :]
+        for li in (chunk, per_way + chunk):
+            recv, sends = lanes[li][0], lanes[li][8]
+            copies[(li, sends - 1)].wait_recv()
+            total = total + recv[(sends - 1) % 2].astype(jnp.float32)
+        out_ref[rows, :] = total
+    for li, lane in enumerate(lanes):
+        sends = lane[8]
+        if sends >= 2:
+            copies[(li, sends - 2)].wait_send()
+        copies[(li, sends - 1)].wait_send()
 
 
 RING_WAYS = 2
@@ -190,7 +206,7 @@
 def ring_reduce(h, order, per_way, link_dtype=jnp.bfloat16):
     n, rows, width = h.shape
     lanes = 2 * per_way
-    piece = rows // lanes
+    piece = rows // per_way
     return pl.pallas_call(
         functools.partial(ring_kernel, tuple(order), per_way),
         out_shape=jax.ShapeDtypeStruct((rows, width), jnp.float32),
@@ -439,10 +455,15 @@
     grad_hattn = apply_back(grad_qkv, full_qkv)
     grad_gain_one = jnp.sum(grad_hattn * normed_a, axis=0)
     grad_tokens = grad_mid + norm_back(grad_hattn * gain_one, normed_a, factor_a)
-    height = out_cols + in_cols + down_lines + qkv_cols + 16
-    tail = 8 + (-height) % (2 * RING_WAYS * 16)
-    gain_two_rows = gain_blocks(grad_gain_two, 1, n_seq, rows)[0]
-    gain_one_rows = gain_blocks(grad_gain_one, 1, n_seq, rows, tail)[0]
+    height = out_cols + in_cols + down_lines + qkv_cols + 8
+    tail = 8 + (-height) % (RING_WAYS * 16)
+    gain_both = jnp.concatenate(
+        [
+            gain_blocks(grad_gain_two, 1, n_seq, rows, 1)[0],
+            gain_blocks(grad_gain_one, 1, n_seq, rows, tail - 1)[0],
+        ],
+        1,
+    )
     blocks = jnp.stack(
         [
             jnp.concatenate(
@@ -454,9 +475,8 @@
                             grad_down[d]
                             .reshape(n_seq, down_cols, down_rows)
                             .reshape(n_seq, down_lines, rows),
-                            gain_two_rows,
                             grad_qkvw[d].reshape(n_seq, qkv_cols, rows),
-                            gain_one_rows,
+                            gain_both,
                         )
                     ),
                 ],
@@ -470,7 +490,6 @@
         blocks.reshape(n_dp, n_seq * depth, rows), "dp", scatter_dimension=0, tiled=True
     )
     late = ring_reduce(half.reshape(n_seq, depth, rows), order, RING_WAYS)
-    last = late[out_cols + in_cols + down_lines + 8 :]
     at = 0
     late_out = late[at : at + out_cols].T
     at += out_cols
@@ -478,15 +497,18 @@
     at += in_cols
     late_down = late[at : at + down_lines].reshape(down_cols, down_rows).T
     at += down_lines
+    late_qkv = late[at : at + qkv_cols].T
+    at += qkv_cols
     late_gain_two = late[at, : gain_mlp.shape[0]]
+    late_gain_one = late[at + 1, : gain_attn.shape[0]]
     return (
         output,
         grad_tokens,
-        last[:qkv_cols].T,
+        late_qkv,
         late_out,
         late_in,
         late_down,
-        last[qkv_cols, : gain_attn.shape[0]],
+        late_gain_one,
         late_gain_two,
     )
 

time: 544 us -> 534 us (0.982)
  Pallas kernels: 147 us -> 140 us
    pallas_call x1, Pallas kernels: 71 us -> 64 us  [ring_reduce(): pl.pallas_call(functools.partial(ring_kernel, tuple(order), per_way), out...]
    unnamed x112 -> x108, local copies, waits for them, and re-layouts: 29 us -> 28.9 us
where the time goes in v10:
time: 534 us; the launch traced here: 523 us
  Pallas kernels  140 us (26%)
  local copies, waits for them, and re-layouts  138 us (26%)
  other arithmetic  75.7 us (14%)
  matrix products  73.9 us (14%)
  waiting for transfers between devices  63.5 us (12%)
  starting transfers between devices  17.7 us (3%)
  between operations  15 us (3%)
    pallas_call x1, Pallas kernels, ring_reduce(): pl.pallas_call(functools.partial(ring_kernel, tuple(order), per_way), out...  64 us
    pallas_call x1, Pallas kernels, attn_bwd(): pl.pallas_call(attn_bwd_kernel, out_shape=(jax.ShapeDtypeStruct((count, w...  55.2 us
    all_gather x2, waiting for transfers between devices, gather_rows(): every = lax.all_gather(payload, ('dp', 'seq'), axis=0, tiled=True)  50.7 us
    unnamed x108, local copies, waits for them, and re-layouts  28.9 us
    dot_general x8, matrix products, grad_t(): lax.dot_general(grad, left[:, d * width:(d + 1) * width], (((0,), (0,)),...  26.6 us
    dot_general x4, matrix products, apply_back(): jnp.einsum('tn,dnr->tdr', grad, weight_t, preferred_element_type=jnp.floa...  25.4 us
    dot_general x4, matrix products, apply_t(): jnp.einsum('tdr,dnr->tn', front(left, n_dp), weight_t, preferred_element_...  21.9 us
    pallas_call x1, Pallas kernels, attn_fwd(): pl.pallas_call(attn_fwd_kernel, out_shape=jax.ShapeDtypeStruct((count, wi...  21 us
  transfers between devices with their start and end apart: 9, of which 4 were waited for; matrix products, arithmetic and copies ran while one was open for 19% of the time, Pallas kernels for 4%

profile of v10, /device:TPU:0, one launch (start us, length us, event | category | flops | bytes accessed | tf_op | source)
XLA Modules:
  0.0 523.4 jit_solution(12400219196196265398)
XLA Ops:
  11.2 4.2 concatenate.59
  19.9 3.5 copy.30
  24.2 50.7 %all-gather.3.cloned.1.call-done = bf16[4864,384]{1,0:T(8,128)(2,1)} async-done(((bf16[152,384]{1,0:T(8,128)(2,1)}), bf16[4864,384]{1,0:T(8,128)(2,1)}) %all-gather.3.cloned.1.call-update) | async-done | bytes 3735568 | tf_op jit(solution)/shard_map/all_gather | solution.py:333
  74.8 4.2 slice.216
  80.4 6.5 %convolution_bitcast_fusion.1 = f32[1024,2304]{1,0:T(8,128)S(1)} fusion(bf16[1024,2,384]{0,2,1:T(8,128)(2,1)S(1)} %bitcast.133, bf16[2,2304,384]{2,1,0:T(8,128)(2,1)} %bitcast.95), kind=kOutput, calls=%fused_computation.4 | convolution fusion | flops 3623878656 | bytes 14548992 | tf_op jit(solution)/shard_map/tdr,dnr->tn/dot_general | solution.py:348
  88.4 3.5 fusion.48
  92.9 2.4 copy.34
  95.3 3.5 copy.31
  98.8 2.7 slice_negate_fusion.2
  101.5 2.5 maximum_multiply_fusion.1
  104.0 3.6 copy.35
  107.6 2.4 copy.32
  109.9 6.7 %add_convert_fusion.1 = (bf16[1024,768]{1,0:T(8,128)(2,1)S(1)}, bf16[1024,768]{1,0:T(8,128)(2,1)S(1)}) fusion(f32[1024,768]{1,0:T(8,128)} %copy.35, f32[1024,768]{1,0:T(8,128)} %copy.30, f32[1024,2304]{1,0:T(8,128)} %copy-done.11, f32[1024,768]{1,0:T(8,128)} %copy.32), kind=kLoop, calls=%fused_computation.56 | loop fusion | flops 4718592 | bytes 18874368 | tf_op jit(solution)/shard_map/convert_element_type | solution.py:394
  117.4 4.0 collective-permute-start
  124.1 5.2 collective-permute-start.2
  130.3 2.6 copy.42
  133.0 6.0 %collective-permute-done.3 = s32[64]{0:T(128)S(1)} collective-permute-done((s32[64]{0:T(128)S(1)}, s32[64]{0:T(128)S(1)}, u32[]{:S(2)}, u32[]{:S(2)}) %collective-permute-start.3) | collective-permute-done | bytes 288 | tf_op jit(solution)/shard_map/ppermute | solution.py:26
  139.1 5.8 %copy.55 = bf16[2,384,2304]{2,1,0:T(8,128)(2,1)} copy(bf16[2,384,2304]{1,2,0:T(8,128)(2,1)} %bitcast.96) | data formatting | bytes 7077888 | tf_op jit(solution)/shard_map/tn,dnr->tdr/dot_general | solution.py:352
  144.9 3.5 pad_maximum_fusion.2.kv_ref
  148.5 21.0 %shard_map.161 = bf16[1024,768]{1,0:T(8,128)(2,1)S(1)} custom-call(bf16[1024,768]{1,0:T(8,128)(2,1)S(1)} %get-tuple-element.87.q_ref, bf16[1152,1536]{1,0:T(8,128)(2,1)} %pad_maximum_fusion.2.kv_ref, s32[1024,1]{1,0:T(8,128)S(1)} %copy-done, s32[1,1152]{1,0:T(1,128)S(1)} %reshape.241.tk_ref), custom_call_target="tpu_custom_call" | custom-call | tf_op jit(solution)/shard_map/pallas_call | solution.py:303
  170.3 2.4 slice.184
  172.7 2.9 slice.189
  175.6 4.1 slice.186
  179.8 4.8 reshape_reshape.9
  184.6 3.2 fusion.51
  189.9 5.8 %copy.46 = bf16[2,384,2304]{2,1,0:T(8,128)(2,1)} copy(bf16[2,384,2304]{1,2,0:T(8,128)(2,1)} %bitcast.97) | data formatting | bytes 7077888 | tf_op jit(solution)/shard_map/tn,dnr->tdr/dot_general | solution.py:352
  195.7 6.5 %fusion.23 = f32[2,576,1024]{2,1,0:T(8,128)} fusion(bf16[2,768,576]{2,1,0:T(8,128)(2,1)} %reshape_reshape.9, bf16[1024,768]{1,0:T(8,128)(2,1)} %param.23), kind=kOutput, calls=%fused_computation.68 | convolution fusion | flops 1811939328 | bytes 8060928 | tf_op jit(solution)/shard_map/tn,dnr->tdr/dot_general | solution.py:352
  202.2 6.3 %copy.44 = f32[1024,1152]{1,0:T(8,128)} copy(f32[1024,1152]{0,1:T(8,128)} %bitcast.119) | data formatting | bytes 9437184 | tf_op jit(solution)/shard_map/reshape | solution.py:353
  208.5 2.4 multiply_convert_fusion.1
  210.9 6.5 %convolution_bitcast_fusion = f32[1024,2304]{1,0:T(8,128)S(1)} fusion(bf16[1024,2,384]{0,2,1:T(8,128)(2,1)S(1)} %bitcast.134, bf16[2,2304,384]{2,1,0:T(8,128)(2,1)} %bitcast.98), kind=kOutput, calls=%fused_computation.3 | convolution fusion | flops 3623878656 | bytes 14548992 | tf_op jit(solution)/shard_map/tdr,dnr->tn/dot_general | solution.py:348
  217.5 11.1 %fusion.25 = (f32[1024,1152]{1,0:T(8,128)}, f32[1024,1152]{1,0:T(8,128)S(1)}) fusion(f32[1024,1152]{1,0:T(8,128)S(1)} %bitcast.94, f32[1024,2304]{1,0:T(8,128)S(1)} %convolution_bitcast_fusion), kind=kLoop, calls=%fused_computation.72 | loop fusion | flops 76677120 | bytes 18874368 | tf_op jit(solution)/shard_map/transpose(jvp())/mul | solution.py:80
  228.6 4.0 multiply_add_fusion
  232.6 9.4 %multiply_reduce_fusion = (f32[768]{0:T(1024)S(1)}, f32[1024]{0:T(1024)S(1)}, f32[1024]{0:T(1024)S(1)}, f32[1024,768]{0,1:T(8,128)S(1)}) fusion(f32[1024,768]{0,1:T(8,128)S(1)} %copy-done.8, f32[1024]{0:T(1024)S(1)} %add_rsqrt_fusion, f32[1024]{0:T(1024)S(1)} %broadcast_multiply_fusion.4, f32[768]{0:T(1024)S(1)} %reshape.263, ...), kind=kOutput, calls=%fused_computation.49 | convolution fusion | flops 3634885888 | bytes 19290112 | tf_op jit(solution)/shard_map/tn,dnr->tdr/dot_general | solution.py:352
  247.0 2.6 convolution_bitcast_fusion.2
  252.0 4.6 fusion.34
  256.6 4.6 fusion.30
  262.8 3.7 convolution_convert_fusion.do_ref
  266.5 55.2 %shard_map.162 = (f32[1024,768]{1,0:T(8,128)}, f32[1152,1536]{1,0:T(8,128)}) custom-call(bf16[1024,768]{1,0:T(8,128)(2,1)S(1)} %get-tuple-element.87.q_ref, bf16[1152,1536]{1,0:T(8,128)(2,1)} %pad_maximum_fusion.2.kv_ref, s32[1024,1]{1,0:T(8,128)S(1)} %copy-done.1, s32[1,1152]{1,0:T(1,128)S(1)} %reshape.241.tk_ref, ...), custom_call_target="tpu_custom_call" | custom-call | tf_op jit(solution)/shard_map/pallas_call | solution.py:315
  321.7 5.4 %convert.21 = bf16[1152,1536]{1,0:T(8,128)(2,1)} convert(f32[1152,1536]{1,0:T(8,128)} %get-tuple-element.49) | non-fusion elementwise | flops 1769472 | bytes 10616832 | tf_op jit(solution)/shard_map/convert.7
  327.7 3.0 slice.192
  332.7 2.4 reshape_reshape.11
  335.2 3.0 copy.56
  338.1 3.4 reshape_reshape.10
  346.2 4.6 collective-permute-start.4
  350.8 4.0 slice_negate_fusion.1
  354.7 3.1 collective-permute-done.4
  361.4 3.2 slice.295
  364.6 3.8 slice.231
  368.4 2.6 copy.53
  372.9 2.4 maximum_multiply_fusion.2
  375.3 2.4 copy.51
  377.6 3.8 copy.54
  381.4 6.1 %subtract_convert_fusion.1 = (bf16[1024,768]{1,0:T(8,128)(2,1)S(1)}, bf16[1024,768]{1,0:T(8,128)(2,1)S(1)}) fusion(f32[1024,768]{1,0:T(8,128)} %copy.51, f32[1024,768]{1,0:T(8,128)} %get-tuple-element.48, f32[1024,768]{1,0:T(8,128)S(1)} %copy-done.6, f32[1024,768]{1,0:T(8,128)} %copy.54, f32[1024,1536]{1,0:T(8,128)} %fusion.40), kind=kLoop, calls=%fused_computation.51 | loop fusion | flops 4718592 | bytes 18874368 | tf_op jit(solution)/shard_map/convert.2
  387.6 4.3 fusion.32
  391.9 4.2 fusion.28
  396.1 5.8 %fusion.18 = (f32[768]{0:T(1024)S(1)}, f32[1024]{0:T(1024)S(1)}, f32[1024]{0:T(1024)S(1)}, f32[1024,768]{0,1:T(8,128)}) fusion(bf16[1024,768]{0,1:T(8,128)(2,1)S(1)} %copy-done.5, f32[1024]{0:T(1024)S(1)} %copy-done.39, f32[1024]{0:T(1024)S(1)} %copy-done.35, f32[768]{0:T(1024)S(1)} %copy-done.37, bf16[768,2304]{1,0:T(8,128)(2,1)S(1)} %bitcast.124, ...), kind=kOutput, calls=%fused_computation.39 | convolution fusion | flops 3645109504 | bytes 12998656 | tf_op jit(solution)/shard_map/tn,dnr->tdr/dot_general | solution.py:352
  413.7 7.4 %pad_maximum_fusion = f32[2,6656,384]{2,1,0:T(8,128)} fusion(f32[1,6656,384]{2,1,0:T(8,128)S(1)} %bitcast.100, f32[1,6656,384]{2,1,0:T(8,128)S(1)} %bitcast.99), kind=kLoop, calls=%fused_computation | loop fusion | flops 5111808 | bytes 40894464 | tf_op jit(solution)/shard_map/stack | solution.py:467
  421.1 4.7 copy.39
  425.8 5.7 %fusion.20 = bf16[1024,768]{0,1:T(8,128)(2,1)} fusion(f32[1024,768]{0,1:T(8,128)S(1)} %copy-done.9, bf16[2,768,576]{2,1,0:T(8,128)(2,1)} %reshape_reshape.9, bf16[1024,2,576]{0,2,1:T(8,128)(2,1)} %bitcast.132), kind=kOutput, calls=%fused_computation.48 | convolution fusion | flops 1813512192 | bytes 8847360 | tf_op jit(solution)/shard_map/tdr,dnr->tn/dot_general | solution.py:348
  431.5 3.1 copy.58
  435.6 6.4 %fusion.17 = f32[1024,768]{0,1:T(8,128)} fusion(f32[1024,768]{0,1:T(8,128)S(1)} %copy-done.3, bf16[1024,768]{0,1:T(8,128)(2,1)} %copy-done.4, f32[1024,768]{0,1:T(8,128)} %get-tuple-element.122, f32[1024]{0:T(1024)S(1)} %broadcast_multiply_fusion, f32[1024]{0:T(1024)S(1)} %broadcast_multiply_fusion.1, f32[768]{0:T(1024)S(1)} %copy-done.37, ...), kind=kLoop, calls=%fused_computation.38 | loop fusion | flops 7077888 | bytes 11029504 | tf_op jit(solution)/shard_map/add | solution.py:457
  441.9 4.2 copy.59
  446.1 3.6 reduce-scatter.2.cloned.1.call-done
  449.7 64.0 %shard_map.163 = f32[416,384]{1,0:T(8,128)S(1)} custom-call(f32[16,416,384]{2,1,0:T(8,128)} %bitcast.110), custom_call_target="tpu_custom_call" | custom-call | tf_op jit(solution)/shard_map/pallas_call | solution.py:210
  (183 shorter events, 57.4 us)
Async XLA Ops:
  7.2 10.0 %copy-start.40 = (s32[1024]{0:T(1024)S(1)}, s32[1024]{0:T(1024)}, u32[]{:S(2)}) copy-start(s32[1024]{0:T(1024)} %param.16) | copy-start | bytes 12292
  7.2 10.0 %copy-start.41 = (s32[1024]{0:T(1024)S(1)}, s32[1024]{0:T(1024)}, u32[]{:S(2)}) copy-start(s32[1024]{0:T(1024)} %param.15) | copy-start | bytes 12292
  7.2 67.7 %all-gather.3.cloned.1.call-start = ((), (), s32[]{:S(2)}) async-start(), calls=%async_computation.1 | async-start | bytes 3852288 | tf_op jit(solution)/shard_map/all_gather | solution.py:333
  9.5 160.0 %all-gather.5.cloned.1.call-start = ((), (), s32[]{:S(2)}) async-start(), calls=%async_computation.2 | async-start | bytes 6893568 | tf_op jit(solution)/shard_map/all_gather | solution.py:333
  15.4 434.3 %reduce-scatter.2.cloned.1.call-start = ((), (), s32[]{:S(2)}) async-start(), calls=%async_computation.3 | async-start | bytes 30670848 | tf_op jit(solution)/shard_map/reduce_scatter | solution.py:489
  17.2 62.7 %copy-start.4 = (bf16[1024,768]{0,1:T(8,128)(2,1)}, bf16[1024,768]{0,1:T(8,128)(2,1)S(1)}, u32[]{:S(2)}) copy-start(bf16[1024,768]{0,1:T(8,128)(2,1)S(1)} %copy.28) | copy-start | bytes 4718596
  23.7 56.2 %copy-start.34 = (f32[1024]{0:T(1024)}, f32[1024]{0:T(1024)S(1)}, u32[]{:S(2)}) copy-start(f32[1024]{0:T(1024)S(1)} %broadcast_multiply_fusion.5) | copy-start | bytes 12292
  24.2 55.7 %copy-start.38 = (f32[1024]{0:T(1024)}, f32[1024]{0:T(1024)S(1)}, u32[]{:S(2)}) copy-start(f32[1024]{0:T(1024)S(1)} %add_rsqrt_fusion.1) | copy-start | bytes 12292
  79.9 7.0 %copy-start.36 = (f32[768]{0:T(1024)}, f32[768]{0:T(1024)S(1)}, u32[]{:S(2)}) copy-start(f32[768]{0:T(1024)S(1)} %reshape.262) | copy-start | bytes 9220
  80.4 6.5 %copy-start.29 = (bf16[1024,768]{0,1:T(8,128)(2,1)}, bf16[1024,768]{0,1:T(8,128)(2,1)S(1)}, u32[]{:S(2)}) copy-start(bf16[1024,768]{0,1:T(8,128)(2,1)S(1)} %fusion.13) | copy-start | bytes 4718596
  86.9 6.0 %copy-start.11 = (f32[1024,2304]{1,0:T(8,128)}, f32[1024,2304]{1,0:T(8,128)S(1)}, u32[]{:S(2)}) copy-start(f32[1024,2304]{1,0:T(8,128)S(1)} %convolution_bitcast_fusion.1) | copy-start | bytes 28311556
  109.9 6.7 %copy-start.12 = (bf16[1024,768]{1,0:T(8,128)(2,1)S(1)}, bf16[1024,768]{1,0:T(8,128)(2,1)}, u32[]{:S(2)}) copy-start(bf16[1024,768]{1,0:T(8,128)(2,1)} %slice.296) | copy-start | bytes 4718596
  117.4 27.5 %collective-permute-start = (bf16[64,1536]{1,0:T(8,128)(2,1)}, bf16[64,1536]{1,0:T(8,128)(2,1)}, u32[]{:S(2)}, u32[]{:S(2)}) collective-permute-start(bf16[64,1536]{1,0:T(8,128)(2,1)} %get-tuple-element.98), channel_id=1, source_target_pairs={{0,1},{1,2},{2,3},{3,4},{4,5},{5,6},{6,7},{7,8},{8,9},{9,10},{10,1... | collective-permute-start | bytes 589832 | tf_op jit(solution)/shard_map/ppermute | solution.py:25
  121.4 23.5 %collective-permute-start.1 = (bf16[64,1536]{1,0:T(8,128)(2,1)}, bf16[64,1536]{1,0:T(8,128)(2,1)}, u32[]{:S(2)}, u32[]{:S(2)}) collective-permute-start(bf16[64,1536]{1,0:T(8,128)(2,1)} %get-tuple-element.99), channel_id=1, source_target_pairs={{1,0},{2,1},{3,2},{4,3},{5,4},{6,5},{7,6},{8,7},{9,8},{10,9},{11,1... | collective-permute-start | bytes 589832 | tf_op jit(solution)/shard_map/ppermute | solution.py:26
  122.8 16.2 %collective-permute-start.3 = (s32[64]{0:T(128)S(1)}, s32[64]{0:T(128)S(1)}, u32[]{:S(2)}, u32[]{:S(2)}) collective-permute-start(s32[64]{0:T(128)S(1)} %get-tuple-element.114), channel_id=1, source_target_pairs={{1,0},{2,1},{3,2},{4,3},{5,4},{6,5},{7,6},{8,7},{9,8},{10,9},{11,1... | collective-permute-start | bytes 776 | tf_op jit(solution)/shard_map/ppermute | solution.py:26
  124.1 14.9 %collective-permute-start.2 = (s32[64]{0:T(128)S(1)}, s32[64]{0:T(128)S(1)}, u32[]{:S(2)}, u32[]{:S(2)}) collective-permute-start(s32[64]{0:T(128)S(1)} %get-tuple-element.115), channel_id=1, source_target_pairs={{0,1},{1,2},{2,3},{3,4},{4,5},{5,6},{6,7},{7,8},{8,9},{9,10},{10,1... | collective-permute-start | bytes 776 | tf_op jit(solution)/shard_map/ppermute | solution.py:25
  144.9 3.6 copy-start
  187.8 1.7 copy-start.7
  208.5 9.0 %slice-start = ((s8[4718592]{0:T(1024)(128)(4,1)}), s8[4194304]{0:T(1024)(128)(4,1)S(1)}, s32[]{:S(2)}) async-start(s8[4718592]{0:T(1024)(128)(4,1)} %bitcast.93), calls=%async_computation.4 | async-start | bytes 8388608
  210.9 6.5 %copy-start.32 = (bf16[1024,768]{0,1:T(8,128)(2,1)}, bf16[1024,768]{0,1:T(8,128)(2,1)S(1)}, u32[]{:S(2)}) copy-start(bf16[1024,768]{0,1:T(8,128)(2,1)S(1)} %multiply_convert_fusion.1) | copy-start | bytes 4718596
  210.9 6.5 %slice-start.1 = ((s8[4718592]{0:T(1024)(128)(4,1)}), s8[524288]{0:T(1024)(128)(4,1)S(1)}, s32[]{:S(2)}) async-start(s8[4718592]{0:T(1024)(128)(4,1)} %bitcast.93), calls=%async_computation.5 | async-start | bytes 1048576
  228.6 4.0 copy-start.8
  232.6 17.1 %copy-start.14 = (bf16[1024,1152]{1,0:T(8,128)(2,1)}, bf16[1024,1152]{1,0:T(8,128)(2,1)S(1)}, u32[]{:S(2)}) copy-start(bf16[1024,1152]{1,0:T(8,128)(2,1)S(1)} %get-tuple-element.85) | copy-start | bytes 7077892
  232.6 9.4 %copy-start.17 = (bf16[1024,768]{0,1:T(8,128)(2,1)S(1)}, bf16[1024,768]{0,1:T(8,128)(2,1)}, u32[]{:S(2)}) copy-start(bf16[1024,768]{0,1:T(8,128)(2,1)} %copy.42) | copy-start | bytes 4718596
  242.9 4.1 copy-start.2
  242.9 4.0 copy-start.28
  244.9 7.0 %slice-start.4 = ((s8[4718592]{0:T(1024)(128)(4,1)}), s8[4194304]{0:T(1024)(128)(4,1)S(1)}, s32[]{:S(2)}) async-start(s8[4718592]{0:T(1024)(128)(4,1)} %bitcast.122), calls=%async_computation.8 | async-start | bytes 8388608
  247.0 5.0 slice-start.2
  247.0 5.0 slice-start.5
  249.6 2.3 slice-start.3
  249.6 2.3 copy-start.33
  256.6 4.6 copy-start.22
  262.8 3.7 copy-start.1
  321.7 6.0 %copy-start.10 = (f32[1152,1536]{1,0:T(8,128)S(1)}, f32[1152,1536]{1,0:T(8,128)}, u32[]{:S(2)}) copy-start(f32[1152,1536]{1,0:T(8,128)} %get-tuple-element.49) | copy-start | bytes 21233668
  335.2 6.4 %copy-start.13 = (f32[1024,768]{1,0:T(8,128)S(1)}, f32[1024,768]{1,0:T(8,128)}, u32[]{:S(2)}) copy-start(f32[1024,768]{1,0:T(8,128)} %get-tuple-element.48) | copy-start | bytes 9437188
  344.9 14.8 %collective-permute-start.5 = (bf16[64,1536]{1,0:T(8,128)(2,1)S(1)}, bf16[64,1536]{1,0:T(8,128)(2,1)S(1)}, u32[]{:S(2)}, u32[]{:S(2)}) collective-permute-start(bf16[64,1536]{1,0:T(8,128)(2,1)S(1)} %get-tuple-element.90), channel_id=1, source_target_pairs={{1,0},{2,1},{3,2},{4,3},{5,4},{6,5},{7,6},{8,7},{9,8},{10,9},{11,1... | collective-permute-start | bytes 589832 | tf_op jit(solution)/shard_map/ppermute | solution.py:34
  346.2 11.7 %collective-permute-start.4 = (bf16[64,1536]{1,0:T(8,128)(2,1)S(1)}, bf16[64,1536]{1,0:T(8,128)(2,1)S(1)}, u32[]{:S(2)}, u32[]{:S(2)}) collective-permute-start(bf16[64,1536]{1,0:T(8,128)(2,1)S(1)} %get-tuple-element.91), channel_id=1, source_target_pairs={{0,1},{1,2},{2,3},{3,4},{4,5},{5,6},{6,7},{7,8},{8,9},{9,10},{10,1... | collective-permute-start | bytes 589832 | tf_op jit(solution)/shard_map/ppermute | solution.py:34
  371.0 1.4 copy-start.18
  371.0 1.9 copy-start.19
  377.6 3.8 copy-start.6
  381.4 6.1 %copy-start.30 = (bf16[1024,768]{0,1:T(8,128)(2,1)S(1)}, bf16[1024,768]{0,1:T(8,128)(2,1)}, u32[]{:S(2)}) copy-start(bf16[1024,768]{0,1:T(8,128)(2,1)} %copy-done.29) | copy-start | bytes 4718596
  381.4 6.1 %copy-start.31 = (bf16[1024,768]{1,0:T(8,128)(2,1)S(1)}, bf16[1024,768]{1,0:T(8,128)(2,1)}, u32[]{:S(2)}) copy-start(bf16[1024,768]{1,0:T(8,128)(2,1)} %slice.295) | copy-start | bytes 4718596
  391.8 4.2 copy-start.5
  391.8 4.2 copy-start.23
  391.8 4.2 copy-start.35
  391.8 4.2 copy-start.37
  391.9 4.2 copy-start.39
  396.1 6.0 %copy-start.21 = (f32[768,384]{1,0:T(8,128)S(1)}, f32[768,384]{1,0:T(8,128)}, u32[]{:S(2)}) copy-start(f32[768,384]{1,0:T(8,128)} %fusion.36) | copy-start | bytes 3538948
  401.9 1.3 copy-start.20
  402.0 2.3 copy-start.25
  404.3 1.5 copy-start.16
  405.8 2.0 copy-start.27
  407.8 2.0 copy-start.24
  409.8 1.5 copy-start.15
  411.3 2.0 copy-start.26
  421.1 4.7 copy-start.9
  431.5 4.1 copy-start.3
Sparse Core Ops, SparseCore 0:
  11.4 63.3 all-gather.2
  78.3 75.9 all-gather.4
  421.2 28.4 reduce-scatter.1
